TPU v7x, 32 devices: a whole 2x2x4 slice. The times are simulated.
32 devices in a mesh: ctx: 8 (over z, x), tp: 4 (over y, core).
Axes of the slice: x: 2, y: 2, z: 4, core: 2. Of those that a mesh axis runs over, the one named last changes fastest.
Arguments:
- tokens: bfloat16 [4, 2048, 1024], P(None, ('ctx', 'tp')), may hold values from -6 to 6
- gain_one: bfloat16 [1024], replicated, may hold values from 0.099609375 to 1.8984375
- shift_one: bfloat16 [1024], replicated, may hold values from -3 to 3
- query_key_value_weight: bfloat16 [1024, 16, 192], P(None, 'tp'), may hold values from -0.1875 to 0.1875
- qv_bias: bfloat16 [16, 128], P('tp'), may hold values from -3 to 3
- attention_out_weight: bfloat16 [16, 64, 1024], P('tp'), may hold values from -0.75 to 0.75
- attention_out_bias: bfloat16 [1024], replicated, may hold values from -3 to 3
- gain_two: bfloat16 [1024], replicated, may hold values from 0.099609375 to 1.8984375
- shift_two: bfloat16 [1024], replicated, may hold values from -3 to 3
- expand_weight: bfloat16 [1024, 4096], P(None, 'tp'), may hold values from -0.1875 to 0.1875
- expand_bias: bfloat16 [4096], P('tp'), may hold values from -3 to 3
- contract_weight: bfloat16 [4096, 1024], P('tp'), may hold values from -0.09375 to 0.09375
- contract_bias: bfloat16 [1024], replicated, may hold values from -3 to 3
- doc_ids: int32 [4, 2048], P(None, 'ctx'), may hold values from 0 to 2, never falling along the last dimension, each value on 1 to 1536 neighbouring positions
- out_grad: bfloat16 [4, 2048, 1024], P(None, ('ctx', 'tp')), may hold values from -6 to 6
Outputs:
- layer_out: bfloat16 [4, 2048, 1024], P(None, ('ctx', 'tp'))
- grad_tokens: float32 [4, 2048, 1024], P(None, ('ctx', 'tp'))
- grad_gainone: float32 [1024], replicated
- grad_shiftone: float32 [1024], replicated
- grad_qkv: float32 [1024, 16, 192], P(None, 'tp')
- grad_qvbias: float32 [16, 128], P('tp')
- grad_outweight: float32 [16, 64, 1024], P('tp')
- grad_outbias: float32 [1024], replicated
- grad_gaintwo: float32 [1024], replicated
- grad_shifttwo: float32 [1024], replicated
- grad_fcweight: float32 [1024, 4096], P(None, 'tp')
- grad_fcbias: float32 [4096], P('tp')
- grad_projweight: float32 [4096, 1024], P('tp')
- grad_projbias: float32 [1024], replicated
Inputs may be any that keep to these rules, and one draw needn't show every extreme that they name: `doc_ids`: in each sequence the document numbers never fall along positions; each of the 3 documents has 1 to 1536 positions, and one has exactly 1536.
All inputs are finite; a program needn't handle non-finite values.
Results may differ from a plain program's by a relative error of at most 0.02.
Values may be sent and summed in bfloat16 or wider, within the bound.
No kernel may reach another device: no remote copies, remote signals or barrier semaphores. Data moves between devices by JAX's collectives and lax.ppermute only.
A program may use at most 256 MiB of HBM per device.

v0:
```python
import jax
import jax.numpy as jnp
from jax import lax
from jax.sharding import PartitionSpec as P

HEAD_DIM = 64


eps = 1e-05
neg_fill = -1e30


def layer_norm(values, gain, shift):
    centre = jnp.mean(values, axis=-1, keepdims=True)
    centred = values - centre
    spread = jnp.mean(centred * centred, axis=-1, keepdims=True)
    return centred * lax.rsqrt(spread + eps) * gain + shift


def gelu_tanh(values):
    return jax.nn.gelu(values, approximate=True)


def gather_attn(values):
    return lax.all_gather(values, "tp", axis=1, tiled=True)


def reduce_attn(values):
    return lax.psum_scatter(
        values.astype(jnp.bfloat16), "tp", scatter_dimension=1, tiled=True
    ).astype(jnp.float32)


def gather_mlp(values):
    return lax.all_gather(values, "tp", axis=1, tiled=True)


def reduce_mlp(values):
    return lax.psum_scatter(
        values.astype(jnp.bfloat16), "tp", scatter_dimension=1, tiled=True
    ).astype(jnp.float32)


def feed_forward(normed_rows, fc_full, fcb_full, proj_full, grad_in):
    pre_activation = jnp.einsum(
        "scd,df->scf", normed_rows, fc_full, preferred_element_type=jnp.float32
    ) + fcb_full.astype(jnp.float32)
    active_rows = gelu_tanh(pre_activation).astype(jnp.bfloat16)
    branch_part = jnp.einsum(
        "scf,fd->scd", active_rows, proj_full, preferred_element_type=jnp.float32
    )
    act_grad = jnp.einsum("scd,fd->scf", grad_in, proj_full, preferred_element_type=jnp.float32)
    pre_grad = jax.vjp(gelu_tanh, pre_activation)[1](act_grad)[0].astype(jnp.bfloat16)
    proj_grad = jnp.einsum("scf,scd->fd", active_rows, grad_in, preferred_element_type=jnp.float32)
    fc_grad = jnp.einsum("scd,scf->df", normed_rows, pre_grad, preferred_element_type=jnp.float32)
    fcb_grad = jnp.sum(pre_grad, axis=(0, 1), dtype=jnp.float32)
    normed_grad = jnp.einsum("scf,df->scd", pre_grad, fc_full, preferred_element_type=jnp.float32)
    return (branch_part, normed_grad, fc_grad, fcb_grad, proj_grad)


def shards(
    tokens,
    gain_one,
    shift_one,
    query_key_value_weight,
    qv_bias,
    attention_out_weight,
    attention_out_bias,
    gain_two,
    shift_two,
    expand_weight,
    expand_bias,
    contract_weight,
    contract_bias,
    doc_ids,
    out_grad,
):
    score_scale = HEAD_DIM ** (-0.5)
    seq_count = tokens.shape[0]
    span_rows = doc_ids.shape[1]
    heads_here = query_key_value_weight.shape[1]
    full_length = span_rows * lax.axis_size("ctx")
    first_query = lax.axis_index("ctx") * span_rows
    query_pos = first_query + jnp.arange(span_rows, dtype=jnp.int32)
    last_query = first_query + span_rows - 1
    all_ids = lax.all_gather(doc_ids, "ctx", axis=1, tiled=True)

    def allowed_mask(offset, block_width):
        key_pos = offset + jnp.arange(block_width, dtype=jnp.int32)
        key_ids = lax.dynamic_slice_in_dim(all_ids, offset, block_width, 1)
        causal = key_pos[None, :] <= query_pos[:, None]
        same_doc = doc_ids[:, :, None] == key_ids[:, None, :]
        return jnp.logical_and(causal[None], same_doc)[:, None]

    def keep_state(carry_state):
        return carry_state

    gain_first = gain_one.astype(jnp.float32)
    shift_first = shift_one.astype(jnp.float32)
    gain_second = gain_two.astype(jnp.float32)
    shift_second = shift_two.astype(jnp.float32)
    inputs = tokens.astype(jnp.float32)
    first_normed = layer_norm(inputs, gain_first, shift_first)
    rows_one = gather_attn(first_normed.astype(jnp.bfloat16))
    packed_values = jnp.einsum(
        "scd,dhe->sche", rows_one, query_key_value_weight, preferred_element_type=jnp.float32
    )
    bias_pair = qv_bias.astype(jnp.float32)
    queries = (packed_values[..., :HEAD_DIM] + bias_pair[:, :HEAD_DIM]).astype(jnp.bfloat16)
    keys_here = packed_values[..., HEAD_DIM : 2 * HEAD_DIM].astype(jnp.bfloat16)
    values_here = (packed_values[..., 2 * HEAD_DIM :] + bias_pair[:, HEAD_DIM:]).astype(
        jnp.bfloat16
    )
    key_value = jnp.concatenate([keys_here, values_here], axis=-1)
    start_state = (
        jnp.full((seq_count, heads_here, span_rows), neg_fill, jnp.float32),
        jnp.zeros((seq_count, heads_here, span_rows), jnp.float32),
        jnp.zeros((seq_count, heads_here, span_rows, HEAD_DIM), jnp.float32),
    )
    folded = start_state
    piece_rows = lax.all_gather(key_value, "ctx", axis=1, tiled=True)
    piece_len = piece_rows.shape[1]
    block_width = min(piece_len, span_rows)

    def attend_block(carry_state, block_index):
        offset = block_index * block_width

        def attend_compute(inner_state):
            row_best, row_total, weighted = inner_state
            one_block = lax.dynamic_slice_in_dim(
                piece_rows, block_index * block_width, block_width, 1
            )
            scores = (
                jnp.einsum(
                    "sqhe,skhe->shqk",
                    queries,
                    one_block[..., :HEAD_DIM],
                    preferred_element_type=jnp.float32,
                )
                * score_scale
            )
            allowed = allowed_mask(offset, block_width)
            row_top = jnp.max(jnp.where(allowed, scores, neg_fill), axis=-1)
            new_best = jnp.maximum(row_best, row_top)
            soft_terms = jnp.where(allowed, jnp.exp(scores - new_best[..., None]), 0.0)
            rescale = jnp.exp(row_best - new_best)
            row_total = row_total * rescale + jnp.sum(soft_terms, axis=-1)
            weighted = weighted * rescale[..., None] + jnp.einsum(
                "shqk,skhe->shqe",
                soft_terms.astype(jnp.bfloat16),
                one_block[..., HEAD_DIM:],
                preferred_element_type=jnp.float32,
            )
            return (new_best, row_total, weighted)

        return (lax.cond(offset <= last_query, attend_compute, keep_state, carry_state), None)

    folded, _ = lax.scan(
        attend_block, folded, jnp.arange(piece_len // block_width, dtype=jnp.int32)
    )
    row_best, row_total, weighted = folded
    mixed_exact = weighted / row_total[..., None]
    log_total = row_best + jnp.log(row_total)
    mixed_low = jnp.transpose(mixed_exact, (0, 2, 1, 3)).astype(jnp.bfloat16)
    attn_part = jnp.einsum(
        "sche,hed->scd", mixed_low, attention_out_weight, preferred_element_type=jnp.float32
    )
    residual_one = inputs + reduce_attn(attn_part) + attention_out_bias.astype(jnp.float32)
    second_normed = layer_norm(residual_one, gain_second, shift_second)
    normed_low = second_normed.astype(jnp.bfloat16)
    grad_rows = out_grad.astype(jnp.float32)
    grad_low = grad_rows.astype(jnp.bfloat16)
    rows_two = gather_mlp(normed_low)
    grad_gathered = gather_mlp(grad_low)
    branch_part, normed_grad, fc_grad, fcb_grad, proj_grad = feed_forward(
        rows_two, expand_weight, expand_bias, contract_weight, grad_gathered
    )
    feedforward_branch = reduce_mlp(branch_part)
    dnormed_two = reduce_mlp(normed_grad)
    layer_out = (residual_one + feedforward_branch + contract_bias.astype(jnp.float32)).astype(
        jnp.bfloat16
    )
    pull_two = jax.vjp(layer_norm, residual_one, gain_second, shift_second)[1]
    res_extra, gain_two_grad, shift_two_grad = pull_two(dnormed_two)
    grad_res = grad_rows + res_extra
    attn_grad_rows = gather_attn(grad_res.astype(jnp.bfloat16))
    dmixed = jnp.einsum(
        "scd,hed->sche", attn_grad_rows, attention_out_weight, preferred_element_type=jnp.float32
    ).astype(jnp.bfloat16)
    outw_grad = jnp.einsum(
        "sche,scd->hed", mixed_low, attn_grad_rows, preferred_element_type=jnp.float32
    )
    dmixed_heads = jnp.transpose(dmixed, (0, 2, 1, 3))
    row_delta = jnp.sum(dmixed_heads.astype(jnp.float32) * mixed_exact, axis=-1)
    back_start = (
        jnp.zeros((seq_count, heads_here, span_rows, HEAD_DIM), jnp.float32),
        jnp.zeros((seq_count, full_length, heads_here, 2 * HEAD_DIM), jnp.float32),
    )
    folded = back_start
    back_piece_rows = lax.all_gather(key_value, "ctx", axis=1, tiled=True)
    piece_len = back_piece_rows.shape[1]
    back_block_width = min(piece_len, span_rows)

    def back_block(carry_state, block_index):
        offset = block_index * back_block_width

        def back_compute(inner_state):
            query_grad, pair_grads = inner_state
            one_block = lax.dynamic_slice_in_dim(
                back_piece_rows, block_index * back_block_width, back_block_width, 1
            )
            keys_block = one_block[..., :HEAD_DIM]
            values_block = one_block[..., HEAD_DIM:]
            scores = (
                jnp.einsum(
                    "sqhe,skhe->shqk", queries, keys_block, preferred_element_type=jnp.float32
                )
                * score_scale
            )
            allowed = allowed_mask(offset, back_block_width)
            soft_terms = jnp.where(allowed, jnp.exp(scores - log_total[..., None]), 0.0)
            soft_grad = jnp.einsum(
                "shqe,skhe->shqk", dmixed_heads, values_block, preferred_element_type=jnp.float32
            )
            score_grad = (soft_terms * (soft_grad - row_delta[..., None])).astype(jnp.bfloat16)
            query_grad = query_grad + score_scale * jnp.einsum(
                "shqk,skhe->shqe", score_grad, keys_block, preferred_element_type=jnp.float32
            )
            key_grad = score_scale * jnp.einsum(
                "shqk,sqhe->skhe", score_grad, queries, preferred_element_type=jnp.float32
            )
            value_grad = jnp.einsum(
                "shqk,shqe->skhe",
                soft_terms.astype(jnp.bfloat16),
                dmixed_heads,
                preferred_element_type=jnp.float32,
            )
            earlier = lax.dynamic_slice_in_dim(pair_grads, offset, back_block_width, 1)
            pair_grads = lax.dynamic_update_slice_in_dim(
                pair_grads, earlier + jnp.concatenate([key_grad, value_grad], axis=-1), offset, 1
            )
            return (query_grad, pair_grads)

        return (lax.cond(offset <= last_query, back_compute, keep_state, carry_state), None)

    folded, _ = lax.scan(
        back_block, folded, jnp.arange(piece_len // back_block_width, dtype=jnp.int32)
    )
    query_grad, pair_grads = folded
    pair_mine = lax.psum_scatter(
        pair_grads.astype(jnp.bfloat16), "ctx", scatter_dimension=1, tiled=True
    )
    query_low = jnp.transpose(query_grad, (0, 2, 1, 3)).astype(jnp.bfloat16)
    packed_grad = jnp.concatenate([query_low, pair_mine], axis=-1)
    qkv_grad = jnp.einsum(
        "scd,sche->dhe", rows_one, packed_grad, preferred_element_type=jnp.float32
    )
    qvb_grad = jnp.concatenate(
        [
            jnp.sum(query_low, axis=(0, 1), dtype=jnp.float32),
            jnp.sum(pair_mine[..., HEAD_DIM:], axis=(0, 1), dtype=jnp.float32),
        ],
        axis=-1,
    )
    normed_one_grad = reduce_attn(
        jnp.einsum(
            "sche,dhe->scd", packed_grad, query_key_value_weight, preferred_element_type=jnp.float32
        )
    )
    pull_one = jax.vjp(layer_norm, inputs, gain_first, shift_first)[1]
    input_extra, gain_one_grad, shift_one_grad = pull_one(normed_one_grad)
    grad_tokens = grad_res + input_extra
    small_sums = lax.psum(
        (
            gain_one_grad,
            shift_one_grad,
            jnp.sum(grad_res, axis=(0, 1)),
            gain_two_grad,
            shift_two_grad,
            jnp.sum(grad_rows, axis=(0, 1)),
        ),
        ("ctx", "tp"),
    )
    qkv_grad, qvb_grad, outw_grad, fc_grad, fcb_grad, proj_grad = (
        lax.psum(qkv_grad.astype(jnp.bfloat16), "ctx").astype(jnp.float32),
        lax.psum(qvb_grad.astype(jnp.bfloat16), "ctx").astype(jnp.float32),
        lax.psum(outw_grad.astype(jnp.bfloat16), "ctx").astype(jnp.float32),
        lax.psum(fc_grad.astype(jnp.bfloat16), "ctx").astype(jnp.float32),
        lax.psum(fcb_grad.astype(jnp.bfloat16), "ctx").astype(jnp.float32),
        lax.psum(proj_grad.astype(jnp.bfloat16), "ctx").astype(jnp.float32),
    )
    return (
        layer_out,
        grad_tokens,
        small_sums[0],
        small_sums[1],
        qkv_grad,
        qvb_grad,
        outw_grad,
        small_sums[2],
        small_sums[3],
        small_sums[4],
        fc_grad,
        fcb_grad,
        proj_grad,
        small_sums[5],
    )


def solution(mesh):
    return jax.shard_map(
        shards,
        mesh=mesh,
        in_specs=(
            P(None, ("ctx", "tp"), None),
            P(),
            P(),
            P(None, "tp", None),
            P("tp", None),
            P("tp", None, None),
            P(),
            P(),
            P(),
            P(None, "tp"),
            P("tp"),
            P("tp", None),
            P(),
            P(None, "ctx"),
            P(None, ("ctx", "tp"), None),
        ),
        out_specs=(
            P(None, ("ctx", "tp"), None),
            P(None, ("ctx", "tp"), None),
            P(),
            P(),
            P(None, "tp", None),
            P("tp", None),
            P("tp", None, None),
            P(),
            P(),
            P(),
            P(None, "tp"),
            P("tp"),
            P("tp", None),
            P(),
        ),
        check_vma=False,
    )
```

profile of v0, /device:TPU:0, one launch (start us, length us, event | category | flops | bytes accessed | tf_op | source)
XLA Modules:
  0.0 1086.0 jit_solution(13244537002679323370)
XLA Ops:
  14.9 24.6 %all-gather.6.cloned.1.call-done = bf16[4,256,1024]{2,1,0:T(8,128)(2,1)} async-done(((bf16[4,64,1024]{2,1,0:T(8,128)(2,1)}), bf16[4,256,1024]{2,1,0:T(8,128)(2,1)}) %all-gather.6.cloned.1.call-update) | async-done | bytes 2097168 | tf_op jit(solution)/shard_map/all_gather | solution.py:25
  39.5 3.9 fusion.56
  44.9 30.9 %all_gather.19 = s32[4,2048]{1,0:T(4,128)S(1)} all-gather(s32[4,256]{1,0:T(4,128)S(1)} %copy-done.8), channel_id=1, replica_groups=mesh['ctx'=8,'tp'=4] {'ctx'}, dimensions={1}, use_global_device_ids=true | all-gather | bytes 36864 | tf_op jit(solution)/shard_map/all_gather | solution.py:86
  75.8 94.9 %all-gather.8.cloned.1.call-done = bf16[4,2048,4,128]{1,3,2,0:T(8,128)(2,1)} async-done(((bf16[4,256,4,128]{1,3,2,0:T(8,128)(2,1)}), bf16[4,2048,4,128]{1,3,2,0:T(8,128)(2,1)}) %all-gather.8.cloned.1.call-update) | async-done | bytes 8388624 | tf_op jit(solution)/shard_map/all_gather | solution.py:121
  171.7 17.7 %while.28 = (s32[]{:T(128)}, f32[4,4,256]{2,1,0:T(4,128)S(1)}, f32[4,4,256]{2,1,0:T(4,128)S(1)}, f32[4,4,256,64]{2,3,1,0:T(8,128)}, s32[8]{0:T(128)S(1)}, /*inde...) while((s32[]{:T(128)}, f32[4,4,256]{2,1,0:T(4,128)S(1)}, ...), condition=%wide.region_7.8_spmd.clone, body=%wide.region_2.7_spmd.clone.sunk | while | flops 281092608 | bytes 26106344 | solution.py:158
  173.0 7.3 conditional.6
  189.5 3.5 bitcast_convert_fusion.3
  193.1 80.6 %reduce-scatter.6.cloned.1.call-done = bf16[4,64,1024]{2,1,0:T(8,128)(2,1)} async-done(((bf16[4,256,1024]{2,1,0:T(8,128)(2,1)}), bf16[4,64,1024]{2,1,0:T(8,128)(2,1)}) %reduce-scatter.6.cloned.1.call-update) | async-done | bytes 524304 | tf_op jit(solution)/shard_map/reduce_scatter | solution.py:29
  279.4 21.9 %all-gather.10.cloned.1.call-done = bf16[4,256,1024]{2,1,0:T(8,128)(2,1)} async-done(((bf16[4,64,1024]{2,1,0:T(8,128)(2,1)}), bf16[4,256,1024]{2,1,0:T(8,128)(2,1)}) %all-gather.10.cloned.1.call-update) | async-done | bytes 2097168 | tf_op jit(solution)/shard_map/all_gather | solution.py:35
  301.3 6.6 fusion.64
  307.9 17.5 %all-gather.12.cloned.1.call-done = bf16[4,256,1024]{2,1,0:T(8,128)(2,1)} async-done(((bf16[4,64,1024]{2,1,0:T(8,128)(2,1)}), bf16[4,256,1024]{2,1,0:T(8,128)(2,1)}) %all-gather.12.cloned.1.call-update) | async-done | bytes 2097168 | tf_op jit(solution)/shard_map/all_gather | solution.py:35
  325.4 7.5 fusion.128
  334.2 3.7 fusion.72
  338.0 31.5 %reduce-scatter.10.cloned.1.call-done = bf16[4,64,1024]{2,1,0:T(8,128)(2,1)} async-done(((bf16[4,256,1024]{2,1,0:T(8,128)(2,1)}), bf16[4,64,1024]{2,1,0:T(8,128)(2,1)}) %reduce-scatter.10.cloned.1.call-update) | async-done | bytes 524304 | tf_op jit(solution)/shard_map/reduce_scatter | solution.py:39
  375.9 22.5 %all-gather.14.cloned.1.call-done = bf16[4,256,1024]{2,1,0:T(8,128)(2,1)} async-done(((bf16[4,64,1024]{2,1,0:T(8,128)(2,1)}), bf16[4,256,1024]{2,1,0:T(8,128)(2,1)}) %all-gather.14.cloned.1.call-update) | async-done | bytes 2097168 | tf_op jit(solution)/shard_map/all_gather | solution.py:25
  398.4 3.6 multiply_reduce_fusion
  403.1 7.9 broadcast_in_dim.52
  410.9 35.1 %while.29 = (s32[]{:T(128)}, f32[4,4,256,64]{2,3,1,0:T(8,128)}, f32[4,2048,4,128]{1,3,2,0:T(8,128)}, s32[8]{0:T(128)S(1)}, s32[]{:T(128)}, /*index=5*/s32[4,256]...) while((s32[]{:T(128)}, f32[4,4,256,64]{2,3,1,0:T(8,128)}, ...), condition=%wide.region_19.20_spmd.clone, body=%wide.region_16.0_spmd.clone.sunk | while | flops 683999744 | bytes 40311272 | solution.py:246
  412.2 24.8 %conditional.7 = ((f32[4,4,256,64]{2,3,1,0:T(8,128)}, f32[4,2048,4,128]{1,3,2,0:T(8,128)})) conditional(s32[]{:T(128)} %convert_element_type.381, (f32[4,4,256,64]{2,3,1,0:T(8,128)}, f32[4,2048,4,128]{1,3,2,0:T(8,128)}) %tuple.83, (s32[]{:T(128)}, s32[]{:T(128)}, s32[4,256]{1,0:T(4,128)S(1)}, s32[4,2048]{1,0:T(4,128)S(1)}, s32[]{:T(128)}, ...), branch_computations={%region_17.17_spmd, %region_18.18_spmd} | conditional | flops 683999744 | bytes 40309940 | solution.py:244
  422.2 3.8 maximum_add_fusion
  426.0 10.9 %dynamic_update_slice.2 = f32[4,2048,4,128]{1,3,2,0:T(8,128)} dynamic-update-slice(f32[4,2048,4,128]{1,3,2,0:T(8,128)} %get-tuple-element.186, f32[4,256,4,128]{1,3,2,0:T(8,128)} %maximum_add_fusion, s32[]{:T(128)} %constant.43.clone, s32[]{:T(128)S(6)} %select_n.21, s32[]{:T(128)} %constant.43.clone, s32[]{:T(128)} %constant.43.clone) | dynamic-update-slice | bytes 4194308 | tf_op jit(solution)/shard_map/while/body/eval_jaxpr/cond/branch_1_fun/dynamic_update_slice | solution.py:239
  446.0 9.1 convert_element_type.190
  456.6 320.3 %reduce-scatter.12.cloned.1.call-done = bf16[4,256,4,128]{1,3,2,0:T(8,128)(2,1)} async-done(((bf16[4,2048,4,128]{1,3,2,0:T(8,128)(2,1)}), bf16[4,256,4,128]{1,3,2,0:T(8,128)(2,1)}) %reduce-scatter.12.cloned.1.call-update) | async-done | bytes 1048592 | tf_op jit(solution)/shard_map/reduce_scatter | solution.py:250
  776.9 4.9 bitcast_convert_fusion.2
  781.9 6.3 fusion.69
  788.5 6.3 bitcast_convert_fusion.1
  794.9 4.4 bitcast_convert_fusion
  806.4 19.7 %all-reduce.1 = (bf16[4,128]{1,0:T(4,128)(2,1)S(1)}, bf16[1024]{0:T(1024)(128)(2,1)S(1)}) all-reduce(bf16[4,128]{1,0:T(4,128)(2,1)S(1)} %pad_maximum_fusion.4, bf16[1024]{0:T(1024)(128)(2,1)S(1)} %get-tuple-element.380), channel_id=1, replica_groups=mesh['ctx'=8,'tp'=4] {'ctx'}, use_global_device_ids=true, to_apply=%region_31.32 | all-reduce | flops 1536 | bytes 6144 | tf_op jit(solution)/shard_map/psum | solution.py:286
  831.5 38.4 %all-reduce = (f32[1024]{0:T(1024)}, f32[1024]{0:T(1024)}, f32[1024]{0:T(1024)}, f32[1024]{0:T(1024)}, f32[1024]{0:T(1024)}, /*index=5*/f32[1024]{0:T(1024)}) all-reduce(f32[1024]{0:T(1024)S(1)} %get-tuple-element.300, f32[1024]{0:T(1024)S(1)} %get-tuple-element.301, ...), channel_id=1, replica_groups=mesh['ctx'=8,'tp'=4] {'ctx','tp'}, use_global_device_ids=true, to_apply=%region_25.26 | all-reduce | flops 6144 | bytes 49152 | tf_op jit(solution)/shard_map/psum | solution.py:273
  869.9 3.5 add_add_fusion.2
  873.5 194.8 %all-reduce.5.cloned.1.call-done = (bf16[1024,4,192]{0,2,1:T(8,128)(2,1)}, bf16[4,64,1024]{2,1,0:T(8,128)(2,1)}, bf16[1024,1024]{1,0:T(8,128)(2,1)}, bf16[1024,1024]{1,0:T(8,128)(2,1)}) async-done(((bf16[1024,4,192]{0,2,1:T(8,128)(2,1)}, bf16[4,64,1024]{2,1,0:T(8,128)(2,1)}, bf16[1024,1024]{1,0:T(8,128)(2,1)}, bf16[1024,1024]{1,0:T(8,128)(2,1)}), (bf16[1024,4,192]{0,2,1:T(8,128)(2,1)}, ...) | async-done | bytes 6291472 | tf_op jit(solution)/shard_map/psum | solution.py:285
  1070.6 3.5 convert_element_type.194
  (196 shorter events, 71.8 us)
Async XLA Ops:
  7.2 318.2 %copy-start = (bf16[1024,1024]{1,0:T(8,128)(2,1)S(1)}, bf16[1024,1024]{1,0:T(8,128)(2,1)}, u32[]{:S(2)}) copy-start(bf16[1024,1024]{1,0:T(8,128)(2,1)} %param.34) | copy-start | bytes 6291460
  7.2 32.3 %all-gather.6.cloned.1.call-start = ((), (), s32[]{:S(2)}) async-start(), calls=%async_computation.5 | async-start | bytes 2621440 | tf_op jit(solution)/shard_map/all_gather | solution.py:25
  8.6 34.8 %copy-start.12 = (f32[4,64]{1,0:T(4,128)}, f32[4,64]{1,0:T(4,128)S(1)}, u32[]{:S(2)}) copy-start(f32[4,64]{1,0:T(4,128)S(1)} %broadcast_multiply_fusion.1) | copy-start | bytes 3076
  10.5 32.9 %copy-start.14 = (f32[4,64]{1,0:T(4,128)}, f32[4,64]{1,0:T(4,128)S(1)}, u32[]{:S(2)}) copy-start(f32[4,64]{1,0:T(4,128)S(1)} %fusion.118) | copy-start | bytes 3076
  11.2 32.2 %copy-start.10 = (f32[1024]{0:T(1024)}, f32[1024]{0:T(1024)S(1)}, u32[]{:S(2)}) copy-start(f32[1024]{0:T(1024)S(1)} %convert_element_type.160) | copy-start | bytes 12292
  14.0 156.6 %all-gather.8.cloned.1.call-start = ((), (), s32[]{:S(2)}) async-start(), calls=%async_computation.6 | async-start | bytes 9437184 | tf_op jit(solution)/shard_map/all_gather | solution.py:121
  44.8 228.9 %reduce-scatter.6.cloned.1.call-start = ((), (), s32[]{:S(2)}) async-start(), calls=%async_computation.7 | async-start | bytes 2621440 | tf_op jit(solution)/shard_map/reduce_scatter | solution.py:29
  174.1 3.0 copy-start.2
  189.4 3.6 copy-start.18
  189.4 3.6 copy-start.19
  189.4 3.6 copy-start.20
  189.4 84.2 %copy-start.1 = (bf16[4,64,1024]{2,1,0:T(8,128)(2,1)S(1)}, bf16[4,64,1024]{2,1,0:T(8,128)(2,1)}, u32[]{:S(2)}) copy-start(bf16[4,64,1024]{2,1,0:T(8,128)(2,1)} %param.23) | copy-start | bytes 1572868
  192.9 86.4 %copy-start.21 = (bf16[1024]{0:T(1024)(128)(2,1)S(1)}, bf16[1024]{0:T(1024)(128)(2,1)}, u32[]{:S(2)}) copy-start(bf16[1024]{0:T(1024)(128)(2,1)} %param.33) | copy-start | bytes 6148
  193.0 108.3 %all-gather.10.cloned.1.call-start = ((), (), s32[]{:S(2)}) async-start(), calls=%async_computation.8 | async-start | bytes 2621440 | tf_op jit(solution)/shard_map/all_gather | solution.py:35
  278.6 46.8 %all-gather.12.cloned.1.call-start = ((), (), s32[]{:S(2)}) async-start(), calls=%async_computation.10 | async-start | bytes 2621440 | tf_op jit(solution)/shard_map/all_gather | solution.py:35
  279.2 90.4 %reduce-scatter.10.cloned.1.call-start = ((), (), s32[]{:S(2)}) async-start(), calls=%async_computation.11 | async-start | bytes 2621440 | tf_op jit(solution)/shard_map/reduce_scatter | solution.py:39
  325.4 8.8 copy-start.23
  337.9 60.4 %all-gather.14.cloned.1.call-start = ((), (), s32[]{:S(2)}) async-start(), calls=%async_computation.12 | async-start | bytes 2621440 | tf_op jit(solution)/shard_map/all_gather | solution.py:25
  375.6 401.3 %reduce-scatter.12.cloned.1.call-start = ((), (), s32[]{:S(2)}) async-start(), calls=%async_computation.13 | async-start | bytes 9437184 | tf_op jit(solution)/shard_map/reduce_scatter | solution.py:250
  455.1 372.2 %reduce-scatter.14.cloned.1.call-start = ((), (), s32[]{:S(2)}) async-start(), calls=%async_computation.14 | async-start | bytes 2621440 | tf_op jit(solution)/shard_map/reduce_scatter | solution.py:29
  781.8 88.1 %reduce-scatter.8.cloned.1.call-start = ((), (), s32[]{:S(2)}) async-start(), calls=%async_computation.9 | async-start | bytes 2621440 | tf_op jit(solution)/shard_map/reduce_scatter | solution.py:39
  788.2 280.1 %all-reduce.5.cloned.1.call-start = ((), (), s32[]{:S(2)}) async-start(), calls=%async_computation.15 | async-start | bytes 12582912 | tf_op jit(solution)/shard_map/psum | solution.py:285
  788.5 6.3 copy-start.25
  788.5 6.3 copy-start.28
  794.9 4.4 copy-start.4
  794.9 4.4 copy-start.26
  804.5 22.9 %copy-start.11 = (f32[1024]{0:T(1024)S(1)}, f32[1024]{0:T(1024)}, u32[]{:S(2)}) copy-start(f32[1024]{0:T(1024)} %copy-done.10) | copy-start | bytes 12292
  804.5 22.9 %copy-start.13 = (f32[4,64]{1,0:T(4,128)S(1)}, f32[4,64]{1,0:T(4,128)}, u32[]{:S(2)}) copy-start(f32[4,64]{1,0:T(4,128)} %copy-done.12) | copy-start | bytes 3076
  804.5 24.2 %copy-start.17 = (f32[4,64]{1,0:T(4,128)S(1)}, f32[4,64]{1,0:T(4,128)}, u32[]{:S(2)}) copy-start(f32[4,64]{1,0:T(4,128)} %copy-done.16) | copy-start | bytes 3076
  804.5 24.2 %copy-start.5 = (bf16[4,64,1024]{2,1,0:T(8,128)(2,1)S(1)}, bf16[4,64,1024]{2,1,0:T(8,128)(2,1)}, u32[]{:S(2)}) copy-start(bf16[4,64,1024]{2,1,0:T(8,128)(2,1)} %reduce-scatter.6.cloned.1.call-done) | copy-start | bytes 1572868
  804.5 24.2 %copy-start.15 = (f32[4,64]{1,0:T(4,128)S(1)}, f32[4,64]{1,0:T(4,128)}, u32[]{:S(2)}) copy-start(f32[4,64]{1,0:T(4,128)} %copy-done.14) | copy-start | bytes 3076
  1068.3 5.7 copy-start.7
  (9 other events, 13.4 us)
Sparse Core Ops, SparseCore 0:
  14.1 25.3 all-gather.5
  44.9 125.6 all-gather.7
  193.1 80.5 reduce-scatter.5
  278.7 22.5 all-gather.9
  302.8 22.5 all-gather.11
  338.1 31.4 reduce-scatter.9
  375.8 22.5 all-gather.13
  455.3 321.6 reduce-scatter.11
  782.0 30.4 reduce-scatter.13
  815.4 32.1 reduce-scatter.7
  853.8 214.5 all-reduce.4
where the time goes:
time: 1100 us; the launch traced here: 1090 us
  waiting for transfers between devices  809 us (74%)
  blocking collectives  89 us (8%)
  matrix products  68.3 us (6%)
  other arithmetic  55.2 us (5%)
  local copies, waits for them, and re-layouts  35.6 us (3%)
  between operations  14.7 us (1%)
  loops' own time  12.7 us (1%)
    reduce_scatter x1, waiting for transfers between devices, shards(): lax.psum_scatter(pair_grads.astype(jnp.bfloat16), 'ctx', scatter_dimensio...  320 us
    psum x1, waiting for transfers between devices, shards(): lax.psum(qkv_grad.astype(jnp.bfloat16), 'ctx').astype(jnp.float32)  195 us
    all_gather x1, waiting for transfers between devices, shards(): piece_rows = lax.all_gather(key_value, 'ctx', axis=1, tiled=True)  94.9 us
    reduce_scatter x2, waiting for transfers between devices, reduce_attn(): lax.psum_scatter(values.astype(jnp.bfloat16), 'tp', scatter_dimension=1,...  80.6 us
    all_gather x2, waiting for transfers between devices, gather_attn(): return lax.all_gather(values, 'tp', axis=1, tiled=True)  47.1 us
    all_gather x2, waiting for transfers between devices, gather_mlp(): return lax.all_gather(values, 'tp', axis=1, tiled=True)  39.4 us
    psum x1, blocking collectives, shards(): lax.psum((gain_one_grad, shift_one_grad, jnp.sum(grad_res, axis=(0, 1)),...  38.4 us
    reduce_scatter x2, waiting for transfers between devices, reduce_mlp(): lax.psum_scatter(values.astype(jnp.bfloat16), 'tp', scatter_dimension=1,...  31.5 us
  transfers between devices with their start and end apart: 11, of which 9 were waited for; matrix products, arithmetic and copies ran while one was open for 4% of the time, Pallas kernels for 0%

commit v1 on v0

--- a/solution.py
+++ b/solution.py
@@ -1,6 +1,8 @@
 import jax
 import jax.numpy as jnp
 from jax import lax
+from jax.experimental import pallas as pl
+from jax.experimental.pallas import tpu as pltpu
 from jax.sharding import PartitionSpec as P
 
 HEAD_DIM = 64
@@ -58,7 +60,7 @@
     return (branch_part, normed_grad, fc_grad, fcb_grad, proj_grad)
 
 
-def shards(
+def shards_plain(
     tokens,
     gain_one,
     shift_one,
@@ -307,9 +309,484 @@
     )
 
 
+bf16 = jnp.bfloat16
+f32 = jnp.float32
+BLK = 512
+PAIR = 2 * HEAD_DIM
+DOC_FAR = -(2.0**100)
+CAUSAL_FAR = -2e30
+
+TP_CORE = [(i, i ^ 1) for i in range(4)]
+TP_ROW = [(i, i ^ 2) for i in range(4)]
+CTX_X = [(i, i ^ 1) for i in range(8)]
+CTX_Z1 = [(i, i ^ 2) for i in range(8)]
+CTX_Z2 = [(i, i ^ 4) for i in range(8)]
+CTX_PLANES = [[0, 2, 4, 6], [1, 3, 5, 7]]
+
+
+def after(values, earlier):
+    return lax.optimization_barrier((values, earlier))[0]
+
+
+def contract(a, b, dims):
+    return lax.dot_general(a, b, (dims, ((), ())), preferred_element_type=f32)
+
+
+def lane_half(rows, head):
+    lanes = lax.broadcasted_iota(jnp.int32, (rows, PAIR), 1)
+    return (lanes >= HEAD_DIM) if head else (lanes < HEAD_DIM)
+
+
+def attend_kernel(
+    first_ref, mine_ref, other_ref, qdoc_ref, kdoc_ref, bias_ref,
+    out_mine_ref, out_other_ref, exact_ref, log_ref, key_ref, value_ref, best_ref, total_ref, acc_ref,
+):
+    i = pl.program_id(0)
+    half = BLK // 2
+    rows = pl.ds(pl.multiple_of(i * half, half), half)
+    block = pl.ds(pl.multiple_of(i * BLK, BLK), BLK)
+    packed = jnp.concatenate([mine_ref[rows, :], other_ref[rows, :]], axis=0)
+    queries = packed[:, :PAIR] * jnp.asarray(HEAD_DIM**-0.5, bf16)
+    key_ref[block, :PAIR] = packed[:, PAIR : 2 * PAIR]
+    key_ref[block, PAIR:] = kdoc_ref[block, :]
+    value_ref[block, :] = packed[:, 2 * PAIR :]
+    qdoc = qdoc_ref[block, :]
+    query_heads = [
+        jnp.concatenate([jnp.where(lane_half(BLK, h), queries, jnp.zeros_like(queries)), qdoc], axis=1)
+        for h in range(2)
+    ]
+    best_ref[...] = jnp.full_like(best_ref, neg_fill)
+    total_ref[...] = jnp.zeros_like(total_ref)
+    acc_ref[...] = jnp.zeros_like(acc_ref)
+
+    def visit(j, bias):
+        keys = pl.ds(pl.multiple_of(j * BLK, BLK), BLK)
+        key_block = key_ref[keys, :]
+        value_block = value_ref[keys, :]
+        for h in range(2):
+            scores = contract(key_block, query_heads[h], ((1,), (1,)))
+            if bias is not None:
+                scores = scores + bias
+            old = best_ref[h : h + 1, :]
+            new = jnp.maximum(old, jnp.max(scores, axis=0, keepdims=True))
+            weights = jnp.exp(scores - new)
+            fade = jnp.exp(old - new)
+            total_ref[h : h + 1, :] = total_ref[h : h + 1, :] * fade + jnp.sum(
+                weights, axis=0, keepdims=True
+            )
+            product = contract(value_block, weights.astype(bf16), ((0,), (0,)))
+            part = slice(h * HEAD_DIM, (h + 1) * HEAD_DIM)
+            acc_ref[part, :] = acc_ref[part, :] * fade + product[part, :]
+            best_ref[h : h + 1, :] = new
+
+    def step(j, carry):
+        visit(j, None)
+        return carry
+
+    lax.fori_loop(first_ref[i], i, step, 0)
+    visit(i, bias_ref[...])
+    for h in range(2):
+        part = slice(h * HEAD_DIM, (h + 1) * HEAD_DIM)
+        acc_ref[part, :] = acc_ref[part, :] / total_ref[h : h + 1, :]
+        log_ref[h : h + 1, block] = best_ref[h : h + 1, :] + jnp.log(total_ref[h : h + 1, :])
+    mixed = acc_ref[...]
+    exact_ref[:, block] = mixed
+    low = jnp.transpose(mixed).astype(bf16)
+    out_mine_ref[rows, :] = low[:half]
+    out_other_ref[rows, :] = low[half:]
+
+
+def attend_back_kernel(
+    first_ref, mine_ref, other_ref, qdoc_ref, kdoc_ref, bias_ref, exact_ref, log_ref, dmine_ref, dother_ref,
+    out_mine_ref, out_other_ref, key_ref, value_ref, dkey_ref, dvalue_ref, dquery_ref,
+):
+    i = pl.program_id(0)
+    half = BLK // 2
+    rows = pl.ds(pl.multiple_of(i * half, half), half)
+    block = pl.ds(pl.multiple_of(i * BLK, BLK), BLK)
+    packed = jnp.concatenate([mine_ref[rows, :], other_ref[rows, :]], axis=0)
+    scale = HEAD_DIM**-0.5
+    queries = packed[:, :PAIR] * jnp.asarray(scale, bf16)
+    key_ref[block, :PAIR] = packed[:, PAIR : 2 * PAIR]
+    key_ref[block, PAIR:] = kdoc_ref[block, :]
+    value_ref[block, :] = packed[:, 2 * PAIR :]
+    dkey_ref[block, :] = jnp.zeros((BLK, PAIR), f32)
+    dvalue_ref[block, :] = jnp.zeros((BLK, PAIR), f32)
+    dquery_ref[...] = jnp.zeros_like(dquery_ref)
+    dmixed = jnp.concatenate([dmine_ref[rows, :], dother_ref[rows, :]], axis=0)
+    qdoc = qdoc_ref[block, :]
+    masked = [jnp.where(lane_half(BLK, h), queries, jnp.zeros_like(queries)) for h in range(2)]
+    dmasked = [jnp.where(lane_half(BLK, h), dmixed, jnp.zeros_like(dmixed)) for h in range(2)]
+    query_heads = [jnp.concatenate([masked[h], qdoc], axis=1) for h in range(2)]
+    product = jnp.transpose(dmixed.astype(f32)) * exact_ref[:, block]
+    deltas = [
+        jnp.sum(product[h * HEAD_DIM : (h + 1) * HEAD_DIM, :], axis=0, keepdims=True) for h in range(2)
+    ]
+    logs = [log_ref[h : h + 1, block] for h in range(2)]
+
+    def visit(j, bias):
+        keys = pl.ds(pl.multiple_of(j * BLK, BLK), BLK)
+        key_block = key_ref[keys, :]
+        value_block = value_ref[keys, :]
+        dkey = dkey_ref[keys, :]
+        dvalue = dvalue_ref[keys, :]
+        for h in range(2):
+            scores = contract(key_block, query_heads[h], ((1,), (1,)))
+            if bias is not None:
+                scores = scores + bias
+            weights = jnp.exp(scores - logs[h])
+            dweights = contract(value_block, dmasked[h], ((1,), (1,)))
+            dscores = (weights * (dweights - deltas[h])).astype(bf16)
+            dvalue = dvalue + contract(weights.astype(bf16), dmasked[h], ((1,), (0,)))
+            dkey = dkey + contract(dscores, masked[h], ((1,), (0,)))
+            part = slice(h * HEAD_DIM, (h + 1) * HEAD_DIM)
+            turned = contract(key_block[:, :PAIR], dscores, ((0,), (0,)))
+            dquery_ref[part, :] = dquery_ref[part, :] + turned[part, :]
+        dkey_ref[keys, :] = dkey
+        dvalue_ref[keys, :] = dvalue
+
+    def step(j, carry):
+        visit(j, None)
+        return carry
+
+    lax.fori_loop(first_ref[i], i, step, 0)
+    visit(i, bias_ref[...])
+    dquery = jnp.transpose(dquery_ref[...] * scale).astype(bf16)
+    out_mine_ref[rows, :PAIR] = dquery[:half]
+    out_other_ref[rows, :PAIR] = dquery[half:]
+
+    @pl.when(i == pl.num_programs(0) - 1)
+    def _():
+        for b in range(4):
+            for side, out in ((0, out_mine_ref), (1, out_other_ref)):
+                source = slice(b * BLK + side * half, b * BLK + (side + 1) * half)
+                target = slice(b * half, (b + 1) * half)
+                out[target, PAIR : 2 * PAIR] = dkey_ref[source, :].astype(bf16)
+                out[target, 2 * PAIR :] = dvalue_ref[source, :].astype(bf16)
+
+
+def whole(shape):
+    return pl.BlockSpec(shape, lambda i: (0,) * len(shape))
+
+
+def attend(first, mine, other, qdoc, kdoc, bias):
+    length = qdoc.shape[0]
+    half = length // 2
+    return pl.pallas_call(
+        attend_kernel,
+        grid=(length // BLK,),
+        in_specs=[
+            pl.BlockSpec(memory_space=pltpu.SMEM),
+            whole(mine.shape), whole(other.shape), whole(qdoc.shape), whole(kdoc.shape), whole(bias.shape),
+        ],
+        out_specs=[whole((half, PAIR)), whole((half, PAIR)), whole((PAIR, length)), whole((2, length))],
+        out_shape=[
+            jax.ShapeDtypeStruct((half, PAIR), bf16),
+            jax.ShapeDtypeStruct((half, PAIR), bf16),
+            jax.ShapeDtypeStruct((PAIR, length), f32),
+            jax.ShapeDtypeStruct((2, length), f32),
+        ],
+        scratch_shapes=[
+            pltpu.VMEM((length, 2 * PAIR), bf16),
+            pltpu.VMEM((length, PAIR), bf16),
+            pltpu.VMEM((2, BLK), f32),
+            pltpu.VMEM((2, BLK), f32),
+            pltpu.VMEM((PAIR, BLK), f32),
+        ],
+        compiler_params=pltpu.CompilerParams(
+            dimension_semantics=("arbitrary",), vmem_limit_bytes=40 << 20
+        ),
+        name="attend",
+    )(first, mine, other, qdoc, kdoc, bias)
+
+
+def attend_back(first, mine, other, qdoc, kdoc, bias, exact, log_total, dmine, dother):
+    length = qdoc.shape[0]
+    half = length // 2
+    operands = (mine, other, qdoc, kdoc, bias, exact, log_total, dmine, dother)
+    return pl.pallas_call(
+        attend_back_kernel,
+        grid=(length // BLK,),
+        in_specs=[pl.BlockSpec(memory_space=pltpu.SMEM)] + [whole(o.shape) for o in operands],
+        out_specs=[whole((half, 3 * PAIR)), whole((half, 3 * PAIR))],
+        out_shape=[jax.ShapeDtypeStruct((half, 3 * PAIR), bf16)] * 2,
+        scratch_shapes=[
+            pltpu.VMEM((length, 2 * PAIR), bf16),
+            pltpu.VMEM((length, PAIR), bf16),
+            pltpu.VMEM((length, PAIR), f32),
+            pltpu.VMEM((length, PAIR), f32),
+            pltpu.VMEM((PAIR, BLK), f32),
+        ],
+        compiler_params=pltpu.CompilerParams(
+            dimension_semantics=("arbitrary",), vmem_limit_bytes=48 << 20
+        ),
+        name="attend_back",
+    )(first, *operands)
+
+
+def planes_swap(values):
+    return lax.all_to_all(values, "ctx", 0, 0, axis_index_groups=CTX_PLANES, tiled=False)
+
+
+def tp_gather(values):
+    core = lax.ppermute(values, "tp", TP_CORE)
+    row = lax.ppermute(values, "tp", TP_ROW)
+    both = lax.ppermute(row, "tp", TP_CORE)
+    return [values, core, row, both]
+
+
+def tp_gather_rows(values):
+    return jnp.stack(tp_gather(values), axis=1)
+
+
+def tp_scatter_rows(make_part):
+    away = jnp.stack([make_part(3), make_part(1)]).astype(bf16)
+    came = lax.ppermute(away, "tp", TP_CORE)
+    across = (make_part(2) + came[0].astype(f32)).astype(bf16)
+    arrived = lax.ppermute(across, "tp", TP_ROW)
+    return make_part(0) + came[1].astype(f32) + arrived.astype(f32)
+
+
+def tp_swap(pieces):
+    return [
+        pieces[0],
+        lax.ppermute(pieces[1], "tp", TP_CORE),
+        lax.ppermute(pieces[2], "tp", TP_ROW),
+        lax.ppermute(pieces[3], "tp", [(i, i ^ 3) for i in range(4)]),
+    ]
+
+
+def sum_ctx(values):
+    for perm in (CTX_X, CTX_Z1, CTX_Z2):
+        values = values + lax.ppermute(values, "ctx", perm)
+    return values
+
+
+def sum_all(values):
+    for perm in (TP_CORE, TP_ROW):
+        values = values + lax.ppermute(values, "tp", perm)
+    return sum_ctx(values)
+
+
+def norm_stats(values):
+    centred = values - jnp.mean(values, axis=-1, keepdims=True)
+    rate = lax.rsqrt(jnp.mean(centred * centred, axis=-1, keepdims=True) + eps)
+    return centred * rate, rate
+
+
+def norm_back(hat, rate, gain, grad):
+    dhat = grad * gain
+    return rate * (
+        dhat
+        - jnp.mean(dhat, axis=-1, keepdims=True)
+        - hat * jnp.mean(dhat * hat, axis=-1, keepdims=True)
+    )
+
+
+def order_pair(values, swapped, axis):
+    first, second = jnp.split(values, 2, axis=axis)
+    return jnp.where(
+        swapped,
+        jnp.concatenate([second, first], axis=axis),
+        jnp.concatenate([first, second], axis=axis),
+    )
+
+
+def shards(
+    tokens,
+    gain_one,
+    shift_one,
+    query_key_value_weight,
+    qv_bias,
+    attention_out_weight,
+    attention_out_bias,
+    gain_two,
+    shift_two,
+    expand_weight,
+    expand_bias,
+    contract_weight,
+    contract_bias,
+    doc_ids,
+    out_grad,
+):
+    width = tokens.shape[2]
+    span = doc_ids.shape[1]
+    piece = tokens.shape[1]
+    planes = tokens.shape[0]
+    here = planes * piece
+    group = here * 4
+    ctx_at = lax.axis_index("ctx")
+    tp_at = lax.axis_index("tp")
+    side = ctx_at % 2
+    swapped = side == 1
+    gain_first, shift_first = gain_one.astype(f32), shift_one.astype(f32)
+    gain_second, shift_second = gain_two.astype(f32), shift_two.astype(f32)
+
+    inputs = planes_swap(tokens).astype(f32)
+
+    qkv_heads = query_key_value_weight.reshape(width, 4, 3, HEAD_DIM)
+    qkv_heads = order_pair(qkv_heads, swapped, 1)
+    qkv_rel = jnp.transpose(qkv_heads.reshape(width, 2, 2, 3, HEAD_DIM), (0, 1, 3, 2, 4)).reshape(
+        width, 2, 3 * PAIR
+    )
+    bias_pairs = order_pair(qv_bias.astype(f32), swapped, 0).reshape(2, 2, 2, HEAD_DIM)
+    bias_rel = jnp.concatenate(
+        [
+            bias_pairs[:, :, 0].reshape(2, PAIR),
+            jnp.zeros((2, PAIR), f32),
+            bias_pairs[:, :, 1].reshape(2, PAIR),
+        ],
+        axis=1,
+    )
+    out_rel = order_pair(attention_out_weight.reshape(4 * HEAD_DIM, width), swapped, 0)
+    out_full = jnp.concatenate(tp_gather(out_rel), axis=0)
+
+    ids = lax.all_to_all(doc_ids, "ctx", 0, 0, axis_index_groups=CTX_PLANES, tiled=False)
+    ids = jnp.stack([ids, lax.ppermute(ids, "ctx", CTX_X)], axis=1).reshape(planes, 2, 2, 2, piece)
+    ids = jnp.where(tp_at % 2 == 1, jnp.flip(ids, 3), ids)
+    ids = jnp.where(tp_at // 2 == 1, jnp.flip(ids, 2), ids).reshape(planes, 2 * span)
+    low_id, high_id = jnp.min(ids, axis=1), jnp.max(ids, axis=1)
+    first_block = jnp.sum((high_id[None, :] < low_id[:, None]).astype(jnp.int32), axis=1)
+    lanes = jnp.arange(PAIR, dtype=jnp.int32)
+    same = ids.reshape(-1, 1) == lanes[None, :]
+    kdoc = same.astype(bf16)
+    qdoc = jnp.where(same, 0.0, DOC_FAR).astype(bf16)
+    place = (
+        ((side ^ jnp.arange(2, dtype=jnp.int32)) * span)[:, None, None]
+        + ((tp_at ^ jnp.arange(4, dtype=jnp.int32)) * piece)[None, :, None]
+        + jnp.arange(piece, dtype=jnp.int32)[None, None, :]
+    ).reshape(-1)
+    bias = jnp.where(place[:, None] <= place[None, :], 0.0, CAUSAL_FAR).astype(f32)
+
+    hat_one, rate_one = norm_stats(inputs)
+    rows_one = tp_gather_rows((hat_one * gain_first + shift_first).astype(bf16)).reshape(group, width)
+
+    def project(j):
+        return (
+            jnp.dot(rows_one, qkv_rel[:, j], preferred_element_type=f32) + bias_rel[j]
+        ).astype(bf16)
+
+    qkv_other = lax.ppermute(project(1), "ctx", CTX_X)
+    qkv_mine = project(0)
+
+    grad_rows = planes_swap(after(out_grad, qkv_mine))
+    grad_gathered = tp_gather_rows(grad_rows).reshape(group, width)
+    grad_rows = grad_rows.astype(f32)
+    act_grad = contract(grad_gathered, contract_weight, ((1,), (1,)))
+
+    mixed_mine, mixed_other, exact, log_total = attend(
+        first_block, qkv_mine, qkv_other, qdoc, kdoc, bias
+    )
+    mixed_heads = jnp.concatenate([mixed_mine, lax.ppermute(mixed_other, "ctx", CTX_X)], axis=1)
+    by_tp = mixed_heads.reshape(planes, 4, piece, 2 * PAIR)
+    mixed_rows = jnp.concatenate(tp_swap([by_tp[:, k] for k in range(4)]), axis=-1)
+    attn_branch = jnp.dot(
+        mixed_rows.reshape(here, width), out_full, preferred_element_type=f32
+    ).reshape(planes, piece, width)
+    residual_one = inputs + attn_branch + attention_out_bias.astype(f32)
+
+    hat_two, rate_two = norm_stats(residual_one)
+    rows_two = tp_gather_rows((hat_two * gain_second + shift_second).astype(bf16)).reshape(group, width)
+    pre_act = jnp.dot(rows_two, expand_weight, preferred_element_type=f32) + expand_bias.astype(f32)
+    active, pull_gelu = jax.vjp(gelu_tanh, pre_act)
+    active = active.astype(bf16)
+    dpre = pull_gelu(act_grad)[0].astype(bf16)
+    dpre_parts = dpre.reshape(planes, 4, piece, -1)
+    dnormed_two = tp_scatter_rows(
+        lambda k: contract(
+            dpre_parts[:, k].reshape(here, -1), expand_weight, ((1,), (1,))
+        ).reshape(planes, piece, width)
+    )
+    fc_grad = contract(rows_two, dpre, ((0,), (0,)))
+    proj_grad = contract(active, grad_gathered, ((0,), (0,)))
+    fcb_grad = jnp.sum(dpre, axis=0, dtype=f32)
+    fc_grad, proj_grad = lax.psum((fc_grad.astype(bf16), proj_grad.astype(bf16)), "ctx")
+
+    grad_res = grad_rows + norm_back(hat_two, rate_two, gain_second, dnormed_two)
+    attn_grad = grad_res.astype(bf16)
+    dmixed = contract(attn_grad.reshape(here, width), out_full, ((1,), (1,))).astype(bf16)
+    dmixed = dmixed.reshape(planes, piece, 4, 2 * PAIR)
+    dmixed = jnp.stack(tp_swap([dmixed[:, :, k] for k in range(4)]), axis=1).reshape(group, 2 * PAIR)
+    dmixed_other = lax.ppermute(dmixed[:, PAIR:], "ctx", CTX_X)
+    grad_mine, grad_other = attend_back(
+        first_block, qkv_mine, qkv_other, qdoc, kdoc, bias, exact, log_total, dmixed[:, :PAIR], dmixed_other
+    )
+    packed_grad = jnp.concatenate([grad_mine, lax.ppermute(grad_other, "ctx", CTX_X)], axis=1)
+
+    branch_in = after(active, dmixed_other).reshape(planes, 4, piece, -1)
+    feedforward_branch = tp_scatter_rows(
+        lambda k: jnp.dot(
+            branch_in[:, k].reshape(here, -1), contract_weight, preferred_element_type=f32
+        ).reshape(planes, piece, width)
+    )
+    layer_out = planes_swap(
+        (residual_one + feedforward_branch + contract_bias.astype(f32)).astype(bf16)
+    )
+
+    attn_grad_rows = tp_gather_rows(after(attn_grad, dmixed_other)).reshape(group, width)
+    outw_grad = contract(mixed_heads, attn_grad_rows, ((0,), (0,)))
+    outw_grad = order_pair(outw_grad.astype(bf16), swapped, 0)
+
+    qkv_flat = qkv_rel.reshape(width, 6 * PAIR)
+    packed_parts = packed_grad.reshape(planes, 4, piece, 6 * PAIR)
+    dnormed_one = tp_scatter_rows(
+        lambda k: contract(
+            packed_parts[:, k].reshape(here, -1), qkv_flat, ((1,), (1,))
+        ).reshape(planes, piece, width)
+    )
+    qkv_grad = contract(rows_one, packed_grad, ((0,), (0,))).astype(bf16)
+    qkv_grad, outw_grad = lax.psum((qkv_grad_order(qkv_grad, swapped), outw_grad), "ctx")
+    bias_sums = jnp.sum(packed_grad, axis=0, dtype=f32)[None]
+    bias_sums = qkv_grad_order(bias_sums, swapped).reshape(4, 3, HEAD_DIM)
+    qvb_grad = jnp.concatenate([bias_sums[:, 0], bias_sums[:, 2]], axis=-1)
+
+    grad_tokens = grad_res + norm_back(hat_one, rate_one, gain_first, dnormed_one)
+    grad_tokens = planes_swap(grad_tokens.astype(bf16)).astype(f32)
+
+    early = sum_all(
+        jnp.stack(
+            [
+                jnp.sum(grad_res, axis=(0, 1)),
+                jnp.sum(dnormed_two * hat_two, axis=(0, 1)),
+                jnp.sum(dnormed_two, axis=(0, 1)),
+                jnp.sum(grad_rows, axis=(0, 1)),
+            ]
+        )
+    )
+    late = sum_all(
+        jnp.stack([jnp.sum(dnormed_one * hat_one, axis=(0, 1)), jnp.sum(dnormed_one, axis=(0, 1))])
+    )
+    fcb_grad = sum_ctx(fcb_grad)
+    qvb_grad = sum_ctx(qvb_grad)
+    return (
+        layer_out,
+        grad_tokens,
+        late[0],
+        late[1],
+        qkv_grad.astype(f32),
+        qvb_grad,
+        outw_grad.astype(f32).reshape(4, HEAD_DIM, width),
+        early[0],
+        early[1],
+        early[2],
+        fc_grad.astype(f32),
+        fcb_grad,
+        proj_grad.astype(f32),
+        early[3],
+    )
+
+
+def qkv_grad_order(values, swapped):
+    rows = values.shape[0]
+    values = jnp.transpose(values.reshape(rows, 2, 3, 2, HEAD_DIM), (0, 1, 3, 2, 4))
+    return order_pair(values, swapped, 1).reshape(rows, 4, 3 * HEAD_DIM)
+
+
 def solution(mesh):
+    sizes = dict(zip(mesh.axis_names, mesh.devices.shape))
+    body = shards if (sizes["ctx"], sizes["tp"]) == (8, 4) else shards_plain
     return jax.shard_map(
-        shards,
+        body,
         mesh=mesh,
         in_specs=(
             P(None, ("ctx", "tp"), None),

time: 1100 us -> 512 us (0.47)
  waiting for transfers between devices: 809 us -> 284 us
  blocking collectives: 89 us -> 0 us
  starting transfers between devices: 1.09 us -> 66.5 us
  Pallas kernels: 0 us -> 24.7 us
  matrix products: 68.3 us -> 47.5 us
  other arithmetic: 55.2 us -> 37.6 us
  loops' own time: 12.7 us -> 0 us
    reduce_scatter x5 -> x0, waiting for transfers between devices: 432 us -> none  [the longest x1 320 us: shards(): lax.psum_scatter(pair_grads.astype(jnp.bfloat16), 'ctx', scatter_dimensio...]
    all_gather x5 -> x0, waiting for transfers between devices: 181 us -> none  [the longest x1 94.9 us: shards(): piece_rows = lax.all_gather(key_value, 'ctx', axis=1, tiled=True)]
    ppermute x0 -> x48, waiting for transfers between devices: none -> 128 us  [the longest x5 38.9 us: tp_gather(): row = lax.ppermute(values, 'tp', TP_ROW)]
    psum x1, waiting for transfers between devices: 195 us -> 132 us  [shards(): lax.psum((qkv_grad_order(qkv_grad, swapped), outw_grad), 'ctx')]
    psum x2 -> x0, blocking collectives: 58.1 us -> none  [the longest x1 38.4 us: shards(): lax.psum((gain_one_grad, shift_one_grad, jnp.sum(grad_res, axis=(0, 1)),...]
    ppermute x0 -> x48, starting transfers between devices: none -> 40.7 us  [the longest x12 18 us: sum_ctx(): values = values + lax.ppermute(values, 'ctx', perm)]
    all_gather x1 -> x0, blocking collectives: 30.9 us -> none  [shards(): all_ids = lax.all_gather(doc_ids, 'ctx', axis=1, tiled=True)]
    all_to_all x0 -> x5, starting transfers between devices: none -> 25.7 us  [the longest x4 19.3 us: planes_swap(): lax.all_to_all(values, 'ctx', 0, 0, axis_index_groups=CTX_PLANES, tiled=F...]
  transfers between devices with their start and end apart: 11 -> 54, of which waited for: 9 -> 25; matrix products, arithmetic and copies ran while one was open for 4% -> 13% of each run, Pallas kernels for 0% -> 2%
where the time goes in v1:
time: 512 us; the launch traced here: 506 us
  waiting for transfers between devices  284 us (55%)
  starting transfers between devices  66.5 us (13%)
  matrix products  47.5 us (9%)
  other arithmetic  37.6 us (7%)
  local copies, waits for them, and re-layouts  30.1 us (6%)
  Pallas kernels  24.7 us (5%)
  between operations  15.3 us (3%)
    psum x1, waiting for transfers between devices, shards(): lax.psum((qkv_grad_order(qkv_grad, swapped), outw_grad), 'ctx')  132 us
    ppermute x5, waiting for transfers between devices, tp_gather(): row = lax.ppermute(values, 'tp', TP_ROW)  38.9 us
    dot_general x14, matrix products, contract(): return lax.dot_general(a, b, (dims, ((), ())), preferred_element_type=f32)  29.4 us
    all_to_all x4, waiting for transfers between devices, planes_swap(): lax.all_to_all(values, 'ctx', 0, 0, axis_index_groups=CTX_PLANES, tiled=F...  25 us
    ppermute x12, waiting for transfers between devices, sum_ctx(): values = values + lax.ppermute(values, 'ctx', perm)  23.6 us
    ppermute x3, waiting for transfers between devices, tp_scatter_rows(): arrived = lax.ppermute(across, 'tp', TP_ROW)  23.5 us
    all_to_all x4, starting transfers between devices, planes_swap(): lax.all_to_all(values, 'ctx', 0, 0, axis_index_groups=CTX_PLANES, tiled=F...  19.3 us
    ppermute x12, starting transfers between devices, sum_ctx(): values = values + lax.ppermute(values, 'ctx', perm)  18 us
  transfers between devices with their start and end apart: 54, of which 25 were waited for; matrix products, arithmetic and copies ran while one was open for 13% of the time, Pallas kernels for 2%

profile of v1, /device:TPU:0, one launch (start us, length us, event | category | flops | bytes accessed | tf_op | source)
XLA Modules:
  0.0 505.8 jit_solution(3923536458112182848)
XLA Ops:
  8.6 6.3 %all-to-all-start.1 = ((s32[4,1,256]{2,1,0:T(1,128)}), s32[4,1,256]{2,1,0:T(1,128)S(1)}, u32[]{:S(2)}, u32[]{:S(2)}) async-start(s32[4,1,256]{2,1,0:T(1,128)} %all_to_all.21), calls=%async_computation.1 | async-start | bytes 8192 | tf_op jit(solution)/shard_map/all_to_all | solution.py:644
  21.5 5.1 %all-to-all-start = ((bf16[4,64,1024]{2,1,0:T(8,128)(2,1)}), bf16[4,64,1024]{2,1,0:T(8,128)(2,1)}, u32[]{:S(2)}, u32[]{:S(2)}) async-start(bf16[4,64,1024]{2,1,0:T(8,128)(2,1)} %param.15), calls=%async_computation | async-start | bytes 1048576 | tf_op jit(solution)/shard_map/all_to_all | solution.py:528
  34.0 6.3 %all-to-all-done = bf16[4,64,1024]{2,1,0:T(8,128)(2,1)} async-done(((bf16[4,64,1024]{2,1,0:T(8,128)(2,1)}), bf16[4,64,1024]{2,1,0:T(8,128)(2,1)}, u32[]{:S(2)}, u32[]{:S(2)}) %all-to-all-start) | async-done | bytes 524320 | tf_op jit(solution)/shard_map/all_to_all | solution.py:528
  45.9 12.3 %collective-permute-done.2 = bf16[4,64,1024]{2,1,0:T(8,128)(2,1)} collective-permute-done((bf16[4,64,1024]{2,1,0:T(8,128)(2,1)}, bf16[4,64,1024]{2,1,0:T(8,128)(2,1)}, u32[]{:S(2)}, u32[]{:S(2)}) %collective-permute-start.2) | collective-permute-done | bytes 524320 | tf_op jit(solution)/shard_map/ppermute | solution.py:533
  70.9 4.1 all-to-all-start.2
  75.5 10.8 %collective-permute-done.4.other_ref = bf16[1024,384]{1,0:T(8,128)(2,1)} collective-permute-done((bf16[1024,384]{1,0:T(8,128)(2,1)}, bf16[1024,384]{1,0:T(8,128)(2,1)}, u32[]{:S(2)}, u32[]{:S(2)}) %collective-permute-start.4) | collective-permute-done | bytes 786464 | tf_op jit(solution)/shard_map/ppermute | solution.py:669
  89.6 10.9 %attend.1 = (bf16[1024,128]{1,0:T(8,128)(2,1)S(1)}, bf16[1024,128]{1,0:T(8,128)(2,1)S(1)}, f32[128,2048]{1,0:T(8,128)S(1)}, f32[2,2048]{1,0:T(2,128)S(1)}) custom-call(s32[4]{0:T(128)S(1)} %convert_reduce_fusion.4.first_ref, bf16[1024,384]{1,0:T(8,128)(2,1)S(1)} %copy-done.5, bf16[1024,384]{1,0:T(8,128)(2,1)} %collective-permute-done.4.other_ref, ...), custom_call_target="tpu_custom_call" | custom-call | tf_op jit(solution)/shard_map/attend/pallas_call | solution.py:475
  103.5 5.9 %collective-permute-done.5 = bf16[1024,128]{1,0:T(8,128)(2,1)S(1)} collective-permute-done((bf16[1024,128]{1,0:T(8,128)(2,1)S(1)}, bf16[1024,128]{1,0:T(8,128)(2,1)S(1)}, u32[]{:S(2)}, u32[]{:S(2)}) %collective-permute-start.5) | collective-permute-done | bytes 262176 | tf_op jit(solution)/shard_map/ppermute | solution.py:680
  113.6 4.1 collective-permute-done.7
  123.9 7.7 %collective-permute-done.16 = bf16[4,64,1024]{2,1,0:T(8,128)(2,1)S(1)} collective-permute-done((bf16[4,64,1024]{2,1,0:T(8,128)(2,1)}, bf16[4,64,1024]{2,1,0:T(8,128)(2,1)S(1)}, u32[]{:S(2)}, u32[]{:S(2)}) %collective-permute-start.16) | collective-permute-done | bytes 524320 | tf_op jit(solution)/shard_map/ppermute | solution.py:533
  132.1 10.3 %collective-permute-done.13 = bf16[4,64,1024]{2,1,0:T(8,128)(2,1)S(1)} collective-permute-done((bf16[4,64,1024]{2,1,0:T(8,128)(2,1)S(1)}, bf16[4,64,1024]{2,1,0:T(8,128)(2,1)S(1)}, u32[]{:S(2)}, u32[]{:S(2)}) %collective-permute-start.13) | collective-permute-done | bytes 524320 | tf_op jit(solution)/shard_map/ppermute | solution.py:533
  149.8 6.5 %convert_reduce_fusion = (f32[1024]{0:T(1024)S(1)}, bf16[1024,1024]{1,0:T(8,128)(2,1)S(1)}, bf16[1024,1024]{1,0:T(8,128)(2,1)}) fusion(f32[1024,1024]{1,0:T(8,128)S(1)} %fusion.113, f32[1024]{0:T(1024)S(1)} %convert_element_type.171, bf16[1024,1024]{1,0:T(8,128)(2,1)S(1)} %bitcast.315, bf16[1024,1024]{1,0:T(8,128)(2,1)S(1)} %copy-done), kind=kOutput, calls=%fused_computation.9 | convolution fusion | flops 2173697024 | bytes 12591104 | tf_op jit(solution)/shard_map/dot_general | solution.py:332
  162.9 12.9 %collective-permute-done.19 = bf16[4,64,1024]{2,1,0:T(8,128)(2,1)S(1)} collective-permute-done((bf16[4,64,1024]{2,1,0:T(8,128)(2,1)S(1)}, bf16[4,64,1024]{2,1,0:T(8,128)(2,1)S(1)}, u32[]{:S(2)}, u32[]{:S(2)}) %collective-permute-start.19) | collective-permute-done | bytes 524320 | tf_op jit(solution)/shard_map/ppermute | solution.py:546
  179.9 3.1 convolution_convert_fusion.4
  190.3 4.3 collective-permute-done.21
  198.3 6.9 %collective-permute-done.23.dother_ref = bf16[1024,128]{1,0:T(8,128)(2,1)S(1)} collective-permute-done((bf16[1024,128]{1,0:T(8,128)(2,1)S(1)}, bf16[1024,128]{1,0:T(8,128)(2,1)S(1)}, u32[]{:S(2)}, u32[]{:S(2)}) %collective-permute-start.23) | collective-permute-done | bytes 262176 | tf_op jit(solution)/shard_map/ppermute | solution.py:710
  205.2 13.8 %attend_back.1 = (bf16[1024,384]{1,0:T(8,128)(2,1)S(1)}, bf16[1024,384]{1,0:T(8,128)(2,1)S(1)}) custom-call(s32[4]{0:T(128)S(1)} %convert_reduce_fusion.4.first_ref, bf16[1024,384]{1,0:T(8,128)(2,1)S(1)} %copy-done.6, bf16[1024,384]{1,0:T(8,128)(2,1)} %collective-permute-done.4.other_ref, bf16[2048,128]{1,0:T(8,128)(2,1)S(1)} %copy-done.4, ...), custom_call_target="tpu_custom_call" | custom-call | tf_op jit(solution)/shard_map/attend_back/pallas_call | solution.py:507
  220.6 3.7 convolution_convert_fusion.1
  224.9 3.8 convolution_convert_fusion
  228.7 8.6 %collective-permute-done.38 = bf16[4,64,1024]{2,1,0:T(8,128)(2,1)S(1)} collective-permute-done((bf16[4,64,1024]{2,1,0:T(8,128)(2,1)S(1)}, bf16[4,64,1024]{2,1,0:T(8,128)(2,1)S(1)}, u32[]{:S(2)}, u32[]{:S(2)}) %collective-permute-start.38) | collective-permute-done | bytes 524320 | tf_op jit(solution)/shard_map/ppermute | solution.py:533
  255.6 3.1 collective-permute-done.45
  258.7 6.5 %collective-permute-start.46 = (f32[1024]{0:T(1024)S(1)}, f32[1024]{0:T(1024)S(1)}, u32[]{:S(2)}, u32[]{:S(2)}) collective-permute-start(f32[1024]{0:T(1024)S(1)} %add.283), channel_id=1, source_target_pairs={{0,8},{4,12},{8,0},{12,4},{16,24},{20,28},{24,16},{28,20},{1,9},{5... | collective-permute-start | bytes 12296 | tf_op jit(solution)/shard_map/ppermute | solution.py:561
  272.5 10.3 %collective-permute-done.25 = bf16[4,64,1024]{2,1,0:T(8,128)(2,1)S(1)} collective-permute-done((bf16[4,64,1024]{2,1,0:T(8,128)(2,1)S(1)}, bf16[4,64,1024]{2,1,0:T(8,128)(2,1)S(1)}, u32[]{:S(2)}, u32[]{:S(2)}) %collective-permute-start.25) | collective-permute-done | bytes 524320 | tf_op jit(solution)/shard_map/ppermute | solution.py:546
  285.7 5.8 %all-to-all-start.3 = ((bf16[4,64,1024]{2,1,0:T(8,128)(2,1)}), bf16[4,64,1024]{2,1,0:T(8,128)(2,1)S(1)}, u32[]{:S(2)}, u32[]{:S(2)}) async-start(bf16[4,64,1024]{2,1,0:T(8,128)(2,1)} %fusion.77), calls=%async_computation.3 | async-start | bytes 1048576 | tf_op jit(solution)/shard_map/all_to_all | solution.py:528
  291.8 3.0 fusion.71
  300.7 18.7 %all-to-all-done.3 = bf16[4,64,1024]{2,1,0:T(8,128)(2,1)S(1)} async-done(((bf16[4,64,1024]{2,1,0:T(8,128)(2,1)}), bf16[4,64,1024]{2,1,0:T(8,128)(2,1)S(1)}, u32[]{:S(2)}, u32[]{:S(2)}) %all-to-all-start.3) | async-done | bytes 524320 | tf_op jit(solution)/shard_map/all_to_all | solution.py:528
  319.4 4.3 all-to-all-start.4
  323.8 3.0 collective-permute-start.47
  329.4 19.6 %collective-permute-done.47 = f32[1024]{0:T(1024)S(1)} collective-permute-done((f32[1024]{0:T(1024)S(1)}, f32[1024]{0:T(1024)S(1)}, u32[]{:S(2)}, u32[]{:S(2)}) %collective-permute-start.47) | collective-permute-done | bytes 4128 | tf_op jit(solution)/shard_map/ppermute | solution.py:561
  349.8 3.0 collective-permute-start.33
  356.5 131.5 %all-reduce.3.cloned.1.call-done = (bf16[1024,4,192]{0,2,1:T(8,128)(2,1)}, bf16[4,64,1024]{2,1,0:T(8,128)(2,1)}, bf16[1024,1024]{1,0:T(8,128)(2,1)}, bf16[1024,1024]{1,0:T(8,128)(2,1)}) async-done(((bf16[1024,4,192]{0,2,1:T(8,128)(2,1)}, bf16[4,64,1024]{2,1,0:T(8,128)(2,1)}, bf16[1024,1024]{1,0:T(8,128)(2,1)}, bf16[1024,1024]{1,0:T(8,128)(2,1)}), (bf16[1024,4,192]{0,2,1:T(8,128)(2,1)}, ...) | async-done | bytes 6291472 | tf_op jit(solution)/shard_map/psum | solution.py:738
  488.1 4.2 convert_element_type.204
  (309 shorter events, 130.0 us)
Async XLA Ops:
  8.6 12.8 %all-to-all-start.1 = ((s32[4,1,256]{2,1,0:T(1,128)}), s32[4,1,256]{2,1,0:T(1,128)S(1)}, u32[]{:S(2)}, u32[]{:S(2)}) async-start(s32[4,1,256]{2,1,0:T(1,128)} %all_to_all.21), calls=%async_computation.1 | async-start | bytes 8192 | tf_op jit(solution)/shard_map/all_to_all | solution.py:644
  17.0 86.0 %collective-permute-start.10 = (bf16[256,1024]{1,0:T(8,128)(2,1)}, bf16[256,1024]{1,0:T(8,128)(2,1)}, u32[]{:S(2)}, u32[]{:S(2)}) collective-permute-start(bf16[256,1024]{1,0:T(8,128)(2,1)} %maximum_select_fusion.1), channel_id=1, source_target_pairs={{0,2},{1,3},{2,0},{3,1},{4,6},{5,7},{6,4},{7,5},{8,10},{9,11},{10,... | collective-permute-start | bytes 1572872 | tf_op jit(solution)/shard_map/ppermute | solution.py:533
  21.5 18.8 %all-to-all-start = ((bf16[4,64,1024]{2,1,0:T(8,128)(2,1)}), bf16[4,64,1024]{2,1,0:T(8,128)(2,1)}, u32[]{:S(2)}, u32[]{:S(2)}) async-start(bf16[4,64,1024]{2,1,0:T(8,128)(2,1)} %param.15), calls=%async_computation | async-start | bytes 1048576 | tf_op jit(solution)/shard_map/all_to_all | solution.py:528
  45.0 13.2 %collective-permute-start.2 = (bf16[4,64,1024]{2,1,0:T(8,128)(2,1)}, bf16[4,64,1024]{2,1,0:T(8,128)(2,1)}, u32[]{:S(2)}, u32[]{:S(2)}) collective-permute-start(bf16[4,64,1024]{2,1,0:T(8,128)(2,1)} %fusion.65), channel_id=1, source_target_pairs={{0,2},{1,3},{2,0},{3,1},{4,6},{5,7},{6,4},{7,5},{8,10},{9,11},{10,... | collective-permute-start | bytes 1572872 | tf_op jit(solution)/shard_map/ppermute | solution.py:533
  45.9 14.7 %collective-permute-start.1 = (bf16[4,64,1024]{2,1,0:T(8,128)(2,1)}, bf16[4,64,1024]{2,1,0:T(8,128)(2,1)S(1)}, u32[]{:S(2)}, u32[]{:S(2)}) collective-permute-start(bf16[4,64,1024]{2,1,0:T(8,128)(2,1)} %fusion.65), channel_id=1, source_target_pairs={{0,1},{1,0},{2,3},{3,2},{4,5},{5,4},{6,7},{7,6},{8,9},{9,8},{10,11... | collective-permute-start | bytes 1572872 | tf_op jit(solution)/shard_map/ppermute | solution.py:532
  66.1 20.3 %collective-permute-start.4 = (bf16[1024,384]{1,0:T(8,128)(2,1)}, bf16[1024,384]{1,0:T(8,128)(2,1)}, u32[]{:S(2)}, u32[]{:S(2)}) collective-permute-start(bf16[1024,384]{1,0:T(8,128)(2,1)} %add_convert_fusion), channel_id=1, source_target_pairs={{0,4},{4,0},{8,12},{12,8},{16,20},{20,16},{24,28},{28,24},{1,5},{5... | collective-permute-start | bytes 2359304 | tf_op jit(solution)/shard_map/ppermute | solution.py:669
  70.9 42.0 %all-to-all-start.2 = ((bf16[4,64,1024]{2,1,0:T(8,128)(2,1)}), bf16[4,64,1024]{2,1,0:T(8,128)(2,1)}, u32[]{:S(2)}, u32[]{:S(2)}) async-start(bf16[4,64,1024]{2,1,0:T(8,128)(2,1)} %param.29), calls=%async_computation.2 | async-start | bytes 1048576 | tf_op jit(solution)/shard_map/all_to_all | solution.py:528
  75.1 413.0 %all-reduce.3.cloned.1.call-start = ((), (), s32[]{:S(2)}) async-start(), calls=%async_computation.5 | async-start | bytes 12582912 | tf_op jit(solution)/shard_map/psum | solution.py:738
  103.0 10.6 %collective-permute-start.11 = (bf16[256,1024]{1,0:T(8,128)(2,1)}, bf16[256,1024]{1,0:T(8,128)(2,1)}, u32[]{:S(2)}, u32[]{:S(2)}) collective-permute-start(bf16[256,1024]{1,0:T(8,128)(2,1)} %collective-permute-done.10), channel_id=1, source_target_pairs={{0,1},{1,0},{2,3},{3,2},{4,5},{5,4},{6,7},{7,6},{8,9},{9,8},{10,11... | collective-permute-start | bytes 1572872 | tf_op jit(solution)/shard_map/ppermute | solution.py:534
  113.0 18.6 %collective-permute-start.16 = (bf16[4,64,1024]{2,1,0:T(8,128)(2,1)}, bf16[4,64,1024]{2,1,0:T(8,128)(2,1)S(1)}, u32[]{:S(2)}, u32[]{:S(2)}) collective-permute-start(bf16[4,64,1024]{2,1,0:T(8,128)(2,1)} %all-to-all-done.2), channel_id=1, source_target_pairs={{0,2},{1,3},{2,0},{3,1},{4,6},{5,7},{6,4},{7,5},{8,10},{9,11},{10,... | collective-permute-start | bytes 1572872 | tf_op jit(solution)/shard_map/ppermute | solution.py:533
  123.0 19.5 %collective-permute-start.13 = (bf16[4,64,1024]{2,1,0:T(8,128)(2,1)S(1)}, bf16[4,64,1024]{2,1,0:T(8,128)(2,1)S(1)}, u32[]{:S(2)}, u32[]{:S(2)}) collective-permute-start(bf16[4,64,1024]{2,1,0:T(8,128)(2,1)S(1)} %add_convert_fusion.2), channel_id=1, source_target_pairs={{0,2},{1,3},{2,0},{3,1},{4,6},{5,7},{6,4},{7,5},{8,10},{9,11},{10,... | collective-permute-start | bytes 1572872 | tf_op jit(solution)/shard_map/ppermute | solution.py:533
  123.5 19.2 %collective-permute-start.15 = (bf16[4,64,1024]{2,1,0:T(8,128)(2,1)}, bf16[4,64,1024]{2,1,0:T(8,128)(2,1)S(1)}, u32[]{:S(2)}, u32[]{:S(2)}) collective-permute-start(bf16[4,64,1024]{2,1,0:T(8,128)(2,1)} %all-to-all-done.2), channel_id=1, source_target_pairs={{0,1},{1,0},{2,3},{3,2},{4,5},{5,4},{6,7},{7,6},{8,9},{9,8},{10,11... | collective-permute-start | bytes 1572872 | tf_op jit(solution)/shard_map/ppermute | solution.py:532
  131.6 11.1 %collective-permute-start.17 = (bf16[4,64,1024]{2,1,0:T(8,128)(2,1)S(1)}, bf16[4,64,1024]{2,1,0:T(8,128)(2,1)S(1)}, u32[]{:S(2)}, u32[]{:S(2)}) collective-permute-start(bf16[4,64,1024]{2,1,0:T(8,128)(2,1)S(1)} %collective-permute-done.16), channel_id=1, source_target_pairs={{0,1},{1,0},{2,3},{3,2},{4,5},{5,4},{6,7},{7,6},{8,9},{9,8},{10,11... | collective-permute-start | bytes 1572872 | tf_op jit(solution)/shard_map/ppermute | solution.py:534
  131.6 12.7 %collective-permute-start.12 = (bf16[4,64,1024]{2,1,0:T(8,128)(2,1)S(1)}, bf16[4,64,1024]{2,1,0:T(8,128)(2,1)S(1)}, u32[]{:S(2)}, u32[]{:S(2)}) collective-permute-start(bf16[4,64,1024]{2,1,0:T(8,128)(2,1)S(1)} %add_convert_fusion.2), channel_id=1, source_target_pairs={{0,1},{1,0},{2,3},{3,2},{4,5},{5,4},{6,7},{7,6},{8,9},{9,8},{10,11... | collective-permute-start | bytes 1572872 | tf_op jit(solution)/shard_map/ppermute | solution.py:532
  161.5 14.3 %collective-permute-start.19 = (bf16[4,64,1024]{2,1,0:T(8,128)(2,1)S(1)}, bf16[4,64,1024]{2,1,0:T(8,128)(2,1)S(1)}, u32[]{:S(2)}, u32[]{:S(2)}) collective-permute-start(bf16[4,64,1024]{2,1,0:T(8,128)(2,1)S(1)} %fusion.78), channel_id=1, source_target_pairs={{0,2},{1,3},{2,0},{3,1},{4,6},{5,7},{6,4},{7,5},{8,10},{9,11},{10,... | collective-permute-start | bytes 1572872 | tf_op jit(solution)/shard_map/ppermute | solution.py:546
  219.1 18.9 %collective-permute-start.26 = (bf16[1024,384]{1,0:T(8,128)(2,1)S(1)}, bf16[1024,384]{1,0:T(8,128)(2,1)S(1)}, u32[]{:S(2)}, u32[]{:S(2)}) collective-permute-start(bf16[1024,384]{1,0:T(8,128)(2,1)S(1)} %get-tuple-element.30), channel_id=1, source_target_pairs={{0,4},{4,0},{8,12},{12,8},{16,20},{20,16},{24,28},{28,24},{1,5},{5... | collective-permute-start | bytes 2359304 | tf_op jit(solution)/shard_map/ppermute | solution.py:714
  224.3 13.0 %collective-permute-start.38 = (bf16[4,64,1024]{2,1,0:T(8,128)(2,1)S(1)}, bf16[4,64,1024]{2,1,0:T(8,128)(2,1)S(1)}, u32[]{:S(2)}, u32[]{:S(2)}) collective-permute-start(bf16[4,64,1024]{2,1,0:T(8,128)(2,1)S(1)} %copy-done.29), channel_id=1, source_target_pairs={{0,2},{1,3},{2,0},{3,1},{4,6},{5,7},{6,4},{7,5},{8,10},{9,11},{10,... | collective-permute-start | bytes 1572872 | tf_op jit(solution)/shard_map/ppermute | solution.py:533
  228.6 13.2 %collective-permute-start.37 = (bf16[4,64,1024]{2,1,0:T(8,128)(2,1)S(1)}, bf16[4,64,1024]{2,1,0:T(8,128)(2,1)S(1)}, u32[]{:S(2)}, u32[]{:S(2)}) collective-permute-start(bf16[4,64,1024]{2,1,0:T(8,128)(2,1)S(1)} %copy-done.29), channel_id=1, source_target_pairs={{0,1},{1,0},{2,3},{3,2},{4,5},{5,4},{6,7},{7,6},{8,9},{9,8},{10,11... | collective-permute-start | bytes 1572872 | tf_op jit(solution)/shard_map/ppermute | solution.py:532
  250.6 15.0 %collective-permute-start.24 = (bf16[2,4,64,1024]{3,2,1,0:T(8,128)(2,1)S(1)}, bf16[2,4,64,1024]{3,2,1,0:T(8,128)(2,1)}, u32[]{:S(2)}, u32[]{:S(2)}) collective-permute-start(bf16[2,4,64,1024]{3,2,1,0:T(8,128)(2,1)S(1)} %pad_maximum_fusion.7), channel_id=1, source_target_pairs={{0,1},{1,0},{2,3},{3,2},{4,5},{5,4},{6,7},{7,6},{8,9},{9,8},{10,11... | collective-permute-start | bytes 3145736 | tf_op jit(solution)/shard_map/ppermute | solution.py:544
  253.0 16.5 %collective-permute-start.27 = (bf16[2,4,64,1024]{3,2,1,0:T(8,128)(2,1)}, bf16[2,4,64,1024]{3,2,1,0:T(8,128)(2,1)}, u32[]{:S(2)}, u32[]{:S(2)}) collective-permute-start(bf16[2,4,64,1024]{3,2,1,0:T(8,128)(2,1)} %pad_maximum_fusion.8), channel_id=1, source_target_pairs={{0,1},{1,0},{2,3},{3,2},{4,5},{5,4},{6,7},{7,6},{8,9},{9,8},{10,11... | collective-permute-start | bytes 3145736 | tf_op jit(solution)/shard_map/ppermute | solution.py:544
  253.5 11.7 %collective-permute-start.42 = (f32[4,1024]{1,0:T(4,128)S(1)}, f32[4,1024]{1,0:T(4,128)S(1)}, u32[]{:S(2)}, u32[]{:S(2)}) collective-permute-start(f32[4,1024]{1,0:T(4,128)S(1)} %fusion.133), channel_id=1, source_target_pairs={{0,4},{4,0},{8,12},{12,8},{16,20},{20,16},{24,28},{28,24},{1,5},{5... | collective-permute-start | bytes 49160 | tf_op jit(solution)/shard_map/ppermute | solution.py:561
  258.7 65.1 %collective-permute-start.46 = (f32[1024]{0:T(1024)S(1)}, f32[1024]{0:T(1024)S(1)}, u32[]{:S(2)}, u32[]{:S(2)}) collective-permute-start(f32[1024]{0:T(1024)S(1)} %add.283), channel_id=1, source_target_pairs={{0,8},{4,12},{8,0},{12,4},{16,24},{20,28},{24,16},{28,20},{1,9},{5... | collective-permute-start | bytes 12296 | tf_op jit(solution)/shard_map/ppermute | solution.py:561
  265.2 61.6 %collective-permute-start.43 = (f32[4,1024]{1,0:T(4,128)S(1)}, f32[4,1024]{1,0:T(4,128)S(1)}, u32[]{:S(2)}, u32[]{:S(2)}) collective-permute-start(f32[4,1024]{1,0:T(4,128)S(1)} %add.280), channel_id=1, source_target_pairs={{0,8},{4,12},{8,0},{12,4},{16,24},{20,28},{24,16},{28,20},{1,9},{5... | collective-permute-start | bytes 49160 | tf_op jit(solution)/shard_map/ppermute | solution.py:561
  267.9 14.9 %collective-permute-start.25 = (bf16[4,64,1024]{2,1,0:T(8,128)(2,1)S(1)}, bf16[4,64,1024]{2,1,0:T(8,128)(2,1)S(1)}, u32[]{:S(2)}, u32[]{:S(2)}) collective-permute-start(bf16[4,64,1024]{2,1,0:T(8,128)(2,1)S(1)} %fusion.73), channel_id=1, source_target_pairs={{0,2},{1,3},{2,0},{3,1},{4,6},{5,7},{6,4},{7,5},{8,10},{9,11},{10,... | collective-permute-start | bytes 1572872 | tf_op jit(solution)/shard_map/ppermute | solution.py:546
  272.0 19.7 %collective-permute-start.28 = (bf16[4,64,1024]{2,1,0:T(8,128)(2,1)}, bf16[4,64,1024]{2,1,0:T(8,128)(2,1)S(1)}, u32[]{:S(2)}, u32[]{:S(2)}) collective-permute-start(bf16[4,64,1024]{2,1,0:T(8,128)(2,1)} %fusion.31), channel_id=1, source_target_pairs={{0,2},{1,3},{2,0},{3,1},{4,6},{5,7},{6,4},{7,5},{8,10},{9,11},{10,... | collective-permute-start | bytes 1572872 | tf_op jit(solution)/shard_map/ppermute | solution.py:546
  285.7 33.7 %all-to-all-start.3 = ((bf16[4,64,1024]{2,1,0:T(8,128)(2,1)}), bf16[4,64,1024]{2,1,0:T(8,128)(2,1)S(1)}, u32[]{:S(2)}, u32[]{:S(2)}) async-start(bf16[4,64,1024]{2,1,0:T(8,128)(2,1)} %fusion.77), calls=%async_computation.3 | async-start | bytes 1048576 | tf_op jit(solution)/shard_map/all_to_all | solution.py:528
  299.9 27.0 %collective-permute-start.31 = (f32[2,1024]{1,0:T(2,128)S(1)}, f32[2,1024]{1,0:T(2,128)S(1)}, u32[]{:S(2)}, u32[]{:S(2)}) collective-permute-start(f32[2,1024]{1,0:T(2,128)S(1)} %fusion.135), channel_id=1, source_target_pairs={{0,4},{4,0},{8,12},{12,8},{16,20},{20,16},{24,28},{28,24},{1,5},{5... | collective-permute-start | bytes 24584 | tf_op jit(solution)/shard_map/ppermute | solution.py:561
  319.4 36.1 %all-to-all-start.4 = ((bf16[4,64,1024]{2,1,0:T(8,128)(2,1)}), bf16[4,64,1024]{2,1,0:T(8,128)(2,1)S(1)}, u32[]{:S(2)}, u32[]{:S(2)}) async-start(bf16[4,64,1024]{2,1,0:T(8,128)(2,1)} %fusion.70), calls=%async_computation.4 | async-start | bytes 1048576 | tf_op jit(solution)/shard_map/all_to_all | solution.py:528
  323.8 25.3 %collective-permute-start.47 = (f32[1024]{0:T(1024)S(1)}, f32[1024]{0:T(1024)S(1)}, u32[]{:S(2)}, u32[]{:S(2)}) collective-permute-start(f32[1024]{0:T(1024)S(1)} %add.284), channel_id=1, source_target_pairs={{0,16},{4,20},{8,24},{12,28},{16,0},{20,4},{24,8},{28,12},{1,17},{... | collective-permute-start | bytes 12296 | tf_op jit(solution)/shard_map/ppermute | solution.py:561
  326.8 22.9 %collective-permute-start.44 = (f32[4,1024]{1,0:T(4,128)S(1)}, f32[4,1024]{1,0:T(4,128)S(1)}, u32[]{:S(2)}, u32[]{:S(2)}) collective-permute-start(f32[4,1024]{1,0:T(4,128)S(1)} %add.281), channel_id=1, source_target_pairs={{0,16},{4,20},{8,24},{12,28},{16,0},{20,4},{24,8},{28,12},{1,17},{... | collective-permute-start | bytes 49160 | tf_op jit(solution)/shard_map/ppermute | solution.py:561
  326.9 22.9 %collective-permute-start.32 = (f32[2,1024]{1,0:T(2,128)S(1)}, f32[2,1024]{1,0:T(2,128)S(1)}, u32[]{:S(2)}, u32[]{:S(2)}) collective-permute-start(f32[2,1024]{1,0:T(2,128)S(1)} %add.272), channel_id=1, source_target_pairs={{0,8},{4,12},{8,0},{12,4},{16,24},{20,28},{24,16},{28,20},{1,9},{5... | collective-permute-start | bytes 24584 | tf_op jit(solution)/shard_map/ppermute | solution.py:561
  329.0 20.7 %collective-permute-start.35 = (f32[4,128]{1,0:T(4,128)S(1)}, f32[4,128]{1,0:T(4,128)S(1)}, u32[]{:S(2)}, u32[]{:S(2)}) collective-permute-start(f32[4,128]{1,0:T(4,128)S(1)} %fusion.134), channel_id=1, source_target_pairs={{0,8},{4,12},{8,0},{12,4},{16,24},{20,28},{24,16},{28,20},{1,9},{5... | collective-permute-start | bytes 6152 | tf_op jit(solution)/shard_map/ppermute | solution.py:561
  (65 other events, 601.4 us)
Sparse Core Ops, SparseCore 0:
  245.0 242.9 all-reduce.2

commit v2 on v1

--- a/solution.py
+++ b/solution.py
@@ -324,12 +324,20 @@
 CTX_PLANES = [[0, 2, 4, 6], [1, 3, 5, 7]]
 
 
-def after(values, earlier):
-    return lax.optimization_barrier((values, earlier))[0]
+def tie(*values):
+    return lax.optimization_barrier(values)
 
 
 def contract(a, b, dims):
     return lax.dot_general(a, b, (dims, ((), ())), preferred_element_type=f32)
+
+
+def head_pair(packed, part):
+    low = part * HEAD_DIM
+    high = (part + 3) * HEAD_DIM
+    return jnp.concatenate(
+        [packed[:, low : low + HEAD_DIM], packed[:, high : high + HEAD_DIM]], axis=1
+    )
 
 
 def lane_half(rows, head):
@@ -346,10 +354,10 @@
     rows = pl.ds(pl.multiple_of(i * half, half), half)
     block = pl.ds(pl.multiple_of(i * BLK, BLK), BLK)
     packed = jnp.concatenate([mine_ref[rows, :], other_ref[rows, :]], axis=0)
-    queries = packed[:, :PAIR] * jnp.asarray(HEAD_DIM**-0.5, bf16)
-    key_ref[block, :PAIR] = packed[:, PAIR : 2 * PAIR]
+    queries = head_pair(packed, 0) * jnp.asarray(HEAD_DIM**-0.5, bf16)
+    key_ref[block, :PAIR] = head_pair(packed, 1)
     key_ref[block, PAIR:] = kdoc_ref[block, :]
-    value_ref[block, :] = packed[:, 2 * PAIR :]
+    value_ref[block, :] = head_pair(packed, 2)
     qdoc = qdoc_ref[block, :]
     query_heads = [
         jnp.concatenate([jnp.where(lane_half(BLK, h), queries, jnp.zeros_like(queries)), qdoc], axis=1)
@@ -398,7 +406,7 @@
 
 def attend_back_kernel(
     first_ref, mine_ref, other_ref, qdoc_ref, kdoc_ref, bias_ref, exact_ref, log_ref, dmine_ref, dother_ref,
-    out_mine_ref, out_other_ref, key_ref, value_ref, dkey_ref, dvalue_ref, dquery_ref,
+    out_mine_ref, out_other_ref, key_ref, value_ref, dkey_ref, dvalue_ref, dquery_ref, dquery_all_ref,
 ):
     i = pl.program_id(0)
     half = BLK // 2
@@ -406,10 +414,10 @@
     block = pl.ds(pl.multiple_of(i * BLK, BLK), BLK)
     packed = jnp.concatenate([mine_ref[rows, :], other_ref[rows, :]], axis=0)
     scale = HEAD_DIM**-0.5
-    queries = packed[:, :PAIR] * jnp.asarray(scale, bf16)
-    key_ref[block, :PAIR] = packed[:, PAIR : 2 * PAIR]
+    queries = head_pair(packed, 0) * jnp.asarray(scale, bf16)
+    key_ref[block, :PAIR] = head_pair(packed, 1)
     key_ref[block, PAIR:] = kdoc_ref[block, :]
-    value_ref[block, :] = packed[:, 2 * PAIR :]
+    value_ref[block, :] = head_pair(packed, 2)
     dkey_ref[block, :] = jnp.zeros((BLK, PAIR), f32)
     dvalue_ref[block, :] = jnp.zeros((BLK, PAIR), f32)
     dquery_ref[...] = jnp.zeros_like(dquery_ref)
@@ -451,9 +459,7 @@
 
     lax.fori_loop(first_ref[i], i, step, 0)
     visit(i, bias_ref[...])
-    dquery = jnp.transpose(dquery_ref[...] * scale).astype(bf16)
-    out_mine_ref[rows, :PAIR] = dquery[:half]
-    out_other_ref[rows, :PAIR] = dquery[half:]
+    dquery_all_ref[block, :] = jnp.transpose(dquery_ref[...] * scale)
 
     @pl.when(i == pl.num_programs(0) - 1)
     def _():
@@ -461,8 +467,10 @@
             for side, out in ((0, out_mine_ref), (1, out_other_ref)):
                 source = slice(b * BLK + side * half, b * BLK + (side + 1) * half)
                 target = slice(b * half, (b + 1) * half)
-                out[target, PAIR : 2 * PAIR] = dkey_ref[source, :].astype(bf16)
-                out[target, 2 * PAIR :] = dvalue_ref[source, :].astype(bf16)
+                grads = [ref[source, :] for ref in (dquery_all_ref, dkey_ref, dvalue_ref)]
+                out[target, :] = jnp.concatenate(
+                    [g[:, h * HEAD_DIM : (h + 1) * HEAD_DIM] for h in range(2) for g in grads], axis=1
+                ).astype(bf16)
 
 
 def whole(shape):
@@ -516,6 +524,7 @@
             pltpu.VMEM((length, PAIR), f32),
             pltpu.VMEM((length, PAIR), f32),
             pltpu.VMEM((PAIR, BLK), f32),
+            pltpu.VMEM((length, PAIR), f32),
         ],
         compiler_params=pltpu.CompilerParams(
             dimension_semantics=("arbitrary",), vmem_limit_bytes=48 << 20
@@ -539,12 +548,14 @@
     return jnp.stack(tp_gather(values), axis=1)
 
 
-def tp_scatter_rows(make_part):
+def tp_scatter_rows(make_part, meanwhile):
     away = jnp.stack([make_part(3), make_part(1)]).astype(bf16)
     came = lax.ppermute(away, "tp", TP_CORE)
     across = (make_part(2) + came[0].astype(f32)).astype(bf16)
+    across, filler = meanwhile(across)
     arrived = lax.ppermute(across, "tp", TP_ROW)
-    return make_part(0) + came[1].astype(f32) + arrived.astype(f32)
+    own, filler = tie(make_part(0) + came[1].astype(f32), filler)
+    return own + arrived.astype(f32), filler
 
 
 def tp_swap(pieces):
@@ -562,10 +573,14 @@
     return values
 
 
-def sum_all(values):
+def sum_tp(values):
     for perm in (TP_CORE, TP_ROW):
         values = values + lax.ppermute(values, "tp", perm)
-    return sum_ctx(values)
+    return values
+
+
+def sum_all(values):
+    return sum_ctx(sum_tp(values))
 
 
 def norm_stats(values):
@@ -618,30 +633,22 @@
     ctx_at = lax.axis_index("ctx")
     tp_at = lax.axis_index("tp")
     side = ctx_at % 2
+    plane = ctx_at // 2
     swapped = side == 1
     gain_first, shift_first = gain_one.astype(f32), shift_one.astype(f32)
     gain_second, shift_second = gain_two.astype(f32), shift_two.astype(f32)
 
-    inputs = planes_swap(tokens).astype(f32)
-
-    qkv_heads = query_key_value_weight.reshape(width, 4, 3, HEAD_DIM)
-    qkv_heads = order_pair(qkv_heads, swapped, 1)
-    qkv_rel = jnp.transpose(qkv_heads.reshape(width, 2, 2, 3, HEAD_DIM), (0, 1, 3, 2, 4)).reshape(
-        width, 2, 3 * PAIR
-    )
-    bias_pairs = order_pair(qv_bias.astype(f32), swapped, 0).reshape(2, 2, 2, HEAD_DIM)
-    bias_rel = jnp.concatenate(
-        [
-            bias_pairs[:, :, 0].reshape(2, PAIR),
-            jnp.zeros((2, PAIR), f32),
-            bias_pairs[:, :, 1].reshape(2, PAIR),
-        ],
-        axis=1,
-    )
+    inputs, doc_ids = tie(planes_swap(tokens), doc_ids)
+    inputs = inputs.astype(f32)
+
+    qkv_rel = jnp.transpose(query_key_value_weight, (1, 2, 0)).reshape(12 * HEAD_DIM, width)
+    qkv_rel = order_pair(qkv_rel, swapped, 0)
+    zero_key = jnp.zeros((4, HEAD_DIM), f32)
+    bias_all = qv_bias.astype(f32)
+    bias_rel = jnp.concatenate([bias_all[:, :HEAD_DIM], zero_key, bias_all[:, HEAD_DIM:]], axis=1)
+    bias_rel = order_pair(bias_rel.reshape(12 * HEAD_DIM), swapped, 0)
     out_rel = order_pair(attention_out_weight.reshape(4 * HEAD_DIM, width), swapped, 0)
-    out_full = jnp.concatenate(tp_gather(out_rel), axis=0)
-
-    ids = lax.all_to_all(doc_ids, "ctx", 0, 0, axis_index_groups=CTX_PLANES, tiled=False)
+    ids = planes_swap(doc_ids)
     ids = jnp.stack([ids, lax.ppermute(ids, "ctx", CTX_X)], axis=1).reshape(planes, 2, 2, 2, piece)
     ids = jnp.where(tp_at % 2 == 1, jnp.flip(ids, 3), ids)
     ids = jnp.where(tp_at // 2 == 1, jnp.flip(ids, 2), ids).reshape(planes, 2 * span)
@@ -661,15 +668,17 @@
     hat_one, rate_one = norm_stats(inputs)
     rows_one = tp_gather_rows((hat_one * gain_first + shift_first).astype(bf16)).reshape(group, width)
 
+    rows_one, out_rel, out_grad = tie(rows_one, out_rel, out_grad)
+
     def project(j):
-        return (
-            jnp.dot(rows_one, qkv_rel[:, j], preferred_element_type=f32) + bias_rel[j]
-        ).astype(bf16)
+        part = slice(j * 6 * HEAD_DIM, (j + 1) * 6 * HEAD_DIM)
+        return (contract(rows_one, qkv_rel[part], ((1,), (1,))) + bias_rel[part]).astype(bf16)
 
     qkv_other = lax.ppermute(project(1), "ctx", CTX_X)
     qkv_mine = project(0)
 
-    grad_rows = planes_swap(after(out_grad, qkv_mine))
+    grad_rows = planes_swap(out_grad)
+    out_full = tp_gather(out_rel)
     grad_gathered = tp_gather_rows(grad_rows).reshape(group, width)
     grad_rows = grad_rows.astype(f32)
     act_grad = contract(grad_gathered, contract_weight, ((1,), (1,)))
@@ -677,11 +686,14 @@
     mixed_mine, mixed_other, exact, log_total = attend(
         first_block, qkv_mine, qkv_other, qdoc, kdoc, bias
     )
-    mixed_heads = jnp.concatenate([mixed_mine, lax.ppermute(mixed_other, "ctx", CTX_X)], axis=1)
+    mixed_arrived = lax.ppermute(mixed_other, "ctx", CTX_X)
+    mixed_arrived, rows_one = tie(mixed_arrived, rows_one)
+    mixed_heads = jnp.concatenate([mixed_mine, mixed_arrived], axis=1)
+    rows_one_x = lax.ppermute(rows_one, "ctx", CTX_X)
     by_tp = mixed_heads.reshape(planes, 4, piece, 2 * PAIR)
-    mixed_rows = jnp.concatenate(tp_swap([by_tp[:, k] for k in range(4)]), axis=-1)
-    attn_branch = jnp.dot(
-        mixed_rows.reshape(here, width), out_full, preferred_element_type=f32
+    mixed_pieces = tp_swap([by_tp[:, k] for k in range(4)])
+    attn_branch = sum(
+        contract(mixed_pieces[k].reshape(here, 2 * PAIR), out_full[k], ((1,), (0,))) for k in range(4)
     ).reshape(planes, piece, width)
     residual_one = inputs + attn_branch + attention_out_bias.astype(f32)
 
@@ -692,60 +704,90 @@
     active = active.astype(bf16)
     dpre = pull_gelu(act_grad)[0].astype(bf16)
     dpre_parts = dpre.reshape(planes, 4, piece, -1)
-    dnormed_two = tp_scatter_rows(
+    def feed_forward_grads(sent):
+        sent, normed, hidden = tie(sent, rows_two, active)
+        fc_part = contract(normed, dpre, ((0,), (0,)))
+        proj_part = contract(hidden, grad_gathered, ((0,), (0,)))
+        return sent, (fc_part.astype(bf16), proj_part.astype(bf16))
+
+    dnormed_two, (fc_grad, proj_grad) = tp_scatter_rows(
         lambda k: contract(
             dpre_parts[:, k].reshape(here, -1), expand_weight, ((1,), (1,))
-        ).reshape(planes, piece, width)
-    )
-    fc_grad = contract(rows_two, dpre, ((0,), (0,)))
-    proj_grad = contract(active, grad_gathered, ((0,), (0,)))
+        ).reshape(planes, piece, width),
+        feed_forward_grads,
+    )
     fcb_grad = jnp.sum(dpre, axis=0, dtype=f32)
-    fc_grad, proj_grad = lax.psum((fc_grad.astype(bf16), proj_grad.astype(bf16)), "ctx")
+    proj_grad, fc_grad = lax.psum((proj_grad, fc_grad), "ctx")
 
     grad_res = grad_rows + norm_back(hat_two, rate_two, gain_second, dnormed_two)
     attn_grad = grad_res.astype(bf16)
-    dmixed = contract(attn_grad.reshape(here, width), out_full, ((1,), (1,))).astype(bf16)
-    dmixed = dmixed.reshape(planes, piece, 4, 2 * PAIR)
-    dmixed = jnp.stack(tp_swap([dmixed[:, :, k] for k in range(4)]), axis=1).reshape(group, 2 * PAIR)
+    attn_rows = attn_grad.reshape(here, width)
+    dmixed = tp_swap(
+        [
+            contract(attn_rows, out_full[k], ((1,), (1,))).astype(bf16).reshape(planes, piece, 2 * PAIR)
+            for k in range(4)
+        ]
+    )
+    dmixed = jnp.stack(dmixed, axis=1).reshape(group, 2 * PAIR)
+    dmixed, attn_grad, active = tie(dmixed, attn_grad, active)
     dmixed_other = lax.ppermute(dmixed[:, PAIR:], "ctx", CTX_X)
     grad_mine, grad_other = attend_back(
         first_block, qkv_mine, qkv_other, qdoc, kdoc, bias, exact, log_total, dmixed[:, :PAIR], dmixed_other
     )
+    grad_mine, grad_other, mixed_heads = tie(grad_mine, grad_other, mixed_heads)
     packed_grad = jnp.concatenate([grad_mine, lax.ppermute(grad_other, "ctx", CTX_X)], axis=1)
 
-    branch_in = after(active, dmixed_other).reshape(planes, 4, piece, -1)
-    feedforward_branch = tp_scatter_rows(
+    branch_in = active.reshape(planes, 4, piece, -1)
+    feedforward_branch, _ = tp_scatter_rows(
         lambda k: jnp.dot(
             branch_in[:, k].reshape(here, -1), contract_weight, preferred_element_type=f32
-        ).reshape(planes, piece, width)
-    )
-    layer_out = planes_swap(
-        (residual_one + feedforward_branch + contract_bias.astype(f32)).astype(bf16)
-    )
-
-    attn_grad_rows = tp_gather_rows(after(attn_grad, dmixed_other)).reshape(group, width)
-    outw_grad = contract(mixed_heads, attn_grad_rows, ((0,), (0,)))
-    outw_grad = order_pair(outw_grad.astype(bf16), swapped, 0)
-
-    qkv_flat = qkv_rel.reshape(width, 6 * PAIR)
+        ).reshape(planes, piece, width),
+        lambda sent: (sent, ()),
+    )
+    layer_low = (residual_one + feedforward_branch + contract_bias.astype(f32)).astype(bf16)
+
+    attn_grad_rows = tp_gather_rows(attn_grad).reshape(group, width)
+    outw = contract(mixed_heads, attn_grad_rows, ((0,), (0,)))
+    outw_came = lax.ppermute(outw[PAIR:].astype(bf16), "ctx", CTX_X)
+    qkv_part = contract(grad_mine, rows_one, ((0,), (0,))) + contract(grad_other, rows_one_x, ((0,), (0,)))
+    outw_part = outw[:PAIR] + outw_came.astype(f32)
+    parts = jnp.concatenate([qkv_part.astype(bf16), outw_part.astype(bf16)], axis=0)
+
     packed_parts = packed_grad.reshape(planes, 4, piece, 6 * PAIR)
-    dnormed_one = tp_scatter_rows(
-        lambda k: contract(
-            packed_parts[:, k].reshape(here, -1), qkv_flat, ((1,), (1,))
-        ).reshape(planes, piece, width)
-    )
-    qkv_grad = contract(rows_one, packed_grad, ((0,), (0,))).astype(bf16)
-    qkv_grad, outw_grad = lax.psum((qkv_grad_order(qkv_grad, swapped), outw_grad), "ctx")
-    bias_sums = jnp.sum(packed_grad, axis=0, dtype=f32)[None]
-    bias_sums = qkv_grad_order(bias_sums, swapped).reshape(4, 3, HEAD_DIM)
-    qvb_grad = jnp.concatenate([bias_sums[:, 0], bias_sums[:, 2]], axis=-1)
-
+    dnormed_one, parts = tp_scatter_rows(
+        lambda k: jnp.dot(
+            packed_parts[:, k].reshape(here, -1), qkv_rel, preferred_element_type=f32
+        ).reshape(planes, piece, width),
+        lambda sent: tie(sent, parts),
+    )
+    parts = parts.reshape(4, PAIR, width)
+    moves = [[(i, i ^ (2 * d)) for i in range(8)] for d in range(4)]
+    came = [
+        lax.ppermute(lax.dynamic_index_in_dim(parts, plane ^ d, 0, keepdims=False), "ctx", moves[d])
+        for d in range(1, 4)
+    ]
+    own = lax.dynamic_index_in_dim(parts, plane, 0, keepdims=False)
     grad_tokens = grad_res + norm_back(hat_one, rate_one, gain_first, dnormed_one)
-    grad_tokens = planes_swap(grad_tokens.astype(bf16)).astype(f32)
-
-    early = sum_all(
+    grad_tokens = planes_swap(grad_tokens.astype(bf16))
+    grad_tokens, layer_low, own, came = tie(grad_tokens, layer_low, own, came)
+    grad_tokens = grad_tokens.astype(f32)
+    total = (own.astype(f32) + sum(c.astype(f32) for c in came)).astype(bf16)
+    layer_out = planes_swap(layer_low)
+
+    wide = jnp.zeros((2, 4, PAIR, width), bf16)
+    for d in range(4):
+        near = total if d == 0 else lax.ppermute(total, "ctx", moves[d])
+        far = lax.ppermute(near, "ctx", CTX_X)
+        wide = lax.dynamic_update_slice(wide, near[None, None], (side, plane ^ d, 0, 0))
+        wide = lax.dynamic_update_slice(wide, far[None, None], (1 - side, plane ^ d, 0, 0))
+    qkv_grad = wide[:, :3].astype(f32).reshape(4, 3 * HEAD_DIM, width)
+    qkv_grad = jnp.transpose(qkv_grad, (2, 0, 1))
+    outw_grad = wide[:, 3].astype(f32)
+    small = sum_tp(
         jnp.stack(
             [
+                jnp.sum(dnormed_one * hat_one, axis=(0, 1)),
+                jnp.sum(dnormed_one, axis=(0, 1)),
                 jnp.sum(grad_res, axis=(0, 1)),
                 jnp.sum(dnormed_two * hat_two, axis=(0, 1)),
                 jnp.sum(dnormed_two, axis=(0, 1)),
@@ -753,33 +795,28 @@
             ]
         )
     )
-    late = sum_all(
-        jnp.stack([jnp.sum(dnormed_one * hat_one, axis=(0, 1)), jnp.sum(dnormed_one, axis=(0, 1))])
-    )
-    fcb_grad = sum_ctx(fcb_grad)
-    qvb_grad = sum_ctx(qvb_grad)
+    bias_sums = jnp.sum(packed_grad, axis=0, dtype=f32)[None]
+    bias_sums = order_pair(bias_sums, swapped, 1)
+    bias_sums = jnp.pad(bias_sums, ((0, 0), (0, width - 12 * HEAD_DIM)))
+    small = sum_ctx(jnp.concatenate([small, fcb_grad[None], bias_sums]))
+    bias_sums = small[7, : 12 * HEAD_DIM].reshape(4, 3, HEAD_DIM)
+    qvb_grad = jnp.concatenate([bias_sums[:, 0], bias_sums[:, 2]], axis=-1)
     return (
         layer_out,
         grad_tokens,
-        late[0],
-        late[1],
-        qkv_grad.astype(f32),
+        small[0],
+        small[1],
+        qkv_grad,
         qvb_grad,
-        outw_grad.astype(f32).reshape(4, HEAD_DIM, width),
-        early[0],
-        early[1],
-        early[2],
+        outw_grad.reshape(4, HEAD_DIM, width),
+        small[2],
+        small[3],
+        small[4],
         fc_grad.astype(f32),
-        fcb_grad,
+        small[6],
         proj_grad.astype(f32),
-        early[3],
-    )
-
-
-def qkv_grad_order(values, swapped):
-    rows = values.shape[0]
-    values = jnp.transpose(values.reshape(rows, 2, 3, 2, HEAD_DIM), (0, 1, 3, 2, 4))
-    return order_pair(values, swapped, 1).reshape(rows, 4, 3 * HEAD_DIM)
+        small[5],
+    )
 
 
 def solution(mesh):

time: 512 us -> 440 us (0.86)
  waiting for transfers between devices: 284 us -> 183 us
  other arithmetic: 37.6 us -> 47.4 us
  starting transfers between devices: 66.5 us -> 76 us
  Pallas kernels: 24.7 us -> 33.4 us
    psum x1, waiting for transfers between devices: 132 us -> 0.02 us  [shards(): proj_grad, fc_grad = lax.psum((proj_grad, fc_grad), 'ctx')]
    ppermute x5 -> x15, waiting for transfers between devices: 8.19 us -> 48.4 us  [the longest x3 28.1 us: shards(): lax.ppermute(lax.dynamic_index_in_dim(parts, plane ^ d, 0, keepdims=False...]
    ppermute x5, waiting for transfers between devices: 38.9 us -> 18 us  [tp_gather(): row = lax.ppermute(values, 'tp', TP_ROW)]
    ppermute x5 -> x15, starting transfers between devices: 3.79 us -> 23.1 us  [the longest x3 9.49 us: shards(): near = total if d == 0 else lax.ppermute(total, 'ctx', moves[d])]
    ppermute x1, waiting for transfers between devices: 6.95 us -> 24.3 us  [shards(): dmixed_other = lax.ppermute(dmixed[:, PAIR:], 'ctx', CTX_X)]
    all_to_all x4 -> x5, waiting for transfers between devices: 25 us -> 7.93 us  [planes_swap(): lax.all_to_all(values, 'ctx', 0, 0, axis_index_groups=CTX_PLANES, tiled=F...]
    ppermute x1, waiting for transfers between devices: 0.68 us -> 15.1 us  [shards(): lax.ppermute(grad_other, 'ctx', CTX_X)]
    dot_general x14 -> x20, matrix products: 29.4 us -> 41.9 us  [contract(): return lax.dot_general(a, b, (dims, ((), ())), preferred_element_type=f32)]
  transfers between devices with their start and end apart: 54 -> 55, of which waited for: 25 -> 25; matrix products, arithmetic and copies ran while one was open for 13% -> 23% of each run, Pallas kernels for 2% -> 8%
where the time goes in v2:
time: 440 us; the launch traced here: 432 us
  waiting for transfers between devices  183 us (42%)
  starting transfers between devices  76 us (17%)
  matrix products  51.2 us (12%)
  other arithmetic  47.4 us (11%)
  Pallas kernels  33.4 us (8%)
  local copies, waits for them, and re-layouts  25.7 us (6%)
  between operations  15.4 us (4%)
    dot_general x20, matrix products, contract(): return lax.dot_general(a, b, (dims, ((), ())), preferred_element_type=f32)  41.9 us
    ppermute x3, waiting for transfers between devices, shards(): lax.ppermute(lax.dynamic_index_in_dim(parts, plane ^ d, 0, keepdims=False...  28.1 us
    ppermute x3, waiting for transfers between devices, tp_scatter_rows(): arrived = lax.ppermute(across, 'tp', TP_ROW)  25 us
    ppermute x1, waiting for transfers between devices, shards(): dmixed_other = lax.ppermute(dmixed[:, PAIR:], 'ctx', CTX_X)  24.3 us
    all_to_all x5, starting transfers between devices, planes_swap(): lax.all_to_all(values, 'ctx', 0, 0, axis_index_groups=CTX_PLANES, tiled=F...  23 us
    pallas_call x1, Pallas kernels, attend_back(): pl.pallas_call(attend_back_kernel, grid=(length // BLK,), in_specs=[pl.Bl...  18.2 us
    ppermute x5, waiting for transfers between devices, tp_gather(): row = lax.ppermute(values, 'tp', TP_ROW)  18 us
    ppermute x3, waiting for transfers between devices, sum_ctx(): values = values + lax.ppermute(values, 'ctx', perm)  16.8 us
  transfers between devices with their start and end apart: 55, of which 25 were waited for; matrix products, arithmetic and copies ran while one was open for 23% of the time, Pallas kernels for 8%

profile of v2, /device:TPU:0, one launch (start us, length us, event | category | flops | bytes accessed | tf_op | source)
XLA Modules:
  0.0 431.6 jit_solution(569207907785587742)
XLA Ops:
  7.2 6.5 %all-to-all-start = ((bf16[4,64,1024]{2,1,0:T(8,128)(2,1)}), bf16[4,64,1024]{2,1,0:T(8,128)(2,1)}, u32[]{:S(2)}, u32[]{:S(2)}) async-start(bf16[4,64,1024]{2,1,0:T(8,128)(2,1)} %param.15), calls=%async_computation | async-start | bytes 1048576 | tf_op jit(solution)/shard_map/all_to_all | solution.py:537
  18.8 3.3 maximum_select_fusion
  22.2 6.0 %all-to-all-done = bf16[4,64,1024]{2,1,0:T(8,128)(2,1)} async-done(((bf16[4,64,1024]{2,1,0:T(8,128)(2,1)}), bf16[4,64,1024]{2,1,0:T(8,128)(2,1)}, u32[]{:S(2)}, u32[]{:S(2)}) %all-to-all-start) | async-done | bytes 524320 | tf_op jit(solution)/shard_map/all_to_all | solution.py:537
  31.4 3.2 all-to-all-start.2
  44.1 5.9 %collective-permute-done.1 = bf16[4,64,1024]{2,1,0:T(8,128)(2,1)} collective-permute-done((bf16[4,64,1024]{2,1,0:T(8,128)(2,1)}, bf16[4,64,1024]{2,1,0:T(8,128)(2,1)}, u32[]{:S(2)}, u32[]{:S(2)}) %collective-permute-start.1) | collective-permute-done | bytes 524320 | tf_op jit(solution)/shard_map/ppermute | solution.py:542
  55.5 4.8 %all-to-all-start.1 = ((bf16[4,64,1024]{2,1,0:T(8,128)(2,1)}), bf16[4,64,1024]{2,1,0:T(8,128)(2,1)}, u32[]{:S(2)}, u32[]{:S(2)}) async-start(bf16[4,64,1024]{2,1,0:T(8,128)(2,1)} %param.29), calls=%async_computation.1 | async-start | bytes 1048576 | tf_op jit(solution)/shard_map/all_to_all | solution.py:537
  60.3 3.2 add_convert_fusion.1
  68.5 14.3 %collective-permute-done.4.other_ref = bf16[1024,384]{1,0:T(8,128)(2,1)S(1)} collective-permute-done((bf16[1024,384]{1,0:T(8,128)(2,1)S(1)}, bf16[1024,384]{1,0:T(8,128)(2,1)S(1)}, u32[]{:S(2)}, u32[]{:S(2)}) %collective-permute-start.4) | collective-permute-done | bytes 786464 | tf_op jit(solution)/shard_map/ppermute | solution.py:677
  82.9 15.2 %attend.1 = (bf16[1024,128]{1,0:T(8,128)(2,1)S(1)}, bf16[1024,128]{1,0:T(8,128)(2,1)}, f32[128,2048]{1,0:T(8,128)S(1)}, f32[2,2048]{1,0:T(2,128)S(1)}) custom-call(s32[4]{0:T(128)S(1)} %convert_reduce_fusion.4.first_ref, bf16[1024,384]{1,0:T(8,128)(2,1)S(1)} %add_convert_fusion.2.mine_ref, bf16[1024,384]{1,0:T(8,128)(2,1)S(1)} %collective-permute-done.4.other_ref, ...), custom_call_target="tpu_custom_call" | custom-call | tf_op jit(solution)/shard_map/attend/pallas_call | solution.py:483
  102.7 3.8 collective-permute-done.5
  112.6 6.3 %collective-permute-done.8 = bf16[4,64,256]{2,1,0:T(8,128)(2,1)S(1)} collective-permute-done((bf16[4,64,256]{2,1,0:T(8,128)(2,1)S(1)}, bf16[4,64,256]{2,1,0:T(8,128)(2,1)S(1)}, u32[]{:S(2)}, u32[]{:S(2)}) %collective-permute-start.8) | collective-permute-done | bytes 131104 | tf_op jit(solution)/shard_map/ppermute | solution.py:565
  125.7 12.1 %collective-permute-done.16 = bf16[4,64,1024]{2,1,0:T(8,128)(2,1)S(1)} collective-permute-done((bf16[4,64,1024]{2,1,0:T(8,128)(2,1)S(1)}, bf16[4,64,1024]{2,1,0:T(8,128)(2,1)S(1)}, u32[]{:S(2)}, u32[]{:S(2)}) %collective-permute-start.16) | collective-permute-done | bytes 524320 | tf_op jit(solution)/shard_map/ppermute | solution.py:542
  145.1 6.5 %convert_reduce_fusion = (f32[1024]{0:T(1024)S(1)}, bf16[1024,1024]{1,0:T(8,128)(2,1)S(1)}, bf16[1024,1024]{1,0:T(8,128)(2,1)}) fusion(f32[1024,1024]{1,0:T(8,128)S(1)} %fusion.123, f32[1024]{0:T(1024)S(1)} %convert_element_type.206, bf16[1024,1024]{1,0:T(8,128)(2,1)S(1)} %bitcast.348, bf16[1024,1024]{1,0:T(8,128)(2,1)S(1)} %copy-done), kind=kOutput, calls=%fused_computation.9 | convolution fusion | flops 2173697024 | bytes 12591104 | tf_op jit(solution)/shard_map/dot_general | solution.py:332
  157.3 3.4 fusion.93
  160.7 3.8 convolution_convert_fusion
  168.8 3.8 convolution_convert_fusion.1
  172.6 6.4 %collective-permute-done.19 = bf16[4,64,1024]{2,1,0:T(8,128)(2,1)} collective-permute-done((bf16[4,64,1024]{2,1,0:T(8,128)(2,1)}, bf16[4,64,1024]{2,1,0:T(8,128)(2,1)}, u32[]{:S(2)}, u32[]{:S(2)}) %collective-permute-start.19) | collective-permute-done | bytes 524320 | tf_op jit(solution)/shard_map/ppermute | solution.py:556
  199.1 24.3 %collective-permute-done.23.dother_ref = bf16[1024,128]{1,0:T(8,128)(2,1)S(1)} collective-permute-done((bf16[1024,128]{1,0:T(8,128)(2,1)S(1)}, bf16[1024,128]{1,0:T(8,128)(2,1)S(1)}, u32[]{:S(2)}, u32[]{:S(2)}) %collective-permute-start.23) | collective-permute-done | bytes 262176 | tf_op jit(solution)/shard_map/ppermute | solution.py:733
  223.4 18.2 %attend_back.1 = (bf16[1024,384]{1,0:T(8,128)(2,1)S(1)}, bf16[1024,384]{1,0:T(8,128)(2,1)S(1)}) custom-call(s32[4]{0:T(128)S(1)} %convert_reduce_fusion.4.first_ref, bf16[1024,384]{1,0:T(8,128)(2,1)S(1)} %copy-done.8, bf16[1024,384]{1,0:T(8,128)(2,1)S(1)} %copy-done.6, bf16[2048,128]{1,0:T(8,128)(2,1)S(1)} %copy-done.4, bf16[2048,128]{1,0:T(8,128)(2,1)S(1)} %copy-done.2, ...), custom_call_target="tpu_custom_call" | custom-call | tf_op jit(solution)/shard_map/attend_back/pallas_call | solution.py:515
  249.6 15.1 %collective-permute-done.24 = bf16[1024,384]{1,0:T(8,128)(2,1)S(1)} collective-permute-done((bf16[1024,384]{1,0:T(8,128)(2,1)S(1)}, bf16[1024,384]{1,0:T(8,128)(2,1)S(1)}, u32[]{:S(2)}, u32[]{:S(2)}) %collective-permute-start.24) | collective-permute-done | bytes 786464 | tf_op jit(solution)/shard_map/ppermute | solution.py:738
  275.3 18.6 %collective-permute-done.31 = bf16[4,64,1024]{2,1,0:T(8,128)(2,1)S(1)} collective-permute-done((bf16[4,64,1024]{2,1,0:T(8,128)(2,1)S(1)}, bf16[4,64,1024]{2,1,0:T(8,128)(2,1)S(1)}, u32[]{:S(2)}, u32[]{:S(2)}) %collective-permute-start.31) | collective-permute-done | bytes 524320 | tf_op jit(solution)/shard_map/ppermute | solution.py:556
  301.4 3.2 fusion.88
  304.6 5.0 %all-to-all-start.3 = ((bf16[4,64,1024]{2,1,0:T(8,128)(2,1)}), bf16[4,64,1024]{2,1,0:T(8,128)(2,1)}, u32[]{:S(2)}, u32[]{:S(2)}) async-start(bf16[4,64,1024]{2,1,0:T(8,128)(2,1)} %fusion.88), calls=%async_computation.3 | async-start | bytes 1048576 | tf_op jit(solution)/shard_map/all_to_all | solution.py:537
  314.2 14.3 %collective-permute-done.40 = f32[8,1024]{1,0:T(8,128)S(1)} collective-permute-done((f32[8,1024]{1,0:T(8,128)S(1)}, f32[8,1024]{1,0:T(8,128)S(1)}, u32[]{:S(2)}, u32[]{:S(2)}) %collective-permute-start.40) | collective-permute-done | bytes 32800 | tf_op jit(solution)/shard_map/ppermute | solution.py:572
  328.5 4.9 %collective-permute-start.41 = (f32[8,1024]{1,0:T(8,128)S(1)}, f32[8,1024]{1,0:T(8,128)S(1)}, u32[]{:S(2)}, u32[]{:S(2)}) collective-permute-start(f32[8,1024]{1,0:T(8,128)S(1)} %add.300), channel_id=1, source_target_pairs={{0,16},{4,20},{8,24},{12,28},{16,0},{20,4},{24,8},{28,12},{1,17},{... | collective-permute-start | bytes 98312 | tf_op jit(solution)/shard_map/ppermute | solution.py:572
  334.1 3.9 collective-permute-start.36
  340.5 13.3 %collective-permute-done.34 = bf16[128,1024]{1,0:T(8,128)(2,1)S(1)} collective-permute-done((bf16[128,1024]{1,0:T(8,128)(2,1)S(1)}, bf16[128,1024]{1,0:T(8,128)(2,1)S(1)}, u32[]{:S(2)}, u32[]{:S(2)}) %collective-permute-start.34) | collective-permute-done | bytes 262176 | tf_op jit(solution)/shard_map/ppermute | solution.py:766
  353.8 14.9 %collective-permute-done.35 = bf16[128,1024]{1,0:T(8,128)(2,1)} collective-permute-done((bf16[128,1024]{1,0:T(8,128)(2,1)S(1)}, bf16[128,1024]{1,0:T(8,128)(2,1)}, u32[]{:S(2)}, u32[]{:S(2)}) %collective-permute-start.35) | collective-permute-done | bytes 262176 | tf_op jit(solution)/shard_map/ppermute | solution.py:766
  373.7 7.1 %collective-permute-start.43 = (bf16[128,1024]{1,0:T(8,128)(2,1)}, bf16[128,1024]{1,0:T(8,128)(2,1)}, u32[]{:S(2)}, u32[]{:S(2)}) collective-permute-start(bf16[128,1024]{1,0:T(8,128)(2,1)} %get-tuple-element.97), channel_id=1, source_target_pairs={{0,8},{4,12},{8,0},{12,4},{16,24},{20,28},{24,16},{28,20},{1,9},{5... | collective-permute-start | bytes 786440 | tf_op jit(solution)/shard_map/ppermute | solution.py:779
  386.5 3.5 all-to-all-start.4
  390.1 4.2 convert_element_type.250
  397.3 10.7 %collective-permute-done.45 = bf16[128,1024]{1,0:T(8,128)(2,1)S(1)} collective-permute-done((bf16[128,1024]{1,0:T(8,128)(2,1)}, bf16[128,1024]{1,0:T(8,128)(2,1)S(1)}, u32[]{:S(2)}, u32[]{:S(2)}) %collective-permute-start.45) | collective-permute-done | bytes 262176 | tf_op jit(solution)/shard_map/ppermute | solution.py:779
  (313 shorter events, 146.9 us)
Async XLA Ops:
  7.2 21.1 %all-to-all-start = ((bf16[4,64,1024]{2,1,0:T(8,128)(2,1)}), bf16[4,64,1024]{2,1,0:T(8,128)(2,1)}, u32[]{:S(2)}, u32[]{:S(2)}) async-start(bf16[4,64,1024]{2,1,0:T(8,128)(2,1)} %param.15), calls=%async_computation | async-start | bytes 1048576 | tf_op jit(solution)/shard_map/all_to_all | solution.py:537
  36.8 13.2 %collective-permute-start.1 = (bf16[4,64,1024]{2,1,0:T(8,128)(2,1)}, bf16[4,64,1024]{2,1,0:T(8,128)(2,1)}, u32[]{:S(2)}, u32[]{:S(2)}) collective-permute-start(bf16[4,64,1024]{2,1,0:T(8,128)(2,1)} %fusion.83), channel_id=1, source_target_pairs={{0,2},{1,3},{2,0},{3,1},{4,6},{5,7},{6,4},{7,5},{8,10},{9,11},{10,... | collective-permute-start | bytes 1572872 | tf_op jit(solution)/shard_map/ppermute | solution.py:542
  38.3 13.2 %collective-permute-start = (bf16[4,64,1024]{2,1,0:T(8,128)(2,1)}, bf16[4,64,1024]{2,1,0:T(8,128)(2,1)}, u32[]{:S(2)}, u32[]{:S(2)}) collective-permute-start(bf16[4,64,1024]{2,1,0:T(8,128)(2,1)} %fusion.83), channel_id=1, source_target_pairs={{0,1},{1,0},{2,3},{3,2},{4,5},{5,4},{6,7},{7,6},{8,9},{9,8},{10,11... | collective-permute-start | bytes 1572872 | tf_op jit(solution)/shard_map/ppermute | solution.py:541
  55.5 45.6 %all-to-all-start.1 = ((bf16[4,64,1024]{2,1,0:T(8,128)(2,1)}), bf16[4,64,1024]{2,1,0:T(8,128)(2,1)}, u32[]{:S(2)}, u32[]{:S(2)}) async-start(bf16[4,64,1024]{2,1,0:T(8,128)(2,1)} %param.29), calls=%async_computation.1 | async-start | bytes 1048576 | tf_op jit(solution)/shard_map/all_to_all | solution.py:537
  60.3 329.8 %all-reduce.4.cloned.1.call-start = ((), (), s32[]{:S(2)}) async-start(), calls=%async_computation.5 | async-start | bytes 8388608 | tf_op jit(solution)/shard_map/psum | solution.py:720
  63.5 19.4 %collective-permute-start.4 = (bf16[1024,384]{1,0:T(8,128)(2,1)S(1)}, bf16[1024,384]{1,0:T(8,128)(2,1)S(1)}, u32[]{:S(2)}, u32[]{:S(2)}) collective-permute-start(bf16[1024,384]{1,0:T(8,128)(2,1)S(1)} %add_convert_fusion.1), channel_id=1, source_target_pairs={{0,4},{4,0},{8,12},{12,8},{16,20},{20,16},{24,28},{28,24},{1,5},{5... | collective-permute-start | bytes 2359304 | tf_op jit(solution)/shard_map/ppermute | solution.py:677
  65.4 35.2 %collective-permute-start.9 = (bf16[256,1024]{1,0:T(8,128)(2,1)}, bf16[256,1024]{1,0:T(8,128)(2,1)}, u32[]{:S(2)}, u32[]{:S(2)}) collective-permute-start(bf16[256,1024]{1,0:T(8,128)(2,1)} %maximum_select_fusion.1), channel_id=1, source_target_pairs={{0,2},{1,3},{2,0},{3,1},{4,6},{5,7},{6,4},{7,5},{8,10},{9,11},{10,... | collective-permute-start | bytes 1572872 | tf_op jit(solution)/shard_map/ppermute | solution.py:542
  100.6 19.6 %collective-permute-start.11 = (bf16[256,1024]{1,0:T(8,128)(2,1)}, bf16[256,1024]{1,0:T(8,128)(2,1)}, u32[]{:S(2)}, u32[]{:S(2)}) collective-permute-start(bf16[256,1024]{1,0:T(8,128)(2,1)} %collective-permute-done.9), channel_id=1, source_target_pairs={{0,1},{1,0},{2,3},{3,2},{4,5},{5,4},{6,7},{7,6},{8,9},{9,8},{10,11... | collective-permute-start | bytes 1572872 | tf_op jit(solution)/shard_map/ppermute | solution.py:543
  101.1 24.1 %collective-permute-start.13 = (bf16[4,64,1024]{2,1,0:T(8,128)(2,1)}, bf16[4,64,1024]{2,1,0:T(8,128)(2,1)S(1)}, u32[]{:S(2)}, u32[]{:S(2)}) collective-permute-start(bf16[4,64,1024]{2,1,0:T(8,128)(2,1)} %all-to-all-done.1), channel_id=1, source_target_pairs={{0,2},{1,3},{2,0},{3,1},{4,6},{5,7},{6,4},{7,5},{8,10},{9,11},{10,... | collective-permute-start | bytes 1572872 | tf_op jit(solution)/shard_map/ppermute | solution.py:542
  123.5 14.3 %collective-permute-start.16 = (bf16[4,64,1024]{2,1,0:T(8,128)(2,1)S(1)}, bf16[4,64,1024]{2,1,0:T(8,128)(2,1)S(1)}, u32[]{:S(2)}, u32[]{:S(2)}) collective-permute-start(bf16[4,64,1024]{2,1,0:T(8,128)(2,1)S(1)} %add_convert_fusion.4), channel_id=1, source_target_pairs={{0,2},{1,3},{2,0},{3,1},{4,6},{5,7},{6,4},{7,5},{8,10},{9,11},{10,... | collective-permute-start | bytes 1572872 | tf_op jit(solution)/shard_map/ppermute | solution.py:542
  125.6 14.0 %collective-permute-start.15 = (bf16[4,64,1024]{2,1,0:T(8,128)(2,1)S(1)}, bf16[4,64,1024]{2,1,0:T(8,128)(2,1)S(1)}, u32[]{:S(2)}, u32[]{:S(2)}) collective-permute-start(bf16[4,64,1024]{2,1,0:T(8,128)(2,1)S(1)} %add_convert_fusion.4), channel_id=1, source_target_pairs={{0,1},{1,0},{2,3},{3,2},{4,5},{5,4},{6,7},{7,6},{8,9},{9,8},{10,11... | collective-permute-start | bytes 1572872 | tf_op jit(solution)/shard_map/ppermute | solution.py:541
  154.7 87.4 %collective-permute-start.26 = (bf16[1024,1024]{1,0:T(8,128)(2,1)}, bf16[1024,1024]{1,0:T(8,128)(2,1)}, u32[]{:S(2)}, u32[]{:S(2)}) collective-permute-start(bf16[1024,1024]{1,0:T(8,128)(2,1)} %bitcast.334), channel_id=1, source_target_pairs={{0,4},{4,0},{8,12},{12,8},{16,20},{20,16},{24,28},{28,24},{1,5},{5... | collective-permute-start | bytes 6291464 | tf_op jit(solution)/shard_map/ppermute | solution.py:692
  164.5 14.5 %collective-permute-start.19 = (bf16[4,64,1024]{2,1,0:T(8,128)(2,1)}, bf16[4,64,1024]{2,1,0:T(8,128)(2,1)}, u32[]{:S(2)}, u32[]{:S(2)}) collective-permute-start(bf16[4,64,1024]{2,1,0:T(8,128)(2,1)} %fusion.93), channel_id=1, source_target_pairs={{0,2},{1,3},{2,0},{3,1},{4,6},{5,7},{6,4},{7,5},{8,10},{9,11},{10,... | collective-permute-start | bytes 1572872 | tf_op jit(solution)/shard_map/ppermute | solution.py:556
  194.9 47.1 %collective-permute-start.28 = (bf16[4,64,1024]{2,1,0:T(8,128)(2,1)S(1)}, bf16[4,64,1024]{2,1,0:T(8,128)(2,1)S(1)}, u32[]{:S(2)}, u32[]{:S(2)}) collective-permute-start(bf16[4,64,1024]{2,1,0:T(8,128)(2,1)S(1)} %convert_element_type.217), channel_id=1, source_target_pairs={{0,2},{1,3},{2,0},{3,1},{4,6},{5,7},{6,4},{7,5},{8,10},{9,11},{10,... | collective-permute-start | bytes 1572872 | tf_op jit(solution)/shard_map/ppermute | solution.py:542
  196.3 49.7 %collective-permute-start.27 = (bf16[4,64,1024]{2,1,0:T(8,128)(2,1)S(1)}, bf16[4,64,1024]{2,1,0:T(8,128)(2,1)S(1)}, u32[]{:S(2)}, u32[]{:S(2)}) collective-permute-start(bf16[4,64,1024]{2,1,0:T(8,128)(2,1)S(1)} %convert_element_type.217), channel_id=1, source_target_pairs={{0,1},{1,0},{2,3},{3,2},{4,5},{5,4},{6,7},{7,6},{8,9},{9,8},{10,11... | collective-permute-start | bytes 1572872 | tf_op jit(solution)/shard_map/ppermute | solution.py:541
  196.7 26.6 %collective-permute-start.23 = (bf16[1024,128]{1,0:T(8,128)(2,1)S(1)}, bf16[1024,128]{1,0:T(8,128)(2,1)S(1)}, u32[]{:S(2)}, u32[]{:S(2)}) collective-permute-start(bf16[1024,128]{1,0:T(8,128)(2,1)S(1)} %get-tuple-element.113), channel_id=1, source_target_pairs={{0,4},{4,0},{8,12},{12,8},{16,20},{20,16},{24,28},{28,24},{1,5},{5... | collective-permute-start | bytes 786440 | tf_op jit(solution)/shard_map/ppermute | solution.py:733
  199.0 67.3 %collective-permute-start.32 = (bf16[2,4,64,1024]{3,2,1,0:T(8,128)(2,1)S(1)}, bf16[2,4,64,1024]{3,2,1,0:T(8,128)(2,1)S(1)}, u32[]{:S(2)}, u32[]{:S(2)}) collective-permute-start(bf16[2,4,64,1024]{3,2,1,0:T(8,128)(2,1)S(1)} %pad_maximum_fusion.7), channel_id=1, source_target_pairs={{0,1},{1,0},{2,3},{3,2},{4,5},{5,4},{6,7},{7,6},{8,9},{9,8},{10,11... | collective-permute-start | bytes 3145736 | tf_op jit(solution)/shard_map/ppermute | solution.py:553
  241.6 23.1 %collective-permute-start.24 = (bf16[1024,384]{1,0:T(8,128)(2,1)S(1)}, bf16[1024,384]{1,0:T(8,128)(2,1)S(1)}, u32[]{:S(2)}, u32[]{:S(2)}) collective-permute-start(bf16[1024,384]{1,0:T(8,128)(2,1)S(1)} %get-tuple-element.67), channel_id=1, source_target_pairs={{0,4},{4,0},{8,12},{12,8},{16,20},{20,16},{24,28},{28,24},{1,5},{5... | collective-permute-start | bytes 2359304 | tf_op jit(solution)/shard_map/ppermute | solution.py:738
  248.1 21.7 %collective-permute-start.30 = (bf16[128,1024]{1,0:T(8,128)(2,1)S(1)}, bf16[128,1024]{1,0:T(8,128)(2,1)S(1)}, u32[]{:S(2)}, u32[]{:S(2)}) collective-permute-start(bf16[128,1024]{1,0:T(8,128)(2,1)S(1)} %slice.285), channel_id=1, source_target_pairs={{0,4},{4,0},{8,12},{12,8},{16,20},{20,16},{24,28},{28,24},{1,5},{5... | collective-permute-start | bytes 786440 | tf_op jit(solution)/shard_map/ppermute | solution.py:751
  268.1 43.7 %collective-permute-start.33 = (bf16[4,64,1024]{2,1,0:T(8,128)(2,1)}, bf16[4,64,1024]{2,1,0:T(8,128)(2,1)}, u32[]{:S(2)}, u32[]{:S(2)}) collective-permute-start(bf16[4,64,1024]{2,1,0:T(8,128)(2,1)} %fusion.92), channel_id=1, source_target_pairs={{0,2},{1,3},{2,0},{3,1},{4,6},{5,7},{6,4},{7,5},{8,10},{9,11},{10,... | collective-permute-start | bytes 1572872 | tf_op jit(solution)/shard_map/ppermute | solution.py:556
  271.5 22.4 %collective-permute-start.31 = (bf16[4,64,1024]{2,1,0:T(8,128)(2,1)S(1)}, bf16[4,64,1024]{2,1,0:T(8,128)(2,1)S(1)}, u32[]{:S(2)}, u32[]{:S(2)}) collective-permute-start(bf16[4,64,1024]{2,1,0:T(8,128)(2,1)S(1)} %fusion.37), channel_id=1, source_target_pairs={{0,2},{1,3},{2,0},{3,1},{4,6},{5,7},{6,4},{7,5},{8,10},{9,11},{10,... | collective-permute-start | bytes 1572872 | tf_op jit(solution)/shard_map/ppermute | solution.py:556
  304.6 64.1 %all-to-all-start.3 = ((bf16[4,64,1024]{2,1,0:T(8,128)(2,1)}), bf16[4,64,1024]{2,1,0:T(8,128)(2,1)}, u32[]{:S(2)}, u32[]{:S(2)}) async-start(bf16[4,64,1024]{2,1,0:T(8,128)(2,1)} %fusion.88), calls=%async_computation.3 | async-start | bytes 1048576 | tf_op jit(solution)/shard_map/all_to_all | solution.py:537
  309.7 18.8 %collective-permute-start.40 = (f32[8,1024]{1,0:T(8,128)S(1)}, f32[8,1024]{1,0:T(8,128)S(1)}, u32[]{:S(2)}, u32[]{:S(2)}) collective-permute-start(f32[8,1024]{1,0:T(8,128)S(1)} %fusion.158), channel_id=1, source_target_pairs={{0,8},{4,12},{8,0},{12,4},{16,24},{20,28},{24,16},{28,20},{1,9},{5... | collective-permute-start | bytes 98312 | tf_op jit(solution)/shard_map/ppermute | solution.py:572
  333.5 20.3 %collective-permute-start.34 = (bf16[128,1024]{1,0:T(8,128)(2,1)S(1)}, bf16[128,1024]{1,0:T(8,128)(2,1)S(1)}, u32[]{:S(2)}, u32[]{:S(2)}) collective-permute-start(bf16[128,1024]{1,0:T(8,128)(2,1)S(1)} %get-tuple-element.110), channel_id=1, source_target_pairs={{0,8},{4,12},{8,0},{12,4},{16,24},{20,28},{24,16},{28,20},{1,9},{5... | collective-permute-start | bytes 786440 | tf_op jit(solution)/shard_map/ppermute | solution.py:766
  333.6 35.1 %collective-permute-start.35 = (bf16[128,1024]{1,0:T(8,128)(2,1)S(1)}, bf16[128,1024]{1,0:T(8,128)(2,1)}, u32[]{:S(2)}, u32[]{:S(2)}) collective-permute-start(bf16[128,1024]{1,0:T(8,128)(2,1)S(1)} %get-tuple-element.109), channel_id=1, source_target_pairs={{0,16},{4,20},{8,24},{12,28},{16,0},{20,4},{24,8},{28,12},{1,17},{... | collective-permute-start | bytes 786440 | tf_op jit(solution)/shard_map/ppermute | solution.py:766
  334.1 34.6 %collective-permute-start.36 = (bf16[128,1024]{1,0:T(8,128)(2,1)S(1)}, bf16[128,1024]{1,0:T(8,128)(2,1)}, u32[]{:S(2)}, u32[]{:S(2)}) collective-permute-start(bf16[128,1024]{1,0:T(8,128)(2,1)S(1)} %get-tuple-element.108), channel_id=1, source_target_pairs={{0,24},{4,28},{8,16},{12,20},{16,8},{20,12},{24,0},{28,4},{1,25},{... | collective-permute-start | bytes 786440 | tf_op jit(solution)/shard_map/ppermute | solution.py:766
  372.3 37.8 %collective-permute-start.42 = (bf16[128,1024]{1,0:T(8,128)(2,1)}, bf16[128,1024]{1,0:T(8,128)(2,1)S(1)}, u32[]{:S(2)}, u32[]{:S(2)}) collective-permute-start(bf16[128,1024]{1,0:T(8,128)(2,1)} %get-tuple-element.97), channel_id=1, source_target_pairs={{0,4},{4,0},{8,12},{12,8},{16,20},{20,16},{24,28},{28,24},{1,5},{5... | collective-permute-start | bytes 786440 | tf_op jit(solution)/shard_map/ppermute | solution.py:780
  373.7 23.1 %collective-permute-start.43 = (bf16[128,1024]{1,0:T(8,128)(2,1)}, bf16[128,1024]{1,0:T(8,128)(2,1)}, u32[]{:S(2)}, u32[]{:S(2)}) collective-permute-start(bf16[128,1024]{1,0:T(8,128)(2,1)} %get-tuple-element.97), channel_id=1, source_target_pairs={{0,8},{4,12},{8,0},{12,4},{16,24},{20,28},{24,16},{28,20},{1,9},{5... | collective-permute-start | bytes 786440 | tf_op jit(solution)/shard_map/ppermute | solution.py:779
  380.8 27.2 %collective-permute-start.45 = (bf16[128,1024]{1,0:T(8,128)(2,1)}, bf16[128,1024]{1,0:T(8,128)(2,1)S(1)}, u32[]{:S(2)}, u32[]{:S(2)}) collective-permute-start(bf16[128,1024]{1,0:T(8,128)(2,1)} %get-tuple-element.97), channel_id=1, source_target_pairs={{0,16},{4,20},{8,24},{12,28},{16,0},{20,4},{24,8},{28,12},{1,17},{... | collective-permute-start | bytes 786440 | tf_op jit(solution)/shard_map/ppermute | solution.py:779
  380.8 27.8 %collective-permute-start.47 = (bf16[128,1024]{1,0:T(8,128)(2,1)}, bf16[128,1024]{1,0:T(8,128)(2,1)S(1)}, u32[]{:S(2)}, u32[]{:S(2)}) collective-permute-start(bf16[128,1024]{1,0:T(8,128)(2,1)} %get-tuple-element.97), channel_id=1, source_target_pairs={{0,24},{4,28},{8,16},{12,20},{16,8},{20,12},{24,0},{28,4},{1,25},{... | collective-permute-start | bytes 786440 | tf_op jit(solution)/shard_map/ppermute | solution.py:779
  386.5 37.2 %all-to-all-start.4 = ((bf16[4,64,1024]{2,1,0:T(8,128)(2,1)}), bf16[4,64,1024]{2,1,0:T(8,128)(2,1)S(1)}, u32[]{:S(2)}, u32[]{:S(2)}) async-start(bf16[4,64,1024]{2,1,0:T(8,128)(2,1)} %add_convert_fusion.3), calls=%async_computation.4 | async-start | bytes 1048576 | tf_op jit(solution)/shard_map/all_to_all | solution.py:537
  396.8 15.7 %collective-permute-start.44 = (bf16[128,1024]{1,0:T(8,128)(2,1)}, bf16[128,1024]{1,0:T(8,128)(2,1)S(1)}, u32[]{:S(2)}, u32[]{:S(2)}) collective-permute-start(bf16[128,1024]{1,0:T(8,128)(2,1)} %collective-permute-done.43), channel_id=1, source_target_pairs={{0,4},{4,0},{8,12},{12,8},{16,20},{20,16},{24,28},{28,24},{1,5},{5... | collective-permute-start | bytes 786440 | tf_op jit(solution)/shard_map/ppermute | solution.py:780
  (67 other events, 796.9 us)
Sparse Core Ops, SparseCore 0:
  172.7 199.0 all-reduce.3

commit v3 on v2

--- a/solution.py
+++ b/solution.py
@@ -351,14 +351,13 @@
 ):
     i = pl.program_id(0)
     half = BLK // 2
-    rows = pl.ds(pl.multiple_of(i * half, half), half)
     block = pl.ds(pl.multiple_of(i * BLK, BLK), BLK)
-    packed = jnp.concatenate([mine_ref[rows, :], other_ref[rows, :]], axis=0)
+    packed = jnp.concatenate([mine_ref[...], other_ref[...]], axis=0)
     queries = head_pair(packed, 0) * jnp.asarray(HEAD_DIM**-0.5, bf16)
     key_ref[block, :PAIR] = head_pair(packed, 1)
-    key_ref[block, PAIR:] = kdoc_ref[block, :]
+    key_ref[block, PAIR:] = kdoc_ref[...]
     value_ref[block, :] = head_pair(packed, 2)
-    qdoc = qdoc_ref[block, :]
+    qdoc = qdoc_ref[...]
     query_heads = [
         jnp.concatenate([jnp.where(lane_half(BLK, h), queries, jnp.zeros_like(queries)), qdoc], axis=1)
         for h in range(2)
@@ -374,7 +373,7 @@
         for h in range(2):
             scores = contract(key_block, query_heads[h], ((1,), (1,)))
             if bias is not None:
-                scores = scores + bias
+                scores = scores + bias.astype(f32)
             old = best_ref[h : h + 1, :]
             new = jnp.maximum(old, jnp.max(scores, axis=0, keepdims=True))
             weights = jnp.exp(scores - new)
@@ -396,12 +395,12 @@
     for h in range(2):
         part = slice(h * HEAD_DIM, (h + 1) * HEAD_DIM)
         acc_ref[part, :] = acc_ref[part, :] / total_ref[h : h + 1, :]
-        log_ref[h : h + 1, block] = best_ref[h : h + 1, :] + jnp.log(total_ref[h : h + 1, :])
+        log_ref[h : h + 1, :] = best_ref[h : h + 1, :] + jnp.log(total_ref[h : h + 1, :])
     mixed = acc_ref[...]
-    exact_ref[:, block] = mixed
+    exact_ref[...] = mixed
     low = jnp.transpose(mixed).astype(bf16)
-    out_mine_ref[rows, :] = low[:half]
-    out_other_ref[rows, :] = low[half:]
+    out_mine_ref[...] = low[:half]
+    out_other_ref[...] = low[half:]
 
 
 def attend_back_kernel(
@@ -410,27 +409,26 @@
 ):
     i = pl.program_id(0)
     half = BLK // 2
-    rows = pl.ds(pl.multiple_of(i * half, half), half)
     block = pl.ds(pl.multiple_of(i * BLK, BLK), BLK)
-    packed = jnp.concatenate([mine_ref[rows, :], other_ref[rows, :]], axis=0)
+    packed = jnp.concatenate([mine_ref[...], other_ref[...]], axis=0)
     scale = HEAD_DIM**-0.5
     queries = head_pair(packed, 0) * jnp.asarray(scale, bf16)
     key_ref[block, :PAIR] = head_pair(packed, 1)
-    key_ref[block, PAIR:] = kdoc_ref[block, :]
+    key_ref[block, PAIR:] = kdoc_ref[...]
     value_ref[block, :] = head_pair(packed, 2)
     dkey_ref[block, :] = jnp.zeros((BLK, PAIR), f32)
     dvalue_ref[block, :] = jnp.zeros((BLK, PAIR), f32)
     dquery_ref[...] = jnp.zeros_like(dquery_ref)
-    dmixed = jnp.concatenate([dmine_ref[rows, :], dother_ref[rows, :]], axis=0)
-    qdoc = qdoc_ref[block, :]
+    dmixed = jnp.concatenate([dmine_ref[...], dother_ref[...]], axis=0)
+    qdoc = qdoc_ref[...]
     masked = [jnp.where(lane_half(BLK, h), queries, jnp.zeros_like(queries)) for h in range(2)]
     dmasked = [jnp.where(lane_half(BLK, h), dmixed, jnp.zeros_like(dmixed)) for h in range(2)]
     query_heads = [jnp.concatenate([masked[h], qdoc], axis=1) for h in range(2)]
-    product = jnp.transpose(dmixed.astype(f32)) * exact_ref[:, block]
+    product = jnp.transpose(dmixed.astype(f32)) * exact_ref[...]
     deltas = [
         jnp.sum(product[h * HEAD_DIM : (h + 1) * HEAD_DIM, :], axis=0, keepdims=True) for h in range(2)
     ]
-    logs = [log_ref[h : h + 1, block] for h in range(2)]
+    logs = [log_ref[h : h + 1, :] for h in range(2)]
 
     def visit(j, bias):
         keys = pl.ds(pl.multiple_of(j * BLK, BLK), BLK)
@@ -441,7 +439,7 @@
         for h in range(2):
             scores = contract(key_block, query_heads[h], ((1,), (1,)))
             if bias is not None:
-                scores = scores + bias
+                scores = scores + bias.astype(f32)
             weights = jnp.exp(scores - logs[h])
             dweights = contract(value_block, dmasked[h], ((1,), (1,)))
             dscores = (weights * (dweights - deltas[h])).astype(bf16)
@@ -477,6 +475,14 @@
     return pl.BlockSpec(shape, lambda i: (0,) * len(shape))
 
 
+def down(rows, cols):
+    return pl.BlockSpec((rows, cols), lambda i: (i, 0))
+
+
+def along(rows, cols):
+    return pl.BlockSpec((rows, cols), lambda i: (0, i))
+
+
 def attend(first, mine, other, qdoc, kdoc, bias):
     length = qdoc.shape[0]
     half = length // 2
@@ -485,9 +491,10 @@
         grid=(length // BLK,),
         in_specs=[
             pl.BlockSpec(memory_space=pltpu.SMEM),
-            whole(mine.shape), whole(other.shape), whole(qdoc.shape), whole(kdoc.shape), whole(bias.shape),
+            down(BLK // 2, 3 * PAIR), down(BLK // 2, 3 * PAIR), down(BLK, PAIR), down(BLK, PAIR),
+            whole(bias.shape),
         ],
-        out_specs=[whole((half, PAIR)), whole((half, PAIR)), whole((PAIR, length)), whole((2, length))],
+        out_specs=[down(BLK // 2, PAIR), down(BLK // 2, PAIR), along(PAIR, BLK), along(2, BLK)],
         out_shape=[
             jax.ShapeDtypeStruct((half, PAIR), bf16),
             jax.ShapeDtypeStruct((half, PAIR), bf16),
@@ -515,7 +522,11 @@
     return pl.pallas_call(
         attend_back_kernel,
         grid=(length // BLK,),
-        in_specs=[pl.BlockSpec(memory_space=pltpu.SMEM)] + [whole(o.shape) for o in operands],
+        in_specs=[
+            pl.BlockSpec(memory_space=pltpu.SMEM),
+            down(BLK // 2, 3 * PAIR), down(BLK // 2, 3 * PAIR), down(BLK, PAIR), down(BLK, PAIR),
+            whole(bias.shape), along(PAIR, BLK), along(2, BLK), down(BLK // 2, PAIR), down(BLK // 2, PAIR),
+        ],
         out_specs=[whole((half, 3 * PAIR)), whole((half, 3 * PAIR))],
         out_shape=[jax.ShapeDtypeStruct((half, 3 * PAIR), bf16)] * 2,
         scratch_shapes=[
@@ -638,8 +649,7 @@
     gain_first, shift_first = gain_one.astype(f32), shift_one.astype(f32)
     gain_second, shift_second = gain_two.astype(f32), shift_two.astype(f32)
 
-    inputs, doc_ids = tie(planes_swap(tokens), doc_ids)
-    inputs = inputs.astype(f32)
+    inputs = planes_swap(tokens).astype(f32)
 
     qkv_rel = jnp.transpose(query_key_value_weight, (1, 2, 0)).reshape(12 * HEAD_DIM, width)
     qkv_rel = order_pair(qkv_rel, swapped, 0)
@@ -648,6 +658,19 @@
     bias_rel = jnp.concatenate([bias_all[:, :HEAD_DIM], zero_key, bias_all[:, HEAD_DIM:]], axis=1)
     bias_rel = order_pair(bias_rel.reshape(12 * HEAD_DIM), swapped, 0)
     out_rel = order_pair(attention_out_weight.reshape(4 * HEAD_DIM, width), swapped, 0)
+    hat_one, rate_one = norm_stats(inputs)
+    rows_one = tp_gather_rows((hat_one * gain_first + shift_first).astype(bf16)).reshape(group, width)
+
+    rows_one, out_rel = tie(rows_one, out_rel)
+
+    def project(j):
+        part = slice(j * 6 * HEAD_DIM, (j + 1) * 6 * HEAD_DIM)
+        return (contract(rows_one, qkv_rel[part], ((1,), (1,))) + bias_rel[part]).astype(bf16)
+
+    qkv_away, out_grad, doc_ids = tie(project(1), out_grad, doc_ids)
+    qkv_other = lax.ppermute(qkv_away, "ctx", CTX_X)
+    qkv_mine = project(0)
+
     ids = planes_swap(doc_ids)
     ids = jnp.stack([ids, lax.ppermute(ids, "ctx", CTX_X)], axis=1).reshape(planes, 2, 2, 2, piece)
     ids = jnp.where(tp_at % 2 == 1, jnp.flip(ids, 3), ids)
@@ -663,19 +686,7 @@
         + ((tp_at ^ jnp.arange(4, dtype=jnp.int32)) * piece)[None, :, None]
         + jnp.arange(piece, dtype=jnp.int32)[None, None, :]
     ).reshape(-1)
-    bias = jnp.where(place[:, None] <= place[None, :], 0.0, CAUSAL_FAR).astype(f32)
-
-    hat_one, rate_one = norm_stats(inputs)
-    rows_one = tp_gather_rows((hat_one * gain_first + shift_first).astype(bf16)).reshape(group, width)
-
-    rows_one, out_rel, out_grad = tie(rows_one, out_rel, out_grad)
-
-    def project(j):
-        part = slice(j * 6 * HEAD_DIM, (j + 1) * 6 * HEAD_DIM)
-        return (contract(rows_one, qkv_rel[part], ((1,), (1,))) + bias_rel[part]).astype(bf16)
-
-    qkv_other = lax.ppermute(project(1), "ctx", CTX_X)
-    qkv_mine = project(0)
+    bias = jnp.where(place[:, None] <= place[None, :], 0.0, CAUSAL_FAR).astype(bf16)
 
     grad_rows = planes_swap(out_grad)
     out_full = tp_gather(out_rel)
@@ -703,18 +714,15 @@
     active, pull_gelu = jax.vjp(gelu_tanh, pre_act)
     active = active.astype(bf16)
     dpre = pull_gelu(act_grad)[0].astype(bf16)
+    fc_grad = contract(rows_two, dpre, ((0,), (0,))).astype(bf16)
+    proj_grad = contract(active, grad_gathered, ((0,), (0,))).astype(bf16)
+    fc_grad, proj_grad, dpre = tie(fc_grad, proj_grad, dpre)
     dpre_parts = dpre.reshape(planes, 4, piece, -1)
-    def feed_forward_grads(sent):
-        sent, normed, hidden = tie(sent, rows_two, active)
-        fc_part = contract(normed, dpre, ((0,), (0,)))
-        proj_part = contract(hidden, grad_gathered, ((0,), (0,)))
-        return sent, (fc_part.astype(bf16), proj_part.astype(bf16))
-
-    dnormed_two, (fc_grad, proj_grad) = tp_scatter_rows(
+    dnormed_two, _ = tp_scatter_rows(
         lambda k: contract(
             dpre_parts[:, k].reshape(here, -1), expand_weight, ((1,), (1,))
         ).reshape(planes, piece, width),
-        feed_forward_grads,
+        lambda sent: (sent, ()),
     )
     fcb_grad = jnp.sum(dpre, axis=0, dtype=f32)
     proj_grad, fc_grad = lax.psum((proj_grad, fc_grad), "ctx")

time: 440 us -> 430 us (0.977)
  waiting for transfers between devices: 183 us -> 196 us
  other arithmetic: 47.4 us -> 35 us
  local copies, waits for them, and re-layouts: 25.7 us -> 17.6 us
  Pallas kernels: 33.4 us -> 25.5 us
  starting transfers between devices: 76 us -> 83.1 us
    ppermute x3, waiting for transfers between devices: 28.1 us -> 10.3 us  [shards(): lax.ppermute(lax.dynamic_index_in_dim(parts, plane ^ d, 0, keepdims=False...]
    all_to_all x5, starting transfers between devices: 23 us -> 32.8 us  [planes_swap(): lax.all_to_all(values, 'ctx', 0, 0, axis_index_groups=CTX_PLANES, tiled=F...]
    ppermute x1, waiting for transfers between devices: 24.3 us -> 30.7 us  [shards(): dmixed_other = lax.ppermute(dmixed[:, PAIR:], 'ctx', CTX_X)]
    ppermute x3, waiting for transfers between devices: 10.7 us -> 16.2 us  [shards(): near = total if d == 0 else lax.ppermute(total, 'ctx', moves[d])]
    all_to_all x5, waiting for transfers between devices: 7.93 us -> 13.3 us  [planes_swap(): lax.all_to_all(values, 'ctx', 0, 0, axis_index_groups=CTX_PLANES, tiled=F...]
    ppermute x5, waiting for transfers between devices: 18 us -> 23.1 us  [tp_gather(): row = lax.ppermute(values, 'tp', TP_ROW)]
    pallas_call x1, Pallas kernels: 18.2 us -> 13.8 us  [attend_back(): pl.pallas_call(attend_back_kernel, grid=(length // BLK,), in_specs=[pl.Bl...]
  transfers between devices with their start and end apart: 55 -> 55, of which waited for: 25 -> 24; matrix products, arithmetic and copies ran while one was open for 23% -> 17% of each run, Pallas kernels for 8% -> 6%
where the time goes in v3:
time: 430 us; the launch traced here: 424 us
  waiting for transfers between devices  196 us (46%)
  starting transfers between devices  83.1 us (19%)
  matrix products  51.5 us (12%)
  other arithmetic  35 us (8%)
  Pallas kernels  25.5 us (6%)
  local copies, waits for them, and re-layouts  17.6 us (4%)
  between operations  15.3 us (4%)
    dot_general x20, matrix products, contract(): return lax.dot_general(a, b, (dims, ((), ())), preferred_element_type=f32)  39 us
    all_to_all x5, starting transfers between devices, planes_swap(): lax.all_to_all(values, 'ctx', 0, 0, axis_index_groups=CTX_PLANES, tiled=F...  32.8 us
    ppermute x1, waiting for transfers between devices, shards(): dmixed_other = lax.ppermute(dmixed[:, PAIR:], 'ctx', CTX_X)  30.7 us
    ppermute x3, waiting for transfers between devices, tp_scatter_rows(): arrived = lax.ppermute(across, 'tp', TP_ROW)  28.4 us
    ppermute x5, waiting for transfers between devices, tp_gather(): row = lax.ppermute(values, 'tp', TP_ROW)  23.1 us
    ppermute x1, waiting for transfers between devices, shards(): lax.ppermute(grad_other, 'ctx', CTX_X)  18.1 us
    ppermute x3, waiting for transfers between devices, shards(): near = total if d == 0 else lax.ppermute(total, 'ctx', moves[d])  16.2 us
    ppermute x1, waiting for transfers between devices, shards(): qkv_other = lax.ppermute(qkv_away, 'ctx', CTX_X)  14.9 us
  transfers between devices with their start and end apart: 55, of which 24 were waited for; matrix products, arithmetic and copies ran while one was open for 17% of the time, Pallas kernels for 6%

profile of v3, /device:TPU:0, one launch (start us, length us, event | category | flops | bytes accessed | tf_op | source)
XLA Modules:
  0.0 424.4 jit_solution(11349365302761464854)
XLA Ops:
  7.2 6.5 %all-to-all-start = ((bf16[4,64,1024]{2,1,0:T(8,128)(2,1)}), bf16[4,64,1024]{2,1,0:T(8,128)(2,1)S(1)}, u32[]{:S(2)}, u32[]{:S(2)}) async-start(bf16[4,64,1024]{2,1,0:T(8,128)(2,1)} %param.15), calls=%async_computation | async-start | bytes 1048576 | tf_op jit(solution)/shard_map/all_to_all | solution.py:548
  20.3 7.9 %all-to-all-done = bf16[4,64,1024]{2,1,0:T(8,128)(2,1)S(1)} async-done(((bf16[4,64,1024]{2,1,0:T(8,128)(2,1)}), bf16[4,64,1024]{2,1,0:T(8,128)(2,1)S(1)}, u32[]{:S(2)}, u32[]{:S(2)}) %all-to-all-start) | async-done | bytes 524320 | tf_op jit(solution)/shard_map/all_to_all | solution.py:548
  30.6 11.3 %collective-permute-done.1 = bf16[4,64,1024]{2,1,0:T(8,128)(2,1)} collective-permute-done((bf16[4,64,1024]{2,1,0:T(8,128)(2,1)S(1)}, bf16[4,64,1024]{2,1,0:T(8,128)(2,1)}, u32[]{:S(2)}, u32[]{:S(2)}) %collective-permute-start.1) | collective-permute-done | bytes 524320 | tf_op jit(solution)/shard_map/ppermute | solution.py:553
  50.6 3.2 all-to-all-start.2
  54.0 5.4 %all-to-all-done.2 = s32[4,1,256]{2,1,0:T(1,128)S(1)} async-done(((s32[4,1,256]{2,1,0:T(1,128)}), s32[4,1,256]{2,1,0:T(1,128)S(1)}, u32[]{:S(2)}, u32[]{:S(2)}) %all-to-all-start.2) | async-done | bytes 4128 | tf_op jit(solution)/shard_map/all_to_all | solution.py:548
  59.3 4.1 all-to-all-start.1
  65.1 3.9 add_convert_fusion.1.mine_ref
  72.6 14.9 %collective-permute-done.4.other_ref = bf16[1024,384]{1,0:T(8,128)(2,1)} collective-permute-done((bf16[1024,384]{1,0:T(8,128)(2,1)}, bf16[1024,384]{1,0:T(8,128)(2,1)}, u32[]{:S(2)}, u32[]{:S(2)}) %collective-permute-start.4) | collective-permute-done | bytes 786464 | tf_op jit(solution)/shard_map/ppermute | solution.py:671
  88.6 11.7 %attend.1 = (bf16[1024,128]{1,0:T(8,128)(2,1)S(1)}, bf16[1024,128]{1,0:T(8,128)(2,1)}, f32[128,2048]{1,0:T(8,128)S(1)}, f32[2,2048]{1,0:T(2,128)S(1)}) custom-call(s32[4]{0:T(128)S(1)} %convert_reduce_fusion.4.first_ref, bf16[1024,384]{1,0:T(8,128)(2,1)S(1)} %copy-done.4, bf16[1024,384]{1,0:T(8,128)(2,1)} %collective-permute-done.4.other_ref, ...), custom_call_target="tpu_custom_call" | custom-call | tf_op jit(solution)/shard_map/attend/pallas_call | solution.py:489
  105.0 4.0 collective-permute-done.5
  115.1 6.1 %collective-permute-done.8 = bf16[4,64,256]{2,1,0:T(8,128)(2,1)S(1)} collective-permute-done((bf16[4,64,256]{2,1,0:T(8,128)(2,1)S(1)}, bf16[4,64,256]{2,1,0:T(8,128)(2,1)S(1)}, u32[]{:S(2)}, u32[]{:S(2)}) %collective-permute-start.8) | collective-permute-done | bytes 131104 | tf_op jit(solution)/shard_map/ppermute | solution.py:576
  127.2 11.8 %collective-permute-done.13 = bf16[4,64,1024]{2,1,0:T(8,128)(2,1)S(1)} collective-permute-done((bf16[4,64,1024]{2,1,0:T(8,128)(2,1)S(1)}, bf16[4,64,1024]{2,1,0:T(8,128)(2,1)S(1)}, u32[]{:S(2)}, u32[]{:S(2)}) %collective-permute-start.13) | collective-permute-done | bytes 524320 | tf_op jit(solution)/shard_map/ppermute | solution.py:553
  144.8 5.4 %multiply_convert_fusion = (bf16[1024,1024]{1,0:T(8,128)(2,1)S(1)}, bf16[1024,1024]{1,0:T(8,128)(2,1)S(1)}) fusion(f32[1024]{0:T(1024)S(1)} %convert_element_type.210, f32[1024,1024]{1,0:T(8,128)S(1)} %fusion.122, bf16[1024,1024]{1,0:T(8,128)(2,1)S(1)} %bitcast.354, bf16[1024,1024]{1,0:T(8,128)(2,1)S(1)} %copy-done), kind=kOutput, calls=%fused_computation.10 | convolution fusion | flops 2171600896 | bytes 12587008 | tf_op jit(solution)/shard_map/dot_general | solution.py:713
  150.2 3.8 convolution_convert_fusion
  154.0 3.7 convolution_convert_fusion.1
  171.3 10.4 %collective-permute-done.19 = bf16[4,64,1024]{2,1,0:T(8,128)(2,1)S(1)} collective-permute-done((bf16[4,64,1024]{2,1,0:T(8,128)(2,1)S(1)}, bf16[4,64,1024]{2,1,0:T(8,128)(2,1)S(1)}, u32[]{:S(2)}, u32[]{:S(2)}) %collective-permute-start.19) | collective-permute-done | bytes 524320 | tf_op jit(solution)/shard_map/ppermute | solution.py:567
  200.8 30.7 %collective-permute-done.23.dother_ref = bf16[1024,128]{1,0:T(8,128)(2,1)S(1)} collective-permute-done((bf16[1024,128]{1,0:T(8,128)(2,1)S(1)}, bf16[1024,128]{1,0:T(8,128)(2,1)S(1)}, u32[]{:S(2)}, u32[]{:S(2)}) %collective-permute-start.23) | collective-permute-done | bytes 262176 | tf_op jit(solution)/shard_map/ppermute | solution.py:741
  231.6 13.8 %attend_back.1 = (bf16[1024,384]{1,0:T(8,128)(2,1)S(1)}, bf16[1024,384]{1,0:T(8,128)(2,1)S(1)}) custom-call(s32[4]{0:T(128)S(1)} %convert_reduce_fusion.4.first_ref, bf16[1024,384]{1,0:T(8,128)(2,1)S(1)} %copy-done.5, bf16[1024,384]{1,0:T(8,128)(2,1)} %collective-permute-done.4.other_ref, bf16[2048,128]{1,0:T(8,128)(2,1)S(1)} %copy-done.3, ...), custom_call_target="tpu_custom_call" | custom-call | tf_op jit(solution)/shard_map/attend_back/pallas_call | solution.py:522
  251.0 18.1 %collective-permute-done.24 = bf16[1024,384]{1,0:T(8,128)(2,1)S(1)} collective-permute-done((bf16[1024,384]{1,0:T(8,128)(2,1)S(1)}, bf16[1024,384]{1,0:T(8,128)(2,1)S(1)}, u32[]{:S(2)}, u32[]{:S(2)}) %collective-permute-start.24) | collective-permute-done | bytes 786464 | tf_op jit(solution)/shard_map/ppermute | solution.py:746
  283.5 18.0 %collective-permute-done.31 = bf16[4,64,1024]{2,1,0:T(8,128)(2,1)S(1)} collective-permute-done((bf16[4,64,1024]{2,1,0:T(8,128)(2,1)S(1)}, bf16[4,64,1024]{2,1,0:T(8,128)(2,1)S(1)}, u32[]{:S(2)}, u32[]{:S(2)}) %collective-permute-start.31) | collective-permute-done | bytes 524320 | tf_op jit(solution)/shard_map/ppermute | solution.py:567
  307.6 2.7 fusion.88
  310.3 15.4 %all-to-all-start.3 = ((bf16[4,64,1024]{2,1,0:T(8,128)(2,1)}), bf16[4,64,1024]{2,1,0:T(8,128)(2,1)}, u32[]{:S(2)}, u32[]{:S(2)}) async-start(bf16[4,64,1024]{2,1,0:T(8,128)(2,1)} %fusion.88), calls=%async_computation.3 | async-start | bytes 1048576 | tf_op jit(solution)/shard_map/all_to_all | solution.py:548
  330.3 13.9 %collective-permute-done.40 = f32[8,1024]{1,0:T(8,128)S(1)} collective-permute-done((f32[8,1024]{1,0:T(8,128)S(1)}, f32[8,1024]{1,0:T(8,128)S(1)}, u32[]{:S(2)}, u32[]{:S(2)}) %collective-permute-start.40) | collective-permute-done | bytes 32800 | tf_op jit(solution)/shard_map/ppermute | solution.py:583
  344.3 4.6 %collective-permute-start.41 = (f32[8,1024]{1,0:T(8,128)S(1)}, f32[8,1024]{1,0:T(8,128)S(1)}, u32[]{:S(2)}, u32[]{:S(2)}) collective-permute-start(f32[8,1024]{1,0:T(8,128)S(1)} %add.300), channel_id=1, source_target_pairs={{0,16},{4,20},{8,24},{12,28},{16,0},{20,4},{24,8},{28,12},{1,17},{... | collective-permute-start | bytes 98312 | tf_op jit(solution)/shard_map/ppermute | solution.py:583
  349.8 3.6 collective-permute-start.36
  353.4 4.2 convert_element_type.254
  360.9 9.7 %collective-permute-done.35 = bf16[128,1024]{1,0:T(8,128)(2,1)} collective-permute-done((bf16[128,1024]{1,0:T(8,128)(2,1)S(1)}, bf16[128,1024]{1,0:T(8,128)(2,1)}, u32[]{:S(2)}, u32[]{:S(2)}) %collective-permute-start.35) | collective-permute-done | bytes 262176 | tf_op jit(solution)/shard_map/ppermute | solution.py:774
  374.0 3.9 collective-permute-start.43
  383.7 3.5 all-to-all-start.4
  387.8 16.1 %collective-permute-done.45 = bf16[128,1024]{1,0:T(8,128)(2,1)S(1)} collective-permute-done((bf16[128,1024]{1,0:T(8,128)(2,1)}, bf16[128,1024]{1,0:T(8,128)(2,1)S(1)}, u32[]{:S(2)}, u32[]{:S(2)}) %collective-permute-start.45) | collective-permute-done | bytes 262176 | tf_op jit(solution)/shard_map/ppermute | solution.py:787
  407.1 3.2 collective-permute-done.46
  410.4 2.7 collective-permute-done.48
  (302 shorter events, 130.6 us)
Async XLA Ops:
  7.2 21.0 %all-to-all-start = ((bf16[4,64,1024]{2,1,0:T(8,128)(2,1)}), bf16[4,64,1024]{2,1,0:T(8,128)(2,1)S(1)}, u32[]{:S(2)}, u32[]{:S(2)}) async-start(bf16[4,64,1024]{2,1,0:T(8,128)(2,1)} %param.15), calls=%async_computation | async-start | bytes 1048576 | tf_op jit(solution)/shard_map/all_to_all | solution.py:548
  28.9 13.1 %collective-permute-start.1 = (bf16[4,64,1024]{2,1,0:T(8,128)(2,1)S(1)}, bf16[4,64,1024]{2,1,0:T(8,128)(2,1)}, u32[]{:S(2)}, u32[]{:S(2)}) collective-permute-start(bf16[4,64,1024]{2,1,0:T(8,128)(2,1)S(1)} %fusion.83), channel_id=1, source_target_pairs={{0,2},{1,3},{2,0},{3,1},{4,6},{5,7},{6,4},{7,5},{8,10},{9,11},{10,... | collective-permute-start | bytes 1572872 | tf_op jit(solution)/shard_map/ppermute | solution.py:553
  59.3 44.0 %all-to-all-start.1 = ((bf16[4,64,1024]{2,1,0:T(8,128)(2,1)}), bf16[4,64,1024]{2,1,0:T(8,128)(2,1)}, u32[]{:S(2)}, u32[]{:S(2)}) async-start(bf16[4,64,1024]{2,1,0:T(8,128)(2,1)} %param.29), calls=%async_computation.1 | async-start | bytes 1048576 | tf_op jit(solution)/shard_map/all_to_all | solution.py:548
  63.5 289.9 %all-reduce.4.cloned.1.call-start = ((), (), s32[]{:S(2)}) async-start(), calls=%async_computation.5 | async-start | bytes 8388608 | tf_op jit(solution)/shard_map/psum | solution.py:728
  69.0 18.5 %collective-permute-start.4 = (bf16[1024,384]{1,0:T(8,128)(2,1)}, bf16[1024,384]{1,0:T(8,128)(2,1)}, u32[]{:S(2)}, u32[]{:S(2)}) collective-permute-start(bf16[1024,384]{1,0:T(8,128)(2,1)} %add_convert_fusion.2), channel_id=1, source_target_pairs={{0,4},{4,0},{8,12},{12,8},{16,20},{20,16},{24,28},{28,24},{1,5},{5... | collective-permute-start | bytes 2359304 | tf_op jit(solution)/shard_map/ppermute | solution.py:671
  69.6 33.3 %collective-permute-start.9 = (bf16[256,1024]{1,0:T(8,128)(2,1)}, bf16[256,1024]{1,0:T(8,128)(2,1)}, u32[]{:S(2)}, u32[]{:S(2)}) collective-permute-start(bf16[256,1024]{1,0:T(8,128)(2,1)} %maximum_select_fusion.1), channel_id=1, source_target_pairs={{0,2},{1,3},{2,0},{3,1},{4,6},{5,7},{6,4},{7,5},{8,10},{9,11},{10,... | collective-permute-start | bytes 1572872 | tf_op jit(solution)/shard_map/ppermute | solution.py:553
  102.9 19.7 %collective-permute-start.11 = (bf16[256,1024]{1,0:T(8,128)(2,1)}, bf16[256,1024]{1,0:T(8,128)(2,1)}, u32[]{:S(2)}, u32[]{:S(2)}) collective-permute-start(bf16[256,1024]{1,0:T(8,128)(2,1)} %collective-permute-done.9), channel_id=1, source_target_pairs={{0,1},{1,0},{2,3},{3,2},{4,5},{5,4},{6,7},{7,6},{8,9},{9,8},{10,11... | collective-permute-start | bytes 1572872 | tf_op jit(solution)/shard_map/ppermute | solution.py:554
  103.4 23.0 %collective-permute-start.16 = (bf16[4,64,1024]{2,1,0:T(8,128)(2,1)}, bf16[4,64,1024]{2,1,0:T(8,128)(2,1)S(1)}, u32[]{:S(2)}, u32[]{:S(2)}) collective-permute-start(bf16[4,64,1024]{2,1,0:T(8,128)(2,1)} %all-to-all-done.1), channel_id=1, source_target_pairs={{0,2},{1,3},{2,0},{3,1},{4,6},{5,7},{6,4},{7,5},{8,10},{9,11},{10,... | collective-permute-start | bytes 1572872 | tf_op jit(solution)/shard_map/ppermute | solution.py:553
  124.8 14.2 %collective-permute-start.13 = (bf16[4,64,1024]{2,1,0:T(8,128)(2,1)S(1)}, bf16[4,64,1024]{2,1,0:T(8,128)(2,1)S(1)}, u32[]{:S(2)}, u32[]{:S(2)}) collective-permute-start(bf16[4,64,1024]{2,1,0:T(8,128)(2,1)S(1)} %add_convert_fusion.4), channel_id=1, source_target_pairs={{0,2},{1,3},{2,0},{3,1},{4,6},{5,7},{6,4},{7,5},{8,10},{9,11},{10,... | collective-permute-start | bytes 1572872 | tf_op jit(solution)/shard_map/ppermute | solution.py:553
  126.3 12.7 %collective-permute-start.15 = (bf16[4,64,1024]{2,1,0:T(8,128)(2,1)}, bf16[4,64,1024]{2,1,0:T(8,128)(2,1)S(1)}, u32[]{:S(2)}, u32[]{:S(2)}) collective-permute-start(bf16[4,64,1024]{2,1,0:T(8,128)(2,1)} %all-to-all-done.1), channel_id=1, source_target_pairs={{0,1},{1,0},{2,3},{3,2},{4,5},{5,4},{6,7},{7,6},{8,9},{9,8},{10,11... | collective-permute-start | bytes 1572872 | tf_op jit(solution)/shard_map/ppermute | solution.py:552
  126.9 17.4 %collective-permute-start.12 = (bf16[4,64,1024]{2,1,0:T(8,128)(2,1)S(1)}, bf16[4,64,1024]{2,1,0:T(8,128)(2,1)S(1)}, u32[]{:S(2)}, u32[]{:S(2)}) collective-permute-start(bf16[4,64,1024]{2,1,0:T(8,128)(2,1)S(1)} %add_convert_fusion.4), channel_id=1, source_target_pairs={{0,1},{1,0},{2,3},{3,2},{4,5},{5,4},{6,7},{7,6},{8,9},{9,8},{10,11... | collective-permute-start | bytes 1572872 | tf_op jit(solution)/shard_map/ppermute | solution.py:552
  162.9 83.8 %collective-permute-start.26 = (bf16[1024,1024]{1,0:T(8,128)(2,1)}, bf16[1024,1024]{1,0:T(8,128)(2,1)}, u32[]{:S(2)}, u32[]{:S(2)}) collective-permute-start(bf16[1024,1024]{1,0:T(8,128)(2,1)} %bitcast.335), channel_id=1, source_target_pairs={{0,4},{4,0},{8,12},{12,8},{16,20},{20,16},{24,28},{28,24},{1,5},{5... | collective-permute-start | bytes 6291464 | tf_op jit(solution)/shard_map/ppermute | solution.py:703
  167.5 14.3 %collective-permute-start.19 = (bf16[4,64,1024]{2,1,0:T(8,128)(2,1)S(1)}, bf16[4,64,1024]{2,1,0:T(8,128)(2,1)S(1)}, u32[]{:S(2)}, u32[]{:S(2)}) collective-permute-start(bf16[4,64,1024]{2,1,0:T(8,128)(2,1)S(1)} %fusion.93), channel_id=1, source_target_pairs={{0,2},{1,3},{2,0},{3,1},{4,6},{5,7},{6,4},{7,5},{8,10},{9,11},{10,... | collective-permute-start | bytes 1572872 | tf_op jit(solution)/shard_map/ppermute | solution.py:567
  195.8 50.9 %collective-permute-start.28 = (bf16[4,64,1024]{2,1,0:T(8,128)(2,1)S(1)}, bf16[4,64,1024]{2,1,0:T(8,128)(2,1)S(1)}, u32[]{:S(2)}, u32[]{:S(2)}) collective-permute-start(bf16[4,64,1024]{2,1,0:T(8,128)(2,1)S(1)} %convert_element_type.221), channel_id=1, source_target_pairs={{0,2},{1,3},{2,0},{3,1},{4,6},{5,7},{6,4},{7,5},{8,10},{9,11},{10,... | collective-permute-start | bytes 1572872 | tf_op jit(solution)/shard_map/ppermute | solution.py:553
  197.2 53.3 %collective-permute-start.27 = (bf16[4,64,1024]{2,1,0:T(8,128)(2,1)S(1)}, bf16[4,64,1024]{2,1,0:T(8,128)(2,1)S(1)}, u32[]{:S(2)}, u32[]{:S(2)}) collective-permute-start(bf16[4,64,1024]{2,1,0:T(8,128)(2,1)S(1)} %convert_element_type.221), channel_id=1, source_target_pairs={{0,1},{1,0},{2,3},{3,2},{4,5},{5,4},{6,7},{7,6},{8,9},{9,8},{10,11... | collective-permute-start | bytes 1572872 | tf_op jit(solution)/shard_map/ppermute | solution.py:552
  197.6 34.0 %collective-permute-start.23 = (bf16[1024,128]{1,0:T(8,128)(2,1)S(1)}, bf16[1024,128]{1,0:T(8,128)(2,1)S(1)}, u32[]{:S(2)}, u32[]{:S(2)}) collective-permute-start(bf16[1024,128]{1,0:T(8,128)(2,1)S(1)} %get-tuple-element.106), channel_id=1, source_target_pairs={{0,4},{4,0},{8,12},{12,8},{16,20},{20,16},{24,28},{28,24},{1,5},{5... | collective-permute-start | bytes 786440 | tf_op jit(solution)/shard_map/ppermute | solution.py:741
  200.8 73.0 %collective-permute-start.32 = (bf16[2,4,64,1024]{3,2,1,0:T(8,128)(2,1)S(1)}, bf16[2,4,64,1024]{3,2,1,0:T(8,128)(2,1)S(1)}, u32[]{:S(2)}, u32[]{:S(2)}) collective-permute-start(bf16[2,4,64,1024]{3,2,1,0:T(8,128)(2,1)S(1)} %pad_maximum_fusion.7), channel_id=1, source_target_pairs={{0,1},{1,0},{2,3},{3,2},{4,5},{5,4},{6,7},{7,6},{8,9},{9,8},{10,11... | collective-permute-start | bytes 3145736 | tf_op jit(solution)/shard_map/ppermute | solution.py:564
  245.4 23.7 %collective-permute-start.24 = (bf16[1024,384]{1,0:T(8,128)(2,1)S(1)}, bf16[1024,384]{1,0:T(8,128)(2,1)S(1)}, u32[]{:S(2)}, u32[]{:S(2)}) collective-permute-start(bf16[1024,384]{1,0:T(8,128)(2,1)S(1)} %get-tuple-element.61), channel_id=1, source_target_pairs={{0,4},{4,0},{8,12},{12,8},{16,20},{20,16},{24,28},{28,24},{1,5},{5... | collective-permute-start | bytes 2359304 | tf_op jit(solution)/shard_map/ppermute | solution.py:746
  275.6 52.3 %collective-permute-start.33 = (bf16[4,64,1024]{2,1,0:T(8,128)(2,1)}, bf16[4,64,1024]{2,1,0:T(8,128)(2,1)}, u32[]{:S(2)}, u32[]{:S(2)}) collective-permute-start(bf16[4,64,1024]{2,1,0:T(8,128)(2,1)} %fusion.92), channel_id=1, source_target_pairs={{0,2},{1,3},{2,0},{3,1},{4,6},{5,7},{6,4},{7,5},{8,10},{9,11},{10,... | collective-permute-start | bytes 1572872 | tf_op jit(solution)/shard_map/ppermute | solution.py:567
  279.7 21.7 %collective-permute-start.31 = (bf16[4,64,1024]{2,1,0:T(8,128)(2,1)S(1)}, bf16[4,64,1024]{2,1,0:T(8,128)(2,1)S(1)}, u32[]{:S(2)}, u32[]{:S(2)}) collective-permute-start(bf16[4,64,1024]{2,1,0:T(8,128)(2,1)S(1)} %fusion.37), channel_id=1, source_target_pairs={{0,2},{1,3},{2,0},{3,1},{4,6},{5,7},{6,4},{7,5},{8,10},{9,11},{10,... | collective-permute-start | bytes 1572872 | tf_op jit(solution)/shard_map/ppermute | solution.py:567
  307.5 18.2 %collective-permute-start.39 = (f32[8,1024]{1,0:T(8,128)S(1)}, f32[8,1024]{1,0:T(8,128)S(1)}, u32[]{:S(2)}, u32[]{:S(2)}) collective-permute-start(f32[8,1024]{1,0:T(8,128)S(1)} %select_maximum_fusion), channel_id=1, source_target_pairs={{0,4},{4,0},{8,12},{12,8},{16,20},{20,16},{24,28},{28,24},{1,5},{5... | collective-permute-start | bytes 98312 | tf_op jit(solution)/shard_map/ppermute | solution.py:583
  310.3 60.3 %all-to-all-start.3 = ((bf16[4,64,1024]{2,1,0:T(8,128)(2,1)}), bf16[4,64,1024]{2,1,0:T(8,128)(2,1)}, u32[]{:S(2)}, u32[]{:S(2)}) async-start(bf16[4,64,1024]{2,1,0:T(8,128)(2,1)} %fusion.88), calls=%async_computation.3 | async-start | bytes 1048576 | tf_op jit(solution)/shard_map/all_to_all | solution.py:548
  325.8 18.5 %collective-permute-start.40 = (f32[8,1024]{1,0:T(8,128)S(1)}, f32[8,1024]{1,0:T(8,128)S(1)}, u32[]{:S(2)}, u32[]{:S(2)}) collective-permute-start(f32[8,1024]{1,0:T(8,128)S(1)} %fusion.157), channel_id=1, source_target_pairs={{0,8},{4,12},{8,0},{12,4},{16,24},{20,28},{24,16},{28,20},{1,9},{5... | collective-permute-start | bytes 98312 | tf_op jit(solution)/shard_map/ppermute | solution.py:583
  344.3 15.8 %collective-permute-start.41 = (f32[8,1024]{1,0:T(8,128)S(1)}, f32[8,1024]{1,0:T(8,128)S(1)}, u32[]{:S(2)}, u32[]{:S(2)}) collective-permute-start(f32[8,1024]{1,0:T(8,128)S(1)} %add.300), channel_id=1, source_target_pairs={{0,16},{4,20},{8,24},{12,28},{16,0},{20,4},{24,8},{28,12},{1,17},{... | collective-permute-start | bytes 98312 | tf_op jit(solution)/shard_map/ppermute | solution.py:583
  349.0 21.5 %collective-permute-start.35 = (bf16[128,1024]{1,0:T(8,128)(2,1)S(1)}, bf16[128,1024]{1,0:T(8,128)(2,1)}, u32[]{:S(2)}, u32[]{:S(2)}) collective-permute-start(bf16[128,1024]{1,0:T(8,128)(2,1)S(1)} %get-tuple-element.102), channel_id=1, source_target_pairs={{0,16},{4,20},{8,24},{12,28},{16,0},{20,4},{24,8},{28,12},{1,17},{... | collective-permute-start | bytes 786440 | tf_op jit(solution)/shard_map/ppermute | solution.py:774
  349.8 20.8 %collective-permute-start.36 = (bf16[128,1024]{1,0:T(8,128)(2,1)S(1)}, bf16[128,1024]{1,0:T(8,128)(2,1)}, u32[]{:S(2)}, u32[]{:S(2)}) collective-permute-start(bf16[128,1024]{1,0:T(8,128)(2,1)S(1)} %get-tuple-element.101), channel_id=1, source_target_pairs={{0,24},{4,28},{8,16},{12,20},{16,8},{20,12},{24,0},{28,4},{1,25},{... | collective-permute-start | bytes 786440 | tf_op jit(solution)/shard_map/ppermute | solution.py:774
  372.8 33.2 %collective-permute-start.42 = (bf16[128,1024]{1,0:T(8,128)(2,1)}, bf16[128,1024]{1,0:T(8,128)(2,1)S(1)}, u32[]{:S(2)}, u32[]{:S(2)}) collective-permute-start(bf16[128,1024]{1,0:T(8,128)(2,1)} %get-tuple-element.91), channel_id=1, source_target_pairs={{0,4},{4,0},{8,12},{12,8},{16,20},{20,16},{24,28},{28,24},{1,5},{5... | collective-permute-start | bytes 786440 | tf_op jit(solution)/shard_map/ppermute | solution.py:788
  374.0 13.2 %collective-permute-start.43 = (bf16[128,1024]{1,0:T(8,128)(2,1)}, bf16[128,1024]{1,0:T(8,128)(2,1)}, u32[]{:S(2)}, u32[]{:S(2)}) collective-permute-start(bf16[128,1024]{1,0:T(8,128)(2,1)} %get-tuple-element.91), channel_id=1, source_target_pairs={{0,8},{4,12},{8,0},{12,4},{16,24},{20,28},{24,16},{28,20},{1,9},{5... | collective-permute-start | bytes 786440 | tf_op jit(solution)/shard_map/ppermute | solution.py:787
  378.0 26.0 %collective-permute-start.45 = (bf16[128,1024]{1,0:T(8,128)(2,1)}, bf16[128,1024]{1,0:T(8,128)(2,1)S(1)}, u32[]{:S(2)}, u32[]{:S(2)}) collective-permute-start(bf16[128,1024]{1,0:T(8,128)(2,1)} %get-tuple-element.91), channel_id=1, source_target_pairs={{0,16},{4,20},{8,24},{12,28},{16,0},{20,4},{24,8},{28,12},{1,17},{... | collective-permute-start | bytes 786440 | tf_op jit(solution)/shard_map/ppermute | solution.py:787
  378.2 26.6 %collective-permute-start.47 = (bf16[128,1024]{1,0:T(8,128)(2,1)}, bf16[128,1024]{1,0:T(8,128)(2,1)S(1)}, u32[]{:S(2)}, u32[]{:S(2)}) collective-permute-start(bf16[128,1024]{1,0:T(8,128)(2,1)} %get-tuple-element.91), channel_id=1, source_target_pairs={{0,24},{4,28},{8,16},{12,20},{16,8},{20,12},{24,0},{28,4},{1,25},{... | collective-permute-start | bytes 786440 | tf_op jit(solution)/shard_map/ppermute | solution.py:787
  383.7 32.8 %all-to-all-start.4 = ((bf16[4,64,1024]{2,1,0:T(8,128)(2,1)}), bf16[4,64,1024]{2,1,0:T(8,128)(2,1)S(1)}, u32[]{:S(2)}, u32[]{:S(2)}) async-start(bf16[4,64,1024]{2,1,0:T(8,128)(2,1)} %add_convert_fusion.3), calls=%async_computation.4 | async-start | bytes 1048576 | tf_op jit(solution)/shard_map/all_to_all | solution.py:548
  387.2 19.8 %collective-permute-start.44 = (bf16[128,1024]{1,0:T(8,128)(2,1)}, bf16[128,1024]{1,0:T(8,128)(2,1)S(1)}, u32[]{:S(2)}, u32[]{:S(2)}) collective-permute-start(bf16[128,1024]{1,0:T(8,128)(2,1)} %collective-permute-done.43), channel_id=1, source_target_pairs={{0,4},{4,0},{8,12},{12,8},{16,20},{20,16},{24,28},{28,24},{1,5},{5... | collective-permute-start | bytes 786440 | tf_op jit(solution)/shard_map/ppermute | solution.py:788
  (61 other events, 720.3 us)
Sparse Core Ops, SparseCore 0:
  164.5 185.1 all-reduce.3

commit v4 on v3

--- a/solution.py
+++ b/solution.py
@@ -649,7 +649,12 @@
     gain_first, shift_first = gain_one.astype(f32), shift_one.astype(f32)
     gain_second, shift_second = gain_two.astype(f32), shift_two.astype(f32)
 
-    inputs = planes_swap(tokens).astype(f32)
+    ids = jnp.pad(doc_ids.astype(bf16), ((0, 0), (0, width - span)))
+    ids = jnp.broadcast_to(ids[:, None], (planes, 16, width))
+    arrived = planes_swap(jnp.concatenate([tokens, ids], axis=1))
+    inputs = arrived[:, :piece].astype(f32)
+    ids = arrived[:, piece, :span]
+    ids = jnp.stack([ids, lax.ppermute(ids, "ctx", CTX_X)], axis=1).astype(jnp.int32)
 
     qkv_rel = jnp.transpose(query_key_value_weight, (1, 2, 0)).reshape(12 * HEAD_DIM, width)
     qkv_rel = order_pair(qkv_rel, swapped, 0)
@@ -663,16 +668,15 @@
 
     rows_one, out_rel = tie(rows_one, out_rel)
 
-    def project(j):
+    def project(rows, j):
         part = slice(j * 6 * HEAD_DIM, (j + 1) * 6 * HEAD_DIM)
-        return (contract(rows_one, qkv_rel[part], ((1,), (1,))) + bias_rel[part]).astype(bf16)
-
-    qkv_away, out_grad, doc_ids = tie(project(1), out_grad, doc_ids)
+        return (contract(rows, qkv_rel[part], ((1,), (1,))) + bias_rel[part]).astype(bf16)
+
+    qkv_away, rows_one = tie(project(rows_one, 1), rows_one)
     qkv_other = lax.ppermute(qkv_away, "ctx", CTX_X)
-    qkv_mine = project(0)
-
-    ids = planes_swap(doc_ids)
-    ids = jnp.stack([ids, lax.ppermute(ids, "ctx", CTX_X)], axis=1).reshape(planes, 2, 2, 2, piece)
+    qkv_mine, out_grad = tie(project(rows_one, 0), out_grad)
+
+    ids = ids.reshape(planes, 2, 2, 2, piece)
     ids = jnp.where(tp_at % 2 == 1, jnp.flip(ids, 3), ids)
     ids = jnp.where(tp_at // 2 == 1, jnp.flip(ids, 2), ids).reshape(planes, 2 * span)
     low_id, high_id = jnp.min(ids, axis=1), jnp.max(ids, axis=1)

time: 430 us -> 429 us (level)
  waiting for transfers between devices: 196 us -> 181 us
  starting transfers between devices: 83.1 us -> 68.8 us
  local copies, waits for them, and re-layouts: 17.6 us -> 28.2 us
  other arithmetic: 35 us -> 44.2 us
  Pallas kernels: 25.5 us -> 33 us
    all_to_all x5 -> x4, starting transfers between devices: 32.8 us -> 18.4 us  [planes_swap(): lax.all_to_all(values, 'ctx', 0, 0, axis_index_groups=CTX_PLANES, tiled=F...]
    all_to_all x5 -> x4, waiting for transfers between devices: 13.3 us -> 7.56 us  [planes_swap(): lax.all_to_all(values, 'ctx', 0, 0, axis_index_groups=CTX_PLANES, tiled=F...]
    ppermute x3, waiting for transfers between devices: 13.9 us -> 8.67 us  [sum_ctx(): values = values + lax.ppermute(values, 'ctx', perm)]
    ppermute x3, waiting for transfers between devices: 28.4 us -> 23.3 us  [tp_scatter_rows(): arrived = lax.ppermute(across, 'tp', TP_ROW)]
    ppermute x5, waiting for transfers between devices: 23.1 us -> 18.7 us  [tp_gather(): row = lax.ppermute(values, 'tp', TP_ROW)]
    unnamed x80 -> x92, local copies, waits for them, and re-layouts: 8.05 us -> 9.02 us
  transfers between devices with their start and end apart: 55 -> 54, of which waited for: 24 -> 24; matrix products, arithmetic and copies ran while one was open for 17% -> 20% of each run, Pallas kernels for 6% -> 8%
where the time goes in v4:
time: 429 us; the launch traced here: 422 us
  waiting for transfers between devices  181 us (42%)
  starting transfers between devices  68.8 us (16%)
  matrix products  52.2 us (12%)
  other arithmetic  44.2 us (10%)
  Pallas kernels  33 us (8%)
  local copies, waits for them, and re-layouts  28.2 us (7%)
  between operations  15.2 us (4%)
    dot_general x20, matrix products, contract(): return lax.dot_general(a, b, (dims, ((), ())), preferred_element_type=f32)  37.7 us
    ppermute x1, waiting for transfers between devices, shards(): dmixed_other = lax.ppermute(dmixed[:, PAIR:], 'ctx', CTX_X)  33.5 us
    ppermute x3, waiting for transfers between devices, tp_scatter_rows(): arrived = lax.ppermute(across, 'tp', TP_ROW)  23.3 us
    ppermute x5, waiting for transfers between devices, tp_gather(): row = lax.ppermute(values, 'tp', TP_ROW)  18.7 us
    ppermute x1, waiting for transfers between devices, shards(): lax.ppermute(grad_other, 'ctx', CTX_X)  18.6 us
    all_to_all x4, starting transfers between devices, planes_swap(): lax.all_to_all(values, 'ctx', 0, 0, axis_index_groups=CTX_PLANES, tiled=F...  18.4 us
    pallas_call x1, Pallas kernels, attend_back(): pl.pallas_call(attend_back_kernel, grid=(length // BLK,), in_specs=[pl.Bl...  18.1 us
    ppermute x3, waiting for transfers between devices, shards(): near = total if d == 0 else lax.ppermute(total, 'ctx', moves[d])  16.7 us
  transfers between devices with their start and end apart: 54, of which 24 were waited for; matrix products, arithmetic and copies ran while one was open for 20% of the time, Pallas kernels for 8%

profile of v4, /device:TPU:0, one launch (start us, length us, event | category | flops | bytes accessed | tf_op | source)
XLA Modules:
  0.0 422.5 jit_solution(5599565251992017115)
XLA Ops:
  10.0 6.4 %all-to-all-start = ((bf16[4,80,1024]{2,1,0:T(8,128)(2,1)}), bf16[4,80,1024]{2,1,0:T(8,128)(2,1)S(1)}, u32[]{:S(2)}, u32[]{:S(2)}) async-start(bf16[4,80,1024]{2,1,0:T(8,128)(2,1)} %pad_maximum_fusion.8), calls=%async_computation | async-start | bytes 1310720 | tf_op jit(solution)/shard_map/all_to_all | solution.py:548
  16.4 2.6 fusion.112
  19.7 4.0 maximum_select_fusion
  26.2 7.5 %all-to-all-done = bf16[4,80,1024]{2,1,0:T(8,128)(2,1)S(1)} async-done(((bf16[4,80,1024]{2,1,0:T(8,128)(2,1)}), bf16[4,80,1024]{2,1,0:T(8,128)(2,1)S(1)}, u32[]{:S(2)}, u32[]{:S(2)}) %all-to-all-start) | async-done | bytes 655392 | tf_op jit(solution)/shard_map/all_to_all | solution.py:548
  41.5 7.0 %collective-permute-done.1 = bf16[4,64,1024]{2,1,0:T(8,128)(2,1)} collective-permute-done((bf16[4,64,1024]{2,1,0:T(8,128)(2,1)}, bf16[4,64,1024]{2,1,0:T(8,128)(2,1)}, u32[]{:S(2)}, u32[]{:S(2)}) %collective-permute-start.1) | collective-permute-done | bytes 524320 | tf_op jit(solution)/shard_map/ppermute | solution.py:553
  58.8 4.1 all-to-all-start.1
  67.2 15.9 %collective-permute-done.4.other_ref = bf16[1024,384]{1,0:T(8,128)(2,1)S(1)} collective-permute-done((bf16[1024,384]{1,0:T(8,128)(2,1)}, bf16[1024,384]{1,0:T(8,128)(2,1)S(1)}, u32[]{:S(2)}, u32[]{:S(2)}) %collective-permute-start.4) | collective-permute-done | bytes 786464 | tf_op jit(solution)/shard_map/ppermute | solution.py:676
  84.2 14.9 %attend.1 = (bf16[1024,128]{1,0:T(8,128)(2,1)S(1)}, bf16[1024,128]{1,0:T(8,128)(2,1)}, f32[128,2048]{1,0:T(8,128)S(1)}, f32[2,2048]{1,0:T(2,128)S(1)}) custom-call(s32[4]{0:T(128)S(1)} %convert_reduce_fusion.4.first_ref, bf16[1024,384]{1,0:T(8,128)(2,1)S(1)} %copy-done.3, bf16[1024,384]{1,0:T(8,128)(2,1)S(1)} %collective-permute-done.4.other_ref, ...), custom_call_target="tpu_custom_call" | custom-call | tf_op jit(solution)/shard_map/attend/pallas_call | solution.py:489
  104.6 4.2 collective-permute-done.5
  114.8 6.0 %collective-permute-done.8 = bf16[4,64,256]{2,1,0:T(8,128)(2,1)S(1)} collective-permute-done((bf16[4,64,256]{2,1,0:T(8,128)(2,1)S(1)}, bf16[4,64,256]{2,1,0:T(8,128)(2,1)S(1)}, u32[]{:S(2)}, u32[]{:S(2)}) %collective-permute-start.8) | collective-permute-done | bytes 131104 | tf_op jit(solution)/shard_map/ppermute | solution.py:576
  126.9 11.8 %collective-permute-done.13 = bf16[4,64,1024]{2,1,0:T(8,128)(2,1)S(1)} collective-permute-done((bf16[4,64,1024]{2,1,0:T(8,128)(2,1)S(1)}, bf16[4,64,1024]{2,1,0:T(8,128)(2,1)S(1)}, u32[]{:S(2)}, u32[]{:S(2)}) %collective-permute-start.13) | collective-permute-done | bytes 524320 | tf_op jit(solution)/shard_map/ppermute | solution.py:553
  144.4 5.4 %multiply_convert_fusion = (bf16[1024,1024]{1,0:T(8,128)(2,1)S(1)}, bf16[1024,1024]{1,0:T(8,128)(2,1)S(1)}) fusion(f32[1024]{0:T(1024)S(1)} %convert_element_type.221, f32[1024,1024]{1,0:T(8,128)S(1)} %fusion.122, bf16[1024,1024]{1,0:T(8,128)(2,1)S(1)} %bitcast.352, bf16[1024,1024]{1,0:T(8,128)(2,1)S(1)} %copy-done), kind=kOutput, calls=%fused_computation.10 | convolution fusion | flops 2171600896 | bytes 12587008 | tf_op jit(solution)/shard_map/dot_general | solution.py:717
  149.9 3.8 convolution_convert_fusion
  153.6 3.8 convolution_convert_fusion.1
  171.0 10.4 %collective-permute-done.19 = bf16[4,64,1024]{2,1,0:T(8,128)(2,1)S(1)} collective-permute-done((bf16[4,64,1024]{2,1,0:T(8,128)(2,1)S(1)}, bf16[4,64,1024]{2,1,0:T(8,128)(2,1)S(1)}, u32[]{:S(2)}, u32[]{:S(2)}) %collective-permute-start.19) | collective-permute-done | bytes 524320 | tf_op jit(solution)/shard_map/ppermute | solution.py:567
  200.4 33.5 %collective-permute-done.23.dother_ref = bf16[1024,128]{1,0:T(8,128)(2,1)S(1)} collective-permute-done((bf16[1024,128]{1,0:T(8,128)(2,1)S(1)}, bf16[1024,128]{1,0:T(8,128)(2,1)S(1)}, u32[]{:S(2)}, u32[]{:S(2)}) %collective-permute-start.23) | collective-permute-done | bytes 262176 | tf_op jit(solution)/shard_map/ppermute | solution.py:745
  233.9 18.1 %attend_back.1 = (bf16[1024,384]{1,0:T(8,128)(2,1)S(1)}, bf16[1024,384]{1,0:T(8,128)(2,1)S(1)}) custom-call(s32[4]{0:T(128)S(1)} %convert_reduce_fusion.4.first_ref, bf16[1024,384]{1,0:T(8,128)(2,1)S(1)} %copy-done.4, bf16[1024,384]{1,0:T(8,128)(2,1)S(1)} %copy-done.6, bf16[2048,128]{1,0:T(8,128)(2,1)S(1)} %copy-done.2, ...), custom_call_target="tpu_custom_call" | custom-call | tf_op jit(solution)/shard_map/attend_back/pallas_call | solution.py:522
  252.5 3.0 fusion.123
  258.2 18.6 %collective-permute-done.24 = bf16[1024,384]{1,0:T(8,128)(2,1)S(1)} collective-permute-done((bf16[1024,384]{1,0:T(8,128)(2,1)S(1)}, bf16[1024,384]{1,0:T(8,128)(2,1)S(1)}, u32[]{:S(2)}, u32[]{:S(2)}) %collective-permute-start.24) | collective-permute-done | bytes 786464 | tf_op jit(solution)/shard_map/ppermute | solution.py:750
  285.1 3.4 collective-permute-done.30
  292.0 2.7 convert_add_fusion.3
  295.4 12.9 %collective-permute-done.31 = bf16[4,64,1024]{2,1,0:T(8,128)(2,1)S(1)} collective-permute-done((bf16[4,64,1024]{2,1,0:T(8,128)(2,1)S(1)}, bf16[4,64,1024]{2,1,0:T(8,128)(2,1)S(1)}, u32[]{:S(2)}, u32[]{:S(2)}) %collective-permute-start.31) | collective-permute-done | bytes 524320 | tf_op jit(solution)/shard_map/ppermute | solution.py:567
  316.1 3.1 fusion.88
  319.2 4.3 %all-to-all-start.2 = ((bf16[4,64,1024]{2,1,0:T(8,128)(2,1)}), bf16[4,64,1024]{2,1,0:T(8,128)(2,1)}, u32[]{:S(2)}, u32[]{:S(2)}) async-start(bf16[4,64,1024]{2,1,0:T(8,128)(2,1)} %fusion.88), calls=%async_computation.2 | async-start | bytes 1048576 | tf_op jit(solution)/shard_map/all_to_all | solution.py:548
  328.0 8.7 %collective-permute-done.40 = f32[8,1024]{1,0:T(8,128)S(1)} collective-permute-done((f32[8,1024]{1,0:T(8,128)S(1)}, f32[8,1024]{1,0:T(8,128)S(1)}, u32[]{:S(2)}, u32[]{:S(2)}) %collective-permute-start.40) | collective-permute-done | bytes 32800 | tf_op jit(solution)/shard_map/ppermute | solution.py:583
  336.7 4.7 %collective-permute-start.41 = (f32[8,1024]{1,0:T(8,128)S(1)}, f32[8,1024]{1,0:T(8,128)S(1)}, u32[]{:S(2)}, u32[]{:S(2)}) collective-permute-start(f32[8,1024]{1,0:T(8,128)S(1)} %add.302), channel_id=1, source_target_pairs={{0,16},{4,20},{8,24},{12,28},{16,0},{20,4},{24,8},{28,12},{1,17},{... | collective-permute-start | bytes 98312 | tf_op jit(solution)/shard_map/ppermute | solution.py:583
  342.3 3.6 collective-permute-start.36
  345.9 4.2 convert_element_type.265
  353.1 10.0 %collective-permute-done.35 = bf16[128,1024]{1,0:T(8,128)(2,1)} collective-permute-done((bf16[128,1024]{1,0:T(8,128)(2,1)S(1)}, bf16[128,1024]{1,0:T(8,128)(2,1)}, u32[]{:S(2)}, u32[]{:S(2)}) %collective-permute-start.35) | collective-permute-done | bytes 262176 | tf_op jit(solution)/shard_map/ppermute | solution.py:778
  368.2 4.1 collective-permute-start.43
  378.1 3.5 all-to-all-start.3
  382.2 16.7 %collective-permute-done.45 = bf16[128,1024]{1,0:T(8,128)(2,1)S(1)} collective-permute-done((bf16[128,1024]{1,0:T(8,128)(2,1)}, bf16[128,1024]{1,0:T(8,128)(2,1)S(1)}, u32[]{:S(2)}, u32[]{:S(2)}) %collective-permute-start.45) | collective-permute-done | bytes 262176 | tf_op jit(solution)/shard_map/ppermute | solution.py:791
  (316 shorter events, 144.4 us)
Async XLA Ops:
  10.0 23.7 %all-to-all-start = ((bf16[4,80,1024]{2,1,0:T(8,128)(2,1)}), bf16[4,80,1024]{2,1,0:T(8,128)(2,1)S(1)}, u32[]{:S(2)}, u32[]{:S(2)}) async-start(bf16[4,80,1024]{2,1,0:T(8,128)(2,1)} %pad_maximum_fusion.8), calls=%async_computation | async-start | bytes 1310720 | tf_op jit(solution)/shard_map/all_to_all | solution.py:548
  35.3 13.2 %collective-permute-start.1 = (bf16[4,64,1024]{2,1,0:T(8,128)(2,1)}, bf16[4,64,1024]{2,1,0:T(8,128)(2,1)}, u32[]{:S(2)}, u32[]{:S(2)}) collective-permute-start(bf16[4,64,1024]{2,1,0:T(8,128)(2,1)} %fusion.83), channel_id=1, source_target_pairs={{0,2},{1,3},{2,0},{3,1},{4,6},{5,7},{6,4},{7,5},{8,10},{9,11},{10,... | collective-permute-start | bytes 1572872 | tf_op jit(solution)/shard_map/ppermute | solution.py:553
  58.8 44.2 %all-to-all-start.1 = ((bf16[4,64,1024]{2,1,0:T(8,128)(2,1)}), bf16[4,64,1024]{2,1,0:T(8,128)(2,1)}, u32[]{:S(2)}, u32[]{:S(2)}) async-start(bf16[4,64,1024]{2,1,0:T(8,128)(2,1)} %param.29), calls=%async_computation.1 | async-start | bytes 1048576 | tf_op jit(solution)/shard_map/all_to_all | solution.py:548
  63.0 283.0 %all-reduce.5.cloned.1.call-start = ((), (), s32[]{:S(2)}) async-start(), calls=%async_computation.4 | async-start | bytes 8388608 | tf_op jit(solution)/shard_map/psum | solution.py:732
  63.2 19.9 %collective-permute-start.4 = (bf16[1024,384]{1,0:T(8,128)(2,1)}, bf16[1024,384]{1,0:T(8,128)(2,1)S(1)}, u32[]{:S(2)}, u32[]{:S(2)}) collective-permute-start(bf16[1024,384]{1,0:T(8,128)(2,1)} %add_convert_fusion.2), channel_id=1, source_target_pairs={{0,4},{4,0},{8,12},{12,8},{16,20},{20,16},{24,28},{28,24},{1,5},{5... | collective-permute-start | bytes 2359304 | tf_op jit(solution)/shard_map/ppermute | solution.py:676
  65.3 37.3 %collective-permute-start.9 = (bf16[256,1024]{1,0:T(8,128)(2,1)}, bf16[256,1024]{1,0:T(8,128)(2,1)}, u32[]{:S(2)}, u32[]{:S(2)}) collective-permute-start(bf16[256,1024]{1,0:T(8,128)(2,1)} %maximum_select_fusion.1), channel_id=1, source_target_pairs={{0,2},{1,3},{2,0},{3,1},{4,6},{5,7},{6,4},{7,5},{8,10},{9,11},{10,... | collective-permute-start | bytes 1572872 | tf_op jit(solution)/shard_map/ppermute | solution.py:553
  102.5 19.7 %collective-permute-start.11 = (bf16[256,1024]{1,0:T(8,128)(2,1)}, bf16[256,1024]{1,0:T(8,128)(2,1)}, u32[]{:S(2)}, u32[]{:S(2)}) collective-permute-start(bf16[256,1024]{1,0:T(8,128)(2,1)} %collective-permute-done.9), channel_id=1, source_target_pairs={{0,1},{1,0},{2,3},{3,2},{4,5},{5,4},{6,7},{7,6},{8,9},{9,8},{10,11... | collective-permute-start | bytes 1572872 | tf_op jit(solution)/shard_map/ppermute | solution.py:554
  103.0 23.0 %collective-permute-start.16 = (bf16[4,64,1024]{2,1,0:T(8,128)(2,1)}, bf16[4,64,1024]{2,1,0:T(8,128)(2,1)S(1)}, u32[]{:S(2)}, u32[]{:S(2)}) collective-permute-start(bf16[4,64,1024]{2,1,0:T(8,128)(2,1)} %all-to-all-done.1), channel_id=1, source_target_pairs={{0,2},{1,3},{2,0},{3,1},{4,6},{5,7},{6,4},{7,5},{8,10},{9,11},{10,... | collective-permute-start | bytes 1572872 | tf_op jit(solution)/shard_map/ppermute | solution.py:553
  124.4 14.2 %collective-permute-start.13 = (bf16[4,64,1024]{2,1,0:T(8,128)(2,1)S(1)}, bf16[4,64,1024]{2,1,0:T(8,128)(2,1)S(1)}, u32[]{:S(2)}, u32[]{:S(2)}) collective-permute-start(bf16[4,64,1024]{2,1,0:T(8,128)(2,1)S(1)} %add_convert_fusion.4), channel_id=1, source_target_pairs={{0,2},{1,3},{2,0},{3,1},{4,6},{5,7},{6,4},{7,5},{8,10},{9,11},{10,... | collective-permute-start | bytes 1572872 | tf_op jit(solution)/shard_map/ppermute | solution.py:553
  126.0 12.6 %collective-permute-start.15 = (bf16[4,64,1024]{2,1,0:T(8,128)(2,1)}, bf16[4,64,1024]{2,1,0:T(8,128)(2,1)S(1)}, u32[]{:S(2)}, u32[]{:S(2)}) collective-permute-start(bf16[4,64,1024]{2,1,0:T(8,128)(2,1)} %all-to-all-done.1), channel_id=1, source_target_pairs={{0,1},{1,0},{2,3},{3,2},{4,5},{5,4},{6,7},{7,6},{8,9},{9,8},{10,11... | collective-permute-start | bytes 1572872 | tf_op jit(solution)/shard_map/ppermute | solution.py:552
  126.0 12.6 %collective-permute-start.17 = (bf16[4,64,1024]{2,1,0:T(8,128)(2,1)S(1)}, bf16[4,64,1024]{2,1,0:T(8,128)(2,1)S(1)}, u32[]{:S(2)}, u32[]{:S(2)}) collective-permute-start(bf16[4,64,1024]{2,1,0:T(8,128)(2,1)S(1)} %collective-permute-done.16), channel_id=1, source_target_pairs={{0,1},{1,0},{2,3},{3,2},{4,5},{5,4},{6,7},{7,6},{8,9},{9,8},{10,11... | collective-permute-start | bytes 1572872 | tf_op jit(solution)/shard_map/ppermute | solution.py:554
  126.5 17.4 %collective-permute-start.12 = (bf16[4,64,1024]{2,1,0:T(8,128)(2,1)S(1)}, bf16[4,64,1024]{2,1,0:T(8,128)(2,1)S(1)}, u32[]{:S(2)}, u32[]{:S(2)}) collective-permute-start(bf16[4,64,1024]{2,1,0:T(8,128)(2,1)S(1)} %add_convert_fusion.4), channel_id=1, source_target_pairs={{0,1},{1,0},{2,3},{3,2},{4,5},{5,4},{6,7},{7,6},{8,9},{9,8},{10,11... | collective-permute-start | bytes 1572872 | tf_op jit(solution)/shard_map/ppermute | solution.py:552
  162.6 89.9 %collective-permute-start.26 = (bf16[1024,1024]{1,0:T(8,128)(2,1)}, bf16[1024,1024]{1,0:T(8,128)(2,1)}, u32[]{:S(2)}, u32[]{:S(2)}) collective-permute-start(bf16[1024,1024]{1,0:T(8,128)(2,1)} %bitcast.333), channel_id=1, source_target_pairs={{0,4},{4,0},{8,12},{12,8},{16,20},{20,16},{24,28},{28,24},{1,5},{5... | collective-permute-start | bytes 6291464 | tf_op jit(solution)/shard_map/ppermute | solution.py:707
  167.1 14.3 %collective-permute-start.19 = (bf16[4,64,1024]{2,1,0:T(8,128)(2,1)S(1)}, bf16[4,64,1024]{2,1,0:T(8,128)(2,1)S(1)}, u32[]{:S(2)}, u32[]{:S(2)}) collective-permute-start(bf16[4,64,1024]{2,1,0:T(8,128)(2,1)S(1)} %fusion.93), channel_id=1, source_target_pairs={{0,2},{1,3},{2,0},{3,1},{4,6},{5,7},{6,4},{7,5},{8,10},{9,11},{10,... | collective-permute-start | bytes 1572872 | tf_op jit(solution)/shard_map/ppermute | solution.py:567
  195.5 56.9 %collective-permute-start.28 = (bf16[4,64,1024]{2,1,0:T(8,128)(2,1)S(1)}, bf16[4,64,1024]{2,1,0:T(8,128)(2,1)S(1)}, u32[]{:S(2)}, u32[]{:S(2)}) collective-permute-start(bf16[4,64,1024]{2,1,0:T(8,128)(2,1)S(1)} %convert_element_type.232), channel_id=1, source_target_pairs={{0,2},{1,3},{2,0},{3,1},{4,6},{5,7},{6,4},{7,5},{8,10},{9,11},{10,... | collective-permute-start | bytes 1572872 | tf_op jit(solution)/shard_map/ppermute | solution.py:553
  196.9 59.7 %collective-permute-start.27 = (bf16[4,64,1024]{2,1,0:T(8,128)(2,1)S(1)}, bf16[4,64,1024]{2,1,0:T(8,128)(2,1)}, u32[]{:S(2)}, u32[]{:S(2)}) collective-permute-start(bf16[4,64,1024]{2,1,0:T(8,128)(2,1)S(1)} %convert_element_type.232), channel_id=1, source_target_pairs={{0,1},{1,0},{2,3},{3,2},{4,5},{5,4},{6,7},{7,6},{8,9},{9,8},{10,11... | collective-permute-start | bytes 1572872 | tf_op jit(solution)/shard_map/ppermute | solution.py:552
  197.3 36.6 %collective-permute-start.23 = (bf16[1024,128]{1,0:T(8,128)(2,1)S(1)}, bf16[1024,128]{1,0:T(8,128)(2,1)S(1)}, u32[]{:S(2)}, u32[]{:S(2)}) collective-permute-start(bf16[1024,128]{1,0:T(8,128)(2,1)S(1)} %get-tuple-element.110), channel_id=1, source_target_pairs={{0,4},{4,0},{8,12},{12,8},{16,20},{20,16},{24,28},{28,24},{1,5},{5... | collective-permute-start | bytes 786440 | tf_op jit(solution)/shard_map/ppermute | solution.py:745
  200.4 79.1 %collective-permute-start.32 = (bf16[2,4,64,1024]{3,2,1,0:T(8,128)(2,1)}, bf16[2,4,64,1024]{3,2,1,0:T(8,128)(2,1)}, u32[]{:S(2)}, u32[]{:S(2)}) collective-permute-start(bf16[2,4,64,1024]{3,2,1,0:T(8,128)(2,1)} %pad_maximum_fusion.7), channel_id=1, source_target_pairs={{0,1},{1,0},{2,3},{3,2},{4,5},{5,4},{6,7},{7,6},{8,9},{9,8},{10,11... | collective-permute-start | bytes 3145736 | tf_op jit(solution)/shard_map/ppermute | solution.py:564
  252.1 24.8 %collective-permute-start.24 = (bf16[1024,384]{1,0:T(8,128)(2,1)S(1)}, bf16[1024,384]{1,0:T(8,128)(2,1)S(1)}, u32[]{:S(2)}, u32[]{:S(2)}) collective-permute-start(bf16[1024,384]{1,0:T(8,128)(2,1)S(1)} %get-tuple-element.63), channel_id=1, source_target_pairs={{0,4},{4,0},{8,12},{12,8},{16,20},{20,16},{24,28},{28,24},{1,5},{5... | collective-permute-start | bytes 2359304 | tf_op jit(solution)/shard_map/ppermute | solution.py:750
  283.5 42.1 %collective-permute-start.33 = (bf16[4,64,1024]{2,1,0:T(8,128)(2,1)}, bf16[4,64,1024]{2,1,0:T(8,128)(2,1)}, u32[]{:S(2)}, u32[]{:S(2)}) collective-permute-start(bf16[4,64,1024]{2,1,0:T(8,128)(2,1)} %fusion.92), channel_id=1, source_target_pairs={{0,2},{1,3},{2,0},{3,1},{4,6},{5,7},{6,4},{7,5},{8,10},{9,11},{10,... | collective-permute-start | bytes 1572872 | tf_op jit(solution)/shard_map/ppermute | solution.py:567
  290.2 18.1 %collective-permute-start.31 = (bf16[4,64,1024]{2,1,0:T(8,128)(2,1)S(1)}, bf16[4,64,1024]{2,1,0:T(8,128)(2,1)S(1)}, u32[]{:S(2)}, u32[]{:S(2)}) collective-permute-start(bf16[4,64,1024]{2,1,0:T(8,128)(2,1)S(1)} %fusion.37), channel_id=1, source_target_pairs={{0,2},{1,3},{2,0},{3,1},{4,6},{5,7},{6,4},{7,5},{8,10},{9,11},{10,... | collective-permute-start | bytes 1572872 | tf_op jit(solution)/shard_map/ppermute | solution.py:567
  319.2 43.9 %all-to-all-start.2 = ((bf16[4,64,1024]{2,1,0:T(8,128)(2,1)}), bf16[4,64,1024]{2,1,0:T(8,128)(2,1)}, u32[]{:S(2)}, u32[]{:S(2)}) async-start(bf16[4,64,1024]{2,1,0:T(8,128)(2,1)} %fusion.88), calls=%async_computation.2 | async-start | bytes 1048576 | tf_op jit(solution)/shard_map/all_to_all | solution.py:548
  323.6 13.2 %collective-permute-start.40 = (f32[8,1024]{1,0:T(8,128)S(1)}, f32[8,1024]{1,0:T(8,128)S(1)}, u32[]{:S(2)}, u32[]{:S(2)}) collective-permute-start(f32[8,1024]{1,0:T(8,128)S(1)} %fusion.157), channel_id=1, source_target_pairs={{0,8},{4,12},{8,0},{12,4},{16,24},{20,28},{24,16},{28,20},{1,9},{5... | collective-permute-start | bytes 98312 | tf_op jit(solution)/shard_map/ppermute | solution.py:583
  336.7 15.9 %collective-permute-start.41 = (f32[8,1024]{1,0:T(8,128)S(1)}, f32[8,1024]{1,0:T(8,128)S(1)}, u32[]{:S(2)}, u32[]{:S(2)}) collective-permute-start(f32[8,1024]{1,0:T(8,128)S(1)} %add.302), channel_id=1, source_target_pairs={{0,16},{4,20},{8,24},{12,28},{16,0},{20,4},{24,8},{28,12},{1,17},{... | collective-permute-start | bytes 98312 | tf_op jit(solution)/shard_map/ppermute | solution.py:583
  341.5 21.5 %collective-permute-start.35 = (bf16[128,1024]{1,0:T(8,128)(2,1)S(1)}, bf16[128,1024]{1,0:T(8,128)(2,1)}, u32[]{:S(2)}, u32[]{:S(2)}) collective-permute-start(bf16[128,1024]{1,0:T(8,128)(2,1)S(1)} %get-tuple-element.104), channel_id=1, source_target_pairs={{0,16},{4,20},{8,24},{12,28},{16,0},{20,4},{24,8},{28,12},{1,17},{... | collective-permute-start | bytes 786440 | tf_op jit(solution)/shard_map/ppermute | solution.py:778
  342.3 20.8 %collective-permute-start.36 = (bf16[128,1024]{1,0:T(8,128)(2,1)S(1)}, bf16[128,1024]{1,0:T(8,128)(2,1)}, u32[]{:S(2)}, u32[]{:S(2)}) collective-permute-start(bf16[128,1024]{1,0:T(8,128)(2,1)S(1)} %get-tuple-element.103), channel_id=1, source_target_pairs={{0,24},{4,28},{8,16},{12,20},{16,8},{20,12},{24,0},{28,4},{1,25},{... | collective-permute-start | bytes 786440 | tf_op jit(solution)/shard_map/ppermute | solution.py:778
  366.7 34.2 %collective-permute-start.42 = (bf16[128,1024]{1,0:T(8,128)(2,1)}, bf16[128,1024]{1,0:T(8,128)(2,1)S(1)}, u32[]{:S(2)}, u32[]{:S(2)}) collective-permute-start(bf16[128,1024]{1,0:T(8,128)(2,1)} %get-tuple-element.93), channel_id=1, source_target_pairs={{0,4},{4,0},{8,12},{12,8},{16,20},{20,16},{24,28},{28,24},{1,5},{5... | collective-permute-start | bytes 786440 | tf_op jit(solution)/shard_map/ppermute | solution.py:792
  368.2 13.4 %collective-permute-start.43 = (bf16[128,1024]{1,0:T(8,128)(2,1)}, bf16[128,1024]{1,0:T(8,128)(2,1)}, u32[]{:S(2)}, u32[]{:S(2)}) collective-permute-start(bf16[128,1024]{1,0:T(8,128)(2,1)} %get-tuple-element.93), channel_id=1, source_target_pairs={{0,8},{4,12},{8,0},{12,4},{16,24},{20,28},{24,16},{28,20},{1,9},{5... | collective-permute-start | bytes 786440 | tf_op jit(solution)/shard_map/ppermute | solution.py:791
  372.3 26.6 %collective-permute-start.45 = (bf16[128,1024]{1,0:T(8,128)(2,1)}, bf16[128,1024]{1,0:T(8,128)(2,1)S(1)}, u32[]{:S(2)}, u32[]{:S(2)}) collective-permute-start(bf16[128,1024]{1,0:T(8,128)(2,1)} %get-tuple-element.93), channel_id=1, source_target_pairs={{0,16},{4,20},{8,24},{12,28},{16,0},{20,4},{24,8},{28,12},{1,17},{... | collective-permute-start | bytes 786440 | tf_op jit(solution)/shard_map/ppermute | solution.py:791
  372.6 26.8 %collective-permute-start.47 = (bf16[128,1024]{1,0:T(8,128)(2,1)}, bf16[128,1024]{1,0:T(8,128)(2,1)S(1)}, u32[]{:S(2)}, u32[]{:S(2)}) collective-permute-start(bf16[128,1024]{1,0:T(8,128)(2,1)} %get-tuple-element.93), channel_id=1, source_target_pairs={{0,24},{4,28},{8,16},{12,20},{16,8},{20,12},{24,0},{28,4},{1,25},{... | collective-permute-start | bytes 786440 | tf_op jit(solution)/shard_map/ppermute | solution.py:791
  378.1 36.6 %all-to-all-start.3 = ((bf16[4,64,1024]{2,1,0:T(8,128)(2,1)}), bf16[4,64,1024]{2,1,0:T(8,128)(2,1)S(1)}, u32[]{:S(2)}, u32[]{:S(2)}) async-start(bf16[4,64,1024]{2,1,0:T(8,128)(2,1)} %add_convert_fusion.3), calls=%async_computation.3 | async-start | bytes 1048576 | tf_op jit(solution)/shard_map/all_to_all | solution.py:548
  381.6 21.8 %collective-permute-start.44 = (bf16[128,1024]{1,0:T(8,128)(2,1)}, bf16[128,1024]{1,0:T(8,128)(2,1)S(1)}, u32[]{:S(2)}, u32[]{:S(2)}) collective-permute-start(bf16[128,1024]{1,0:T(8,128)(2,1)} %collective-permute-done.43), channel_id=1, source_target_pairs={{0,4},{4,0},{8,12},{12,8},{16,20},{20,16},{24,28},{28,24},{1,5},{5... | collective-permute-start | bytes 786440 | tf_op jit(solution)/shard_map/ppermute | solution.py:792
  (66 other events, 772.5 us)
Sparse Core Ops, SparseCore 0:
  163.2 173.1 all-reduce.4

commit v5 on v4

--- a/solution.py
+++ b/solution.py
@@ -784,17 +784,6 @@
     grad_tokens, layer_low, own, came = tie(grad_tokens, layer_low, own, came)
     grad_tokens = grad_tokens.astype(f32)
     total = (own.astype(f32) + sum(c.astype(f32) for c in came)).astype(bf16)
-    layer_out = planes_swap(layer_low)
-
-    wide = jnp.zeros((2, 4, PAIR, width), bf16)
-    for d in range(4):
-        near = total if d == 0 else lax.ppermute(total, "ctx", moves[d])
-        far = lax.ppermute(near, "ctx", CTX_X)
-        wide = lax.dynamic_update_slice(wide, near[None, None], (side, plane ^ d, 0, 0))
-        wide = lax.dynamic_update_slice(wide, far[None, None], (1 - side, plane ^ d, 0, 0))
-    qkv_grad = wide[:, :3].astype(f32).reshape(4, 3 * HEAD_DIM, width)
-    qkv_grad = jnp.transpose(qkv_grad, (2, 0, 1))
-    outw_grad = wide[:, 3].astype(f32)
     small = sum_tp(
         jnp.stack(
             [
@@ -807,6 +796,18 @@
             ]
         )
     )
+    total, small = tie(total, small)
+    layer_out = planes_swap(layer_low)
+
+    wide = jnp.zeros((2, 4, PAIR, width), bf16)
+    for d in range(4):
+        near = total if d == 0 else lax.ppermute(total, "ctx", moves[d])
+        far = lax.ppermute(near, "ctx", CTX_X)
+        wide = lax.dynamic_update_slice(wide, near[None, None], (side, plane ^ d, 0, 0))
+        wide = lax.dynamic_update_slice(wide, far[None, None], (1 - side, plane ^ d, 0, 0))
+    qkv_grad = wide[:, :3].astype(f32).reshape(4, 3 * HEAD_DIM, width)
+    qkv_grad = jnp.transpose(qkv_grad, (2, 0, 1))
+    outw_grad = wide[:, 3].astype(f32)
     bias_sums = jnp.sum(packed_grad, axis=0, dtype=f32)[None]
     bias_sums = order_pair(bias_sums, swapped, 1)
     bias_sums = jnp.pad(bias_sums, ((0, 0), (0, width - 12 * HEAD_DIM)))

time: 429 us -> 459 us (1.070)
  waiting for transfers between devices: 181 us -> 211 us
  starting transfers between devices: 68.8 us -> 80.4 us
  Pallas kernels: 33 us -> 24.8 us
    ppermute x3, waiting for transfers between devices: 10.4 us -> 37 us  [shards(): lax.ppermute(lax.dynamic_index_in_dim(parts, plane ^ d, 0, keepdims=False...]
    ppermute x3, waiting for transfers between devices: 16.7 us -> 0.01 us  [shards(): near = total if d == 0 else lax.ppermute(total, 'ctx', moves[d])]
    ppermute x3, waiting for transfers between devices: 8.67 us -> 24.4 us  [sum_ctx(): values = values + lax.ppermute(values, 'ctx', perm)]
    all_to_all x4, starting transfers between devices: 18.4 us -> 30.1 us  [planes_swap(): lax.all_to_all(values, 'ctx', 0, 0, axis_index_groups=CTX_PLANES, tiled=F...]
    ppermute x4, waiting for transfers between devices: 1.88 us -> 8.84 us  [shards(): far = lax.ppermute(near, 'ctx', CTX_X)]
  transfers between devices with their start and end apart: 54 -> 54, of which waited for: 24 -> 24; matrix products, arithmetic and copies ran while one was open for 20% -> 19% of each run, Pallas kernels for 8% -> 5%
where the time goes in v5:
time: 459 us; the launch traced here: 452 us
  waiting for transfers between devices  211 us (46%)
  starting transfers between devices  80.4 us (18%)
  matrix products  49.5 us (11%)
  other arithmetic  40.6 us (9%)
  local copies, waits for them, and re-layouts  30.7 us (7%)
  Pallas kernels  24.8 us (5%)
  between operations  15.2 us (3%)
    dot_general x20, matrix products, contract(): return lax.dot_general(a, b, (dims, ((), ())), preferred_element_type=f32)  37.1 us
    ppermute x3, waiting for transfers between devices, shards(): lax.ppermute(lax.dynamic_index_in_dim(parts, plane ^ d, 0, keepdims=False...  37 us
    ppermute x1, waiting for transfers between devices, shards(): dmixed_other = lax.ppermute(dmixed[:, PAIR:], 'ctx', CTX_X)  32.1 us
    all_to_all x4, starting transfers between devices, planes_swap(): lax.all_to_all(values, 'ctx', 0, 0, axis_index_groups=CTX_PLANES, tiled=F...  30.1 us
    ppermute x3, waiting for transfers between devices, sum_ctx(): values = values + lax.ppermute(values, 'ctx', perm)  24.4 us
    ppermute x3, waiting for transfers between devices, tp_scatter_rows(): arrived = lax.ppermute(across, 'tp', TP_ROW)  23.4 us
    ppermute x1, waiting for transfers between devices, shards(): lax.ppermute(grad_other, 'ctx', CTX_X)  19 us
    ppermute x5, waiting for transfers between devices, tp_gather(): row = lax.ppermute(values, 'tp', TP_ROW)  18.8 us
  transfers between devices with their start and end apart: 54, of which 24 were waited for; matrix products, arithmetic and copies ran while one was open for 19% of the time, Pallas kernels for 5%

profile of v5, /device:TPU:0, one launch (start us, length us, event | category | flops | bytes accessed | tf_op | source)
XLA Modules:
  0.0 452.4 jit_solution(11966437496595459697)
XLA Ops:
  10.0 6.4 %all-to-all-start = ((bf16[4,80,1024]{2,1,0:T(8,128)(2,1)}), bf16[4,80,1024]{2,1,0:T(8,128)(2,1)S(1)}, u32[]{:S(2)}, u32[]{:S(2)}) async-start(bf16[4,80,1024]{2,1,0:T(8,128)(2,1)} %pad_maximum_fusion.8), calls=%async_computation | async-start | bytes 1310720 | tf_op jit(solution)/shard_map/all_to_all | solution.py:548
  16.4 2.6 fusion.112
  19.7 4.0 maximum_select_fusion
  26.2 7.6 %all-to-all-done = bf16[4,80,1024]{2,1,0:T(8,128)(2,1)S(1)} async-done(((bf16[4,80,1024]{2,1,0:T(8,128)(2,1)}), bf16[4,80,1024]{2,1,0:T(8,128)(2,1)S(1)}, u32[]{:S(2)}, u32[]{:S(2)}) %all-to-all-start) | async-done | bytes 655392 | tf_op jit(solution)/shard_map/all_to_all | solution.py:548
  41.5 7.0 %collective-permute-done.1 = bf16[4,64,1024]{2,1,0:T(8,128)(2,1)} collective-permute-done((bf16[4,64,1024]{2,1,0:T(8,128)(2,1)}, bf16[4,64,1024]{2,1,0:T(8,128)(2,1)}, u32[]{:S(2)}, u32[]{:S(2)}) %collective-permute-start.1) | collective-permute-done | bytes 524320 | tf_op jit(solution)/shard_map/ppermute | solution.py:553
  58.5 4.1 all-to-all-start.1
  66.9 15.9 %collective-permute-done.4.other_ref = bf16[1024,384]{1,0:T(8,128)(2,1)S(1)} collective-permute-done((bf16[1024,384]{1,0:T(8,128)(2,1)}, bf16[1024,384]{1,0:T(8,128)(2,1)S(1)}, u32[]{:S(2)}, u32[]{:S(2)}) %collective-permute-start.4) | collective-permute-done | bytes 786464 | tf_op jit(solution)/shard_map/ppermute | solution.py:676
  83.9 11.2 %attend.1 = (bf16[1024,128]{1,0:T(8,128)(2,1)S(1)}, bf16[1024,128]{1,0:T(8,128)(2,1)}, f32[128,2048]{1,0:T(8,128)S(1)}, f32[2,2048]{1,0:T(2,128)S(1)}) custom-call(s32[4]{0:T(128)S(1)} %convert_reduce_fusion.4.first_ref, bf16[1024,384]{1,0:T(8,128)(2,1)S(1)} %copy-done.3, bf16[1024,384]{1,0:T(8,128)(2,1)S(1)} %collective-permute-done.4.other_ref, ...), custom_call_target="tpu_custom_call" | custom-call | tf_op jit(solution)/shard_map/attend/pallas_call | solution.py:489
  100.6 4.2 collective-permute-done.5
  110.9 5.9 %collective-permute-done.8 = bf16[4,64,256]{2,1,0:T(8,128)(2,1)S(1)} collective-permute-done((bf16[4,64,256]{2,1,0:T(8,128)(2,1)S(1)}, bf16[4,64,256]{2,1,0:T(8,128)(2,1)S(1)}, u32[]{:S(2)}, u32[]{:S(2)}) %collective-permute-start.8) | collective-permute-done | bytes 131104 | tf_op jit(solution)/shard_map/ppermute | solution.py:576
  122.8 11.8 %collective-permute-done.13 = bf16[4,64,1024]{2,1,0:T(8,128)(2,1)S(1)} collective-permute-done((bf16[4,64,1024]{2,1,0:T(8,128)(2,1)S(1)}, bf16[4,64,1024]{2,1,0:T(8,128)(2,1)S(1)}, u32[]{:S(2)}, u32[]{:S(2)}) %collective-permute-start.13) | collective-permute-done | bytes 524320 | tf_op jit(solution)/shard_map/ppermute | solution.py:553
  140.4 5.4 %multiply_convert_fusion = (bf16[1024,1024]{1,0:T(8,128)(2,1)S(1)}, bf16[1024,1024]{1,0:T(8,128)(2,1)S(1)}) fusion(f32[1024]{0:T(1024)S(1)} %convert_element_type.221, f32[1024,1024]{1,0:T(8,128)S(1)} %fusion.122, bf16[1024,1024]{1,0:T(8,128)(2,1)S(1)} %bitcast.352, bf16[1024,1024]{1,0:T(8,128)(2,1)S(1)} %copy-done), kind=kOutput, calls=%fused_computation.10 | convolution fusion | flops 2171600896 | bytes 12587008 | tf_op jit(solution)/shard_map/dot_general | solution.py:717
  145.9 3.8 convolution_convert_fusion
  149.6 3.7 convolution_convert_fusion.1
  167.0 10.4 %collective-permute-done.19 = bf16[4,64,1024]{2,1,0:T(8,128)(2,1)S(1)} collective-permute-done((bf16[4,64,1024]{2,1,0:T(8,128)(2,1)S(1)}, bf16[4,64,1024]{2,1,0:T(8,128)(2,1)S(1)}, u32[]{:S(2)}, u32[]{:S(2)}) %collective-permute-start.19) | collective-permute-done | bytes 524320 | tf_op jit(solution)/shard_map/ppermute | solution.py:567
  195.1 32.1 %collective-permute-done.23.dother_ref = bf16[1024,128]{1,0:T(8,128)(2,1)S(1)} collective-permute-done((bf16[1024,128]{1,0:T(8,128)(2,1)S(1)}, bf16[1024,128]{1,0:T(8,128)(2,1)S(1)}, u32[]{:S(2)}, u32[]{:S(2)}) %collective-permute-start.23) | collective-permute-done | bytes 262176 | tf_op jit(solution)/shard_map/ppermute | solution.py:745
  227.2 13.7 %attend_back.1 = (bf16[1024,384]{1,0:T(8,128)(2,1)S(1)}, bf16[1024,384]{1,0:T(8,128)(2,1)S(1)}) custom-call(s32[4]{0:T(128)S(1)} %convert_reduce_fusion.4.first_ref, bf16[1024,384]{1,0:T(8,128)(2,1)S(1)} %copy-done.4, bf16[1024,384]{1,0:T(8,128)(2,1)S(1)} %copy-done.6, bf16[2048,128]{1,0:T(8,128)(2,1)S(1)} %copy-done.2, ...), custom_call_target="tpu_custom_call" | custom-call | tf_op jit(solution)/shard_map/attend_back/pallas_call | solution.py:522
  241.3 2.8 fusion.123
  245.3 19.0 %collective-permute-done.24 = bf16[1024,384]{1,0:T(8,128)(2,1)S(1)} collective-permute-done((bf16[1024,384]{1,0:T(8,128)(2,1)S(1)}, bf16[1024,384]{1,0:T(8,128)(2,1)S(1)}, u32[]{:S(2)}, u32[]{:S(2)}) %collective-permute-start.24) | collective-permute-done | bytes 786464 | tf_op jit(solution)/shard_map/ppermute | solution.py:750
  271.2 5.5 %collective-permute-done.30 = bf16[128,1024]{1,0:T(8,128)(2,1)S(1)} collective-permute-done((bf16[128,1024]{1,0:T(8,128)(2,1)S(1)}, bf16[128,1024]{1,0:T(8,128)(2,1)S(1)}, u32[]{:S(2)}, u32[]{:S(2)}) %collective-permute-start.30) | collective-permute-done | bytes 262176 | tf_op jit(solution)/shard_map/ppermute | solution.py:763
  282.3 13.0 %collective-permute-done.31 = bf16[4,64,1024]{2,1,0:T(8,128)(2,1)S(1)} collective-permute-done((bf16[4,64,1024]{2,1,0:T(8,128)(2,1)S(1)}, bf16[4,64,1024]{2,1,0:T(8,128)(2,1)S(1)}, u32[]{:S(2)}, u32[]{:S(2)}) %collective-permute-start.31) | collective-permute-done | bytes 524320 | tf_op jit(solution)/shard_map/ppermute | solution.py:567
  297.2 16.0 %all-to-all-start.2 = ((bf16[4,64,1024]{2,1,0:T(8,128)(2,1)}), bf16[4,64,1024]{2,1,0:T(8,128)(2,1)}, u32[]{:S(2)}, u32[]{:S(2)}) async-start(bf16[4,64,1024]{2,1,0:T(8,128)(2,1)} %fusion.88), calls=%async_computation.2 | async-start | bytes 1048576 | tf_op jit(solution)/shard_map/all_to_all | solution.py:548
  325.1 23.3 %collective-permute-done.34 = bf16[128,1024]{1,0:T(8,128)(2,1)} collective-permute-done((bf16[128,1024]{1,0:T(8,128)(2,1)S(1)}, bf16[128,1024]{1,0:T(8,128)(2,1)}, u32[]{:S(2)}, u32[]{:S(2)}) %collective-permute-start.34) | collective-permute-done | bytes 262176 | tf_op jit(solution)/shard_map/ppermute | solution.py:778
  348.4 13.7 %collective-permute-done.35 = bf16[128,1024]{1,0:T(8,128)(2,1)} collective-permute-done((bf16[128,1024]{1,0:T(8,128)(2,1)S(1)}, bf16[128,1024]{1,0:T(8,128)(2,1)}, u32[]{:S(2)}, u32[]{:S(2)}) %collective-permute-start.35) | collective-permute-done | bytes 262176 | tf_op jit(solution)/shard_map/ppermute | solution.py:778
  367.4 6.2 %collective-permute-start.40 = (f32[8,1024]{1,0:T(8,128)S(1)}, f32[8,1024]{1,0:T(8,128)S(1)}, u32[]{:S(2)}, u32[]{:S(2)}) collective-permute-start(f32[8,1024]{1,0:T(8,128)S(1)} %fusion.157), channel_id=1, source_target_pairs={{0,8},{4,12},{8,0},{12,4},{16,24},{20,28},{24,16},{28,20},{1,9},{5... | collective-permute-start | bytes 98312 | tf_op jit(solution)/shard_map/ppermute | solution.py:583
  373.6 4.2 convert_element_type.265
  383.5 2.7 collective-permute-start.47
  388.3 3.5 all-to-all-start.3
  391.8 2.9 collective-permute-start.41
  397.1 21.9 %collective-permute-done.41 = f32[8,1024]{1,0:T(8,128)S(1)} collective-permute-done((f32[8,1024]{1,0:T(8,128)S(1)}, f32[8,1024]{1,0:T(8,128)S(1)}, u32[]{:S(2)}, u32[]{:S(2)}) %collective-permute-start.41) | collective-permute-done | bytes 32800 | tf_op jit(solution)/shard_map/ppermute | solution.py:583
  426.3 3.6 collective-permute-done.44
  431.3 3.9 collective-permute-done.46
  (309 shorter events, 145.2 us)
Async XLA Ops:
  10.0 23.7 %all-to-all-start = ((bf16[4,80,1024]{2,1,0:T(8,128)(2,1)}), bf16[4,80,1024]{2,1,0:T(8,128)(2,1)S(1)}, u32[]{:S(2)}, u32[]{:S(2)}) async-start(bf16[4,80,1024]{2,1,0:T(8,128)(2,1)} %pad_maximum_fusion.8), calls=%async_computation | async-start | bytes 1310720 | tf_op jit(solution)/shard_map/all_to_all | solution.py:548
  58.5 40.5 %all-to-all-start.1 = ((bf16[4,64,1024]{2,1,0:T(8,128)(2,1)}), bf16[4,64,1024]{2,1,0:T(8,128)(2,1)}, u32[]{:S(2)}, u32[]{:S(2)}) async-start(bf16[4,64,1024]{2,1,0:T(8,128)(2,1)} %param.29), calls=%async_computation.1 | async-start | bytes 1048576 | tf_op jit(solution)/shard_map/all_to_all | solution.py:548
  62.7 311.0 %all-reduce.5.cloned.1.call-start = ((), (), s32[]{:S(2)}) async-start(), calls=%async_computation.4 | async-start | bytes 8388608 | tf_op jit(solution)/shard_map/psum | solution.py:732
  62.9 19.9 %collective-permute-start.4 = (bf16[1024,384]{1,0:T(8,128)(2,1)}, bf16[1024,384]{1,0:T(8,128)(2,1)S(1)}, u32[]{:S(2)}, u32[]{:S(2)}) collective-permute-start(bf16[1024,384]{1,0:T(8,128)(2,1)} %add_convert_fusion.2), channel_id=1, source_target_pairs={{0,4},{4,0},{8,12},{12,8},{16,20},{20,16},{24,28},{28,24},{1,5},{5... | collective-permute-start | bytes 2359304 | tf_op jit(solution)/shard_map/ppermute | solution.py:676
  65.0 33.5 %collective-permute-start.9 = (bf16[256,1024]{1,0:T(8,128)(2,1)}, bf16[256,1024]{1,0:T(8,128)(2,1)}, u32[]{:S(2)}, u32[]{:S(2)}) collective-permute-start(bf16[256,1024]{1,0:T(8,128)(2,1)} %maximum_select_fusion.1), channel_id=1, source_target_pairs={{0,2},{1,3},{2,0},{3,1},{4,6},{5,7},{6,4},{7,5},{8,10},{9,11},{10,... | collective-permute-start | bytes 1572872 | tf_op jit(solution)/shard_map/ppermute | solution.py:553
  98.5 19.7 %collective-permute-start.11 = (bf16[256,1024]{1,0:T(8,128)(2,1)}, bf16[256,1024]{1,0:T(8,128)(2,1)}, u32[]{:S(2)}, u32[]{:S(2)}) collective-permute-start(bf16[256,1024]{1,0:T(8,128)(2,1)} %collective-permute-done.9), channel_id=1, source_target_pairs={{0,1},{1,0},{2,3},{3,2},{4,5},{5,4},{6,7},{7,6},{8,9},{9,8},{10,11... | collective-permute-start | bytes 1572872 | tf_op jit(solution)/shard_map/ppermute | solution.py:554
  99.0 23.0 %collective-permute-start.16 = (bf16[4,64,1024]{2,1,0:T(8,128)(2,1)}, bf16[4,64,1024]{2,1,0:T(8,128)(2,1)S(1)}, u32[]{:S(2)}, u32[]{:S(2)}) collective-permute-start(bf16[4,64,1024]{2,1,0:T(8,128)(2,1)} %all-to-all-done.1), channel_id=1, source_target_pairs={{0,2},{1,3},{2,0},{3,1},{4,6},{5,7},{6,4},{7,5},{8,10},{9,11},{10,... | collective-permute-start | bytes 1572872 | tf_op jit(solution)/shard_map/ppermute | solution.py:553
  120.4 14.2 %collective-permute-start.13 = (bf16[4,64,1024]{2,1,0:T(8,128)(2,1)S(1)}, bf16[4,64,1024]{2,1,0:T(8,128)(2,1)S(1)}, u32[]{:S(2)}, u32[]{:S(2)}) collective-permute-start(bf16[4,64,1024]{2,1,0:T(8,128)(2,1)S(1)} %add_convert_fusion.4), channel_id=1, source_target_pairs={{0,2},{1,3},{2,0},{3,1},{4,6},{5,7},{6,4},{7,5},{8,10},{9,11},{10,... | collective-permute-start | bytes 1572872 | tf_op jit(solution)/shard_map/ppermute | solution.py:553
  122.5 17.4 %collective-permute-start.12 = (bf16[4,64,1024]{2,1,0:T(8,128)(2,1)S(1)}, bf16[4,64,1024]{2,1,0:T(8,128)(2,1)S(1)}, u32[]{:S(2)}, u32[]{:S(2)}) collective-permute-start(bf16[4,64,1024]{2,1,0:T(8,128)(2,1)S(1)} %add_convert_fusion.4), channel_id=1, source_target_pairs={{0,1},{1,0},{2,3},{3,2},{4,5},{5,4},{6,7},{7,6},{8,9},{9,8},{10,11... | collective-permute-start | bytes 1572872 | tf_op jit(solution)/shard_map/ppermute | solution.py:552
  158.5 82.7 %collective-permute-start.26 = (bf16[1024,1024]{1,0:T(8,128)(2,1)}, bf16[1024,1024]{1,0:T(8,128)(2,1)}, u32[]{:S(2)}, u32[]{:S(2)}) collective-permute-start(bf16[1024,1024]{1,0:T(8,128)(2,1)} %bitcast.333), channel_id=1, source_target_pairs={{0,4},{4,0},{8,12},{12,8},{16,20},{20,16},{24,28},{28,24},{1,5},{5... | collective-permute-start | bytes 6291464 | tf_op jit(solution)/shard_map/ppermute | solution.py:707
  163.1 14.3 %collective-permute-start.19 = (bf16[4,64,1024]{2,1,0:T(8,128)(2,1)S(1)}, bf16[4,64,1024]{2,1,0:T(8,128)(2,1)S(1)}, u32[]{:S(2)}, u32[]{:S(2)}) collective-permute-start(bf16[4,64,1024]{2,1,0:T(8,128)(2,1)S(1)} %fusion.93), channel_id=1, source_target_pairs={{0,2},{1,3},{2,0},{3,1},{4,6},{5,7},{6,4},{7,5},{8,10},{9,11},{10,... | collective-permute-start | bytes 1572872 | tf_op jit(solution)/shard_map/ppermute | solution.py:567
  191.1 54.2 %collective-permute-start.28 = (bf16[4,64,1024]{2,1,0:T(8,128)(2,1)S(1)}, bf16[4,64,1024]{2,1,0:T(8,128)(2,1)S(1)}, u32[]{:S(2)}, u32[]{:S(2)}) collective-permute-start(bf16[4,64,1024]{2,1,0:T(8,128)(2,1)S(1)} %convert_element_type.232), channel_id=1, source_target_pairs={{0,2},{1,3},{2,0},{3,1},{4,6},{5,7},{6,4},{7,5},{8,10},{9,11},{10,... | collective-permute-start | bytes 1572872 | tf_op jit(solution)/shard_map/ppermute | solution.py:553
  192.5 73.4 %collective-permute-start.27 = (bf16[4,64,1024]{2,1,0:T(8,128)(2,1)S(1)}, bf16[4,64,1024]{2,1,0:T(8,128)(2,1)S(1)}, u32[]{:S(2)}, u32[]{:S(2)}) collective-permute-start(bf16[4,64,1024]{2,1,0:T(8,128)(2,1)S(1)} %convert_element_type.232), channel_id=1, source_target_pairs={{0,1},{1,0},{2,3},{3,2},{4,5},{5,4},{6,7},{7,6},{8,9},{9,8},{10,11... | collective-permute-start | bytes 1572872 | tf_op jit(solution)/shard_map/ppermute | solution.py:552
  192.9 34.3 %collective-permute-start.23 = (bf16[1024,128]{1,0:T(8,128)(2,1)S(1)}, bf16[1024,128]{1,0:T(8,128)(2,1)S(1)}, u32[]{:S(2)}, u32[]{:S(2)}) collective-permute-start(bf16[1024,128]{1,0:T(8,128)(2,1)S(1)} %get-tuple-element.112), channel_id=1, source_target_pairs={{0,4},{4,0},{8,12},{12,8},{16,20},{20,16},{24,28},{28,24},{1,5},{5... | collective-permute-start | bytes 786440 | tf_op jit(solution)/shard_map/ppermute | solution.py:745
  195.0 73.3 %collective-permute-start.32 = (bf16[2,4,64,1024]{3,2,1,0:T(8,128)(2,1)S(1)}, bf16[2,4,64,1024]{3,2,1,0:T(8,128)(2,1)S(1)}, u32[]{:S(2)}, u32[]{:S(2)}) collective-permute-start(bf16[2,4,64,1024]{3,2,1,0:T(8,128)(2,1)S(1)} %pad_maximum_fusion.7), channel_id=1, source_target_pairs={{0,1},{1,0},{2,3},{3,2},{4,5},{5,4},{6,7},{7,6},{8,9},{9,8},{10,11... | collective-permute-start | bytes 3145736 | tf_op jit(solution)/shard_map/ppermute | solution.py:564
  240.9 23.5 %collective-permute-start.24 = (bf16[1024,384]{1,0:T(8,128)(2,1)S(1)}, bf16[1024,384]{1,0:T(8,128)(2,1)S(1)}, u32[]{:S(2)}, u32[]{:S(2)}) collective-permute-start(bf16[1024,384]{1,0:T(8,128)(2,1)S(1)} %get-tuple-element.65), channel_id=1, source_target_pairs={{0,4},{4,0},{8,12},{12,8},{16,20},{20,16},{24,28},{28,24},{1,5},{5... | collective-permute-start | bytes 2359304 | tf_op jit(solution)/shard_map/ppermute | solution.py:750
  245.3 20.6 %collective-permute-start.29 = (bf16[4,64,1024]{2,1,0:T(8,128)(2,1)S(1)}, bf16[4,64,1024]{2,1,0:T(8,128)(2,1)S(1)}, u32[]{:S(2)}, u32[]{:S(2)}) collective-permute-start(bf16[4,64,1024]{2,1,0:T(8,128)(2,1)S(1)} %collective-permute-done.28), channel_id=1, source_target_pairs={{0,1},{1,0},{2,3},{3,2},{4,5},{5,4},{6,7},{7,6},{8,9},{9,8},{10,11... | collective-permute-start | bytes 1572872 | tf_op jit(solution)/shard_map/ppermute | solution.py:554
  269.9 52.9 %collective-permute-start.33 = (bf16[4,64,1024]{2,1,0:T(8,128)(2,1)}, bf16[4,64,1024]{2,1,0:T(8,128)(2,1)}, u32[]{:S(2)}, u32[]{:S(2)}) collective-permute-start(bf16[4,64,1024]{2,1,0:T(8,128)(2,1)} %fusion.92), channel_id=1, source_target_pairs={{0,2},{1,3},{2,0},{3,1},{4,6},{5,7},{6,4},{7,5},{8,10},{9,11},{10,... | collective-permute-start | bytes 1572872 | tf_op jit(solution)/shard_map/ppermute | solution.py:567
  278.4 16.9 %collective-permute-start.31 = (bf16[4,64,1024]{2,1,0:T(8,128)(2,1)S(1)}, bf16[4,64,1024]{2,1,0:T(8,128)(2,1)S(1)}, u32[]{:S(2)}, u32[]{:S(2)}) collective-permute-start(bf16[4,64,1024]{2,1,0:T(8,128)(2,1)S(1)} %fusion.37), channel_id=1, source_target_pairs={{0,2},{1,3},{2,0},{3,1},{4,6},{5,7},{6,4},{7,5},{8,10},{9,11},{10,... | collective-permute-start | bytes 1572872 | tf_op jit(solution)/shard_map/ppermute | solution.py:567
  297.2 65.0 %all-to-all-start.2 = ((bf16[4,64,1024]{2,1,0:T(8,128)(2,1)}), bf16[4,64,1024]{2,1,0:T(8,128)(2,1)}, u32[]{:S(2)}, u32[]{:S(2)}) async-start(bf16[4,64,1024]{2,1,0:T(8,128)(2,1)} %fusion.88), calls=%async_computation.2 | async-start | bytes 1048576 | tf_op jit(solution)/shard_map/all_to_all | solution.py:548
  316.6 31.8 %collective-permute-start.34 = (bf16[128,1024]{1,0:T(8,128)(2,1)S(1)}, bf16[128,1024]{1,0:T(8,128)(2,1)}, u32[]{:S(2)}, u32[]{:S(2)}) collective-permute-start(bf16[128,1024]{1,0:T(8,128)(2,1)S(1)} %get-tuple-element.107), channel_id=1, source_target_pairs={{0,8},{4,12},{8,0},{12,4},{16,24},{20,28},{24,16},{28,20},{1,9},{5... | collective-permute-start | bytes 786440 | tf_op jit(solution)/shard_map/ppermute | solution.py:778
  318.7 43.5 %collective-permute-start.35 = (bf16[128,1024]{1,0:T(8,128)(2,1)S(1)}, bf16[128,1024]{1,0:T(8,128)(2,1)}, u32[]{:S(2)}, u32[]{:S(2)}) collective-permute-start(bf16[128,1024]{1,0:T(8,128)(2,1)S(1)} %get-tuple-element.106), channel_id=1, source_target_pairs={{0,16},{4,20},{8,24},{12,28},{16,0},{20,4},{24,8},{28,12},{1,17},{... | collective-permute-start | bytes 786440 | tf_op jit(solution)/shard_map/ppermute | solution.py:778
  321.0 41.1 %collective-permute-start.36 = (bf16[128,1024]{1,0:T(8,128)(2,1)S(1)}, bf16[128,1024]{1,0:T(8,128)(2,1)}, u32[]{:S(2)}, u32[]{:S(2)}) collective-permute-start(bf16[128,1024]{1,0:T(8,128)(2,1)S(1)} %get-tuple-element.105), channel_id=1, source_target_pairs={{0,24},{4,28},{8,16},{12,20},{16,8},{20,12},{24,0},{28,4},{1,25},{... | collective-permute-start | bytes 786440 | tf_op jit(solution)/shard_map/ppermute | solution.py:778
  367.4 24.4 %collective-permute-start.40 = (f32[8,1024]{1,0:T(8,128)S(1)}, f32[8,1024]{1,0:T(8,128)S(1)}, u32[]{:S(2)}, u32[]{:S(2)}) collective-permute-start(f32[8,1024]{1,0:T(8,128)S(1)} %fusion.157), channel_id=1, source_target_pairs={{0,8},{4,12},{8,0},{12,4},{16,24},{20,28},{24,16},{28,20},{1,9},{5... | collective-permute-start | bytes 98312 | tf_op jit(solution)/shard_map/ppermute | solution.py:583
  380.4 42.6 %collective-permute-start.42 = (bf16[128,1024]{1,0:T(8,128)(2,1)S(1)}, bf16[128,1024]{1,0:T(8,128)(2,1)}, u32[]{:S(2)}, u32[]{:S(2)}) collective-permute-start(bf16[128,1024]{1,0:T(8,128)(2,1)S(1)} %add_convert_fusion.5), channel_id=1, source_target_pairs={{0,4},{4,0},{8,12},{12,8},{16,20},{20,16},{24,28},{28,24},{1,5},{5... | collective-permute-start | bytes 786440 | tf_op jit(solution)/shard_map/ppermute | solution.py:805
  381.8 38.6 %collective-permute-start.43 = (bf16[128,1024]{1,0:T(8,128)(2,1)S(1)}, bf16[128,1024]{1,0:T(8,128)(2,1)}, u32[]{:S(2)}, u32[]{:S(2)}) collective-permute-start(bf16[128,1024]{1,0:T(8,128)(2,1)S(1)} %add_convert_fusion.5), channel_id=1, source_target_pairs={{0,8},{4,12},{8,0},{12,4},{16,24},{20,28},{24,16},{28,20},{1,9},{5... | collective-permute-start | bytes 786440 | tf_op jit(solution)/shard_map/ppermute | solution.py:804
  381.9 39.1 %collective-permute-start.45 = (bf16[128,1024]{1,0:T(8,128)(2,1)S(1)}, bf16[128,1024]{1,0:T(8,128)(2,1)S(1)}, u32[]{:S(2)}, u32[]{:S(2)}) collective-permute-start(bf16[128,1024]{1,0:T(8,128)(2,1)S(1)} %add_convert_fusion.5), channel_id=1, source_target_pairs={{0,16},{4,20},{8,24},{12,28},{16,0},{20,4},{24,8},{28,12},{1,17},{... | collective-permute-start | bytes 786440 | tf_op jit(solution)/shard_map/ppermute | solution.py:804
  383.5 39.0 %collective-permute-start.47 = (bf16[128,1024]{1,0:T(8,128)(2,1)S(1)}, bf16[128,1024]{1,0:T(8,128)(2,1)S(1)}, u32[]{:S(2)}, u32[]{:S(2)}) collective-permute-start(bf16[128,1024]{1,0:T(8,128)(2,1)S(1)} %add_convert_fusion.5), channel_id=1, source_target_pairs={{0,24},{4,28},{8,16},{12,20},{16,8},{20,12},{24,0},{28,4},{1,25},{... | collective-permute-start | bytes 786440 | tf_op jit(solution)/shard_map/ppermute | solution.py:804
  388.3 56.3 %all-to-all-start.3 = ((bf16[4,64,1024]{2,1,0:T(8,128)(2,1)}), bf16[4,64,1024]{2,1,0:T(8,128)(2,1)S(1)}, u32[]{:S(2)}, u32[]{:S(2)}) async-start(bf16[4,64,1024]{2,1,0:T(8,128)(2,1)} %add_convert_fusion.3), calls=%async_computation.3 | async-start | bytes 1048576 | tf_op jit(solution)/shard_map/all_to_all | solution.py:548
  391.8 27.1 %collective-permute-start.41 = (f32[8,1024]{1,0:T(8,128)S(1)}, f32[8,1024]{1,0:T(8,128)S(1)}, u32[]{:S(2)}, u32[]{:S(2)}) collective-permute-start(f32[8,1024]{1,0:T(8,128)S(1)} %add.305), channel_id=1, source_target_pairs={{0,16},{4,20},{8,24},{12,28},{16,0},{20,4},{24,8},{28,12},{1,17},{... | collective-permute-start | bytes 98312 | tf_op jit(solution)/shard_map/ppermute | solution.py:583
  420.9 14.3 %collective-permute-start.46 = (bf16[128,1024]{1,0:T(8,128)(2,1)S(1)}, bf16[128,1024]{1,0:T(8,128)(2,1)S(1)}, u32[]{:S(2)}, u32[]{:S(2)}) collective-permute-start(bf16[128,1024]{1,0:T(8,128)(2,1)S(1)} %collective-permute-done.45), channel_id=1, source_target_pairs={{0,4},{4,0},{8,12},{12,8},{16,20},{20,16},{24,28},{28,24},{1,5},{5... | collective-permute-start | bytes 786440 | tf_op jit(solution)/shard_map/ppermute | solution.py:805
  422.5 15.6 %collective-permute-start.48 = (bf16[128,1024]{1,0:T(8,128)(2,1)S(1)}, bf16[128,1024]{1,0:T(8,128)(2,1)S(1)}, u32[]{:S(2)}, u32[]{:S(2)}) collective-permute-start(bf16[128,1024]{1,0:T(8,128)(2,1)S(1)} %collective-permute-done.47), channel_id=1, source_target_pairs={{0,4},{4,0},{8,12},{12,8},{16,20},{20,16},{24,28},{28,24},{1,5},{5... | collective-permute-start | bytes 786440 | tf_op jit(solution)/shard_map/ppermute | solution.py:805
  (62 other events, 706.1 us)
Sparse Core Ops, SparseCore 0:
  159.2 191.8 all-reduce.4
